TPU v7x, 256 devices: a whole 4x4x8 slice. The times are simulated.
256 devices in a mesh: dp: 64 (over y_lo, z, x), chan: 4 (over y_hi, core).
Axes of the slice: x: 4, y: 4 (y_hi: 2, y_lo: 2; y = y_hi * 2 + y_lo), z: 8, core: 2. Of those that a mesh axis runs over, the one named last changes fastest.
Arguments:
- inputs: bfloat16 [512, 128, 512], P(('dp', 'chan')), may hold values from -6 to 6
- cotangent: bfloat16 [512, 128, 512], P(('dp', 'chan')), may hold values from -24 to 24
- expand_w: bfloat16 [512, 2048], P(None, 'chan'), may hold values from -0.25 to 0.25
- expand_b: float32 [2048], P('chan'), may hold values from -3 to 3
- depth_k: float32 [25, 2048], P(None, 'chan'), may hold values from -1.25 to 1.25
- depth_b: float32 [2048], P('chan'), may hold values from -3 to 3
- project_w: bfloat16 [2048, 512], P('chan'), may hold values from -0.125 to 0.125
Outputs:
- input_grad: bfloat16 [512, 128, 512], P(('dp', 'chan'))
- expand_w_grad: float32 [512, 2048], P(None, 'chan')
- expand_b_grad: float32 [2048], P('chan')
- depth_k_grad: float32 [25, 2048], P(None, 'chan')
- depth_b_grad: float32 [2048], P('chan')
- project_w_grad: float32 [2048, 512], P('chan')
All inputs are finite; a program needn't handle non-finite values.
Results may differ from a plain program's by a relative error of at most 0.007.
Values may be sent and summed in bfloat16 or wider, within the bound.
A program may use at most 64 MiB of HBM per device.

v0:
```python
import jax
import jax.numpy as jnp
from jax import lax
from jax.experimental import pallas as pl
from jax.experimental.pallas import tpu as pltpu
from jax.sharding import Mesh, PartitionSpec as P

MESH_ID = pl.DeviceIdType.MESH
ALL_AXES = ("y_lo", "z", "x", "y_hi", "core")
ROW_AXES = ("y_lo", "z", "x")
CHAN_AXES = ("y_hi", "core")


def _sum_kernel(nx, nz, data, out, xs, zs, ys, sems):
    (xsend, xrecv, zsend, zrecv, ysend, yrecv, gzsend, gzrecv, gxsend, gxrecv) = sems
    coords = [lax.axis_index(a) for a in ALL_AXES]
    iy, iz, ix = coords[0], coords[1], coords[2]

    def dev(y=None, z=None, x=None):
        c = list(coords)
        if y is not None:
            c[0] = y
        if z is not None:
            c[1] = z
        if x is not None:
            c[2] = x
        return tuple(c)

    x_next = [dev(x=lax.rem(ix + 1, nx)), dev(x=lax.rem(ix + nx - 1, nx))]
    z_next = [dev(z=lax.rem(iz + 1, nz)), dev(z=lax.rem(iz + nz - 1, nz))]
    partner = dev(y=1 - iy)

    barrier = pltpu.get_barrier_semaphore()
    for d in (x_next[0], x_next[1], z_next[0], z_next[1], partner):
        pl.semaphore_signal(barrier, inc=1, device_id=d, device_id_type=MESH_ID)
    pl.semaphore_wait(barrier, 5)

    rows = data.shape[0]
    half = rows // 2
    bx = half // nx
    bz = bx // nz
    steps = (1, -1)

    def xblock(h, k):
        return pl.ds(pl.multiple_of(h * half + lax.rem(k + 4 * nx, nx) * bx, 8), bx)

    def zblock(k):
        return pl.ds(pl.multiple_of(lax.rem(k + 4 * nz, nz) * bz, 8), bz)

    def oblock(h, kx, kz):
        at = h * half + lax.rem(kx + 4 * nx, nx) * bx + lax.rem(kz + 4 * nz, nz) * bz
        return pl.ds(pl.multiple_of(at, 8), bz)

    def obig(h, kx):
        return pl.ds(pl.multiple_of(h * half + lax.rem(kx + 4 * nx, nx) * bx, 8), bx)

    for s in range(nx - 1):
        copies = []
        for h in range(2):
            sg = steps[h]
            src = data.at[xblock(h, ix - sg)] if s == 0 else xs.at[h, s - 1]
            c = pltpu.make_async_remote_copy(
                src_ref=src, dst_ref=xs.at[h, s], send_sem=xsend.at[h * nx + s],
                recv_sem=xrecv.at[h * nx + s], device_id=x_next[h], device_id_type=MESH_ID)
            c.start()
            copies.append(c)
        for h in range(2):
            sg = steps[h]
            copies[h].wait_recv()
            xs[h, s] = xs[h, s] + data[xblock(h, ix - sg * (s + 2))]
            copies[h].wait_send()
    last = nx - 2
    for s in range(nz - 1):
        copies = []
        for h in range(2):
            sg = steps[h]
            src = xs.at[h, last, zblock(iz - sg)] if s == 0 else zs.at[h, s - 1]
            c = pltpu.make_async_remote_copy(
                src_ref=src, dst_ref=zs.at[h, s], send_sem=zsend.at[h * nz + s],
                recv_sem=zrecv.at[h * nz + s], device_id=z_next[h], device_id_type=MESH_ID)
            c.start()
            copies.append(c)
        for h in range(2):
            sg = steps[h]
            copies[h].wait_recv()
            zs[h, s] = zs[h, s] + xs[h, last, zblock(iz - sg * (s + 2))]
            copies[h].wait_send()
    zl = nz - 2
    c = pltpu.make_async_remote_copy(
        src_ref=zs.at[:, zl], dst_ref=ys, send_sem=ysend.at[0], recv_sem=yrecv.at[0],
        device_id=partner, device_id_type=MESH_ID)
    c.start()
    c.wait_recv()
    for h in range(2):
        out[oblock(h, ix, iz)] = zs[h, zl] + ys[h]
    c.wait_send()
    for s in range(nz - 1):
        copies = []
        for h in range(2):
            sg = steps[h]
            loc = oblock(h, ix, iz - sg * s)
            c = pltpu.make_async_remote_copy(
                src_ref=out.at[loc], dst_ref=out.at[loc], send_sem=gzsend.at[h * nz + s],
                recv_sem=gzrecv.at[h * nz + s], device_id=z_next[h], device_id_type=MESH_ID)
            c.start()
            copies.append(c)
        for h in range(2):
            copies[h].wait_recv()
            copies[h].wait_send()
    for s in range(nx - 1):
        copies = []
        for h in range(2):
            sg = steps[h]
            loc = obig(h, ix - sg * s)
            c = pltpu.make_async_remote_copy(
                src_ref=out.at[loc], dst_ref=out.at[loc], send_sem=gxsend.at[h * nx + s],
                recv_sem=gxrecv.at[h * nx + s], device_id=x_next[h], device_id_type=MESH_ID)
            c.start()
            copies.append(c)
        for h in range(2):
            copies[h].wait_recv()
            copies[h].wait_send()


def row_group_allreduce(flat, nx, nz):
    rows, cols = flat.shape
    half = rows // 2
    bx = half // nx
    bz = bx // nz
    sems = [pltpu.SemaphoreType.DMA((2 * nx,)), pltpu.SemaphoreType.DMA((2 * nx,)),
            pltpu.SemaphoreType.DMA((2 * nz,)), pltpu.SemaphoreType.DMA((2 * nz,)),
            pltpu.SemaphoreType.DMA((1,)), pltpu.SemaphoreType.DMA((1,)),
            pltpu.SemaphoreType.DMA((2 * nz,)), pltpu.SemaphoreType.DMA((2 * nz,)),
            pltpu.SemaphoreType.DMA((2 * nx,)), pltpu.SemaphoreType.DMA((2 * nx,))]

    def body(data, out, xs, zs, ys, *s):
        _sum_kernel(nx, nz, data, out, xs, zs, ys, s)

    return pl.pallas_call(
        body,
        out_shape=jax.ShapeDtypeStruct((rows, cols), jnp.float32),
        in_specs=[pl.BlockSpec(memory_space=pltpu.VMEM)],
        out_specs=pl.BlockSpec(memory_space=pltpu.VMEM),
        scratch_shapes=[
            pltpu.VMEM((2, nx - 1, bx, cols), jnp.float32),
            pltpu.VMEM((2, nz - 1, bz, cols), jnp.float32),
            pltpu.VMEM((2, bz, cols), jnp.float32),
        ] + sems,
        compiler_params=pltpu.CompilerParams(collective_id=0, has_side_effects=True,
                                             vmem_limit_bytes=48 * 1024 * 1024),
    )(flat)


def extended(block, sides, width):
    for axis, dim in sides:
        count = 1
        for name in axis:
            count *= lax.axis_size(name)
        forward = [(i, i + 1) for i in range(count - 1)]
        backward = [(target, source) for source, target in forward]
        low = lax.ppermute(
            lax.slice_in_dim(block, block.shape[dim] - width, None, axis=dim), axis, forward
        )
        high = lax.ppermute(lax.slice_in_dim(block, 0, width, axis=dim), axis, backward)
        block = jnp.concatenate([low, block, high], axis=dim)
    return block


def gelu_parts(pre):
    cdf = 0.5 * (1.0 + lax.erf(pre * 0.7071067811865476))
    dens = jnp.exp(-0.5 * pre * pre) * 0.3989422804014327
    return (pre * cdf, cdf + pre * dens)


def row_group_sum(terms):
    lanes = 128
    flat = jnp.concatenate([t.reshape(-1, lanes) for t in terms], axis=0)
    rows = flat.shape[0]
    nx, nz = lax.axis_size("x"), lax.axis_size("z")
    quantum = 16 * nx * nz
    padded_rows = -(-rows // quantum) * quantum
    flat = jnp.pad(flat, ((0, padded_rows - rows), (0, 0)))
    flat = row_group_allreduce(flat, nx, nz)
    out = []
    at = 0
    for t in terms:
        size = t.size // lanes
        out.append(flat[at : at + size].reshape(t.shape))
        at += size
    return out


def shards(inputs, cotangent, expand_w, expand_b, depth_k, depth_b, project_w):
    rows_in, rows_cot = (
        lax.all_gather(inputs, CHAN_AXES, axis=0, tiled=True),
        lax.all_gather(cotangent, CHAN_AXES, axis=0, tiled=True),
    )
    nrows, ncols, cin = rows_in.shape
    hslice = expand_w.shape[1]
    flat_inputs = rows_in.reshape(nrows * ncols, cin)
    flat_cotan = rows_cot.reshape(nrows * ncols, cin)
    pre_one = (
        jnp.dot(flat_inputs, expand_w, preferred_element_type=jnp.float32).reshape(
            nrows, ncols, hslice
        )
        + expand_b
    )
    hidden, slope_one = gelu_parts(pre_one)
    hidden = hidden.astype(jnp.bfloat16)
    rimmed = extended(hidden, ((ROW_AXES, 0),), 2)
    padded = jnp.pad(rimmed, ((0, 0), (2, 2), (0, 0))).astype(jnp.float32)
    pre_two = jnp.zeros((nrows, ncols, hslice), jnp.float32) + depth_b
    for row_tap in range(5):
        for col_tap in range(5):
            pre_two = (
                pre_two
                + depth_k[5 * row_tap + col_tap]
                * padded[row_tap : row_tap + nrows, col_tap : col_tap + ncols]
            )
    mixed, slope_two = gelu_parts(pre_two)
    mixed = mixed.astype(jnp.bfloat16).reshape(nrows * ncols, hslice)
    grad_w2 = jnp.dot(mixed.T, flat_cotan, preferred_element_type=jnp.float32)
    grad_mixed = jnp.dot(flat_cotan, project_w.T, preferred_element_type=jnp.float32).reshape(
        nrows, ncols, hslice
    )
    grad_pre = (grad_mixed * slope_two).astype(jnp.bfloat16)
    grad_pre_f = grad_pre.astype(jnp.float32)
    grad_bd = jnp.sum(grad_pre_f, axis=(0, 1))
    grad_rimmed = extended(grad_pre, ((ROW_AXES, 0),), 2)
    grad_pad = jnp.pad(grad_rimmed, ((0, 0), (2, 2), (0, 0))).astype(jnp.float32)
    taps = []
    grad_hidden = jnp.zeros((nrows, ncols, hslice), jnp.float32)
    for row_tap in range(5):
        for col_tap in range(5):
            taps.append(
                jnp.sum(
                    padded[row_tap : row_tap + nrows, col_tap : col_tap + ncols] * grad_pre_f,
                    axis=(0, 1),
                )
            )
            grad_hidden = (
                grad_hidden
                + depth_k[5 * row_tap + col_tap]
                * grad_pad[4 - row_tap : 4 - row_tap + nrows, 4 - col_tap : 4 - col_tap + ncols]
            )
    grad_k = jnp.stack(taps, axis=0)
    grad_act = (grad_hidden * slope_one).astype(jnp.bfloat16)
    flat_act = grad_act.reshape(nrows * ncols, hslice)
    grad_b1 = jnp.sum(flat_act.astype(jnp.float32), axis=0)
    grad_w1 = jnp.dot(flat_inputs.T, flat_act, preferred_element_type=jnp.float32)
    summed = row_group_sum([grad_w1, grad_b1[None], grad_k, grad_bd[None], grad_w2])
    summed[1] = summed[1][0]
    summed[3] = summed[3][0]
    own_part = lax.psum_scatter(
        jnp.einsum("rwh,ch->rwc", grad_act, expand_w, preferred_element_type=jnp.float32),
        CHAN_AXES,
        scatter_dimension=0,
        tiled=True,
    )
    input_grad = (cotangent.astype(jnp.float32) + own_part).astype(jnp.bfloat16)
    return (input_grad, summed[0], summed[1], summed[2], summed[3], summed[4])


def solution(mesh):
    fine = Mesh(mesh.devices.reshape(2, 8, 4, 2, 2), ROW_AXES + CHAN_AXES)
    rows = ROW_AXES + CHAN_AXES
    in_specs = (
        P(rows, None, None),
        P(rows, None, None),
        P(None, CHAN_AXES),
        P(CHAN_AXES),
        P(None, CHAN_AXES),
        P(CHAN_AXES),
        P(CHAN_AXES, None),
    )
    out_specs = (
        P(rows, None, None),
        P(None, CHAN_AXES),
        P(CHAN_AXES),
        P(None, CHAN_AXES),
        P(CHAN_AXES),
        P(CHAN_AXES, None),
    )
    return jax.shard_map(shards, mesh=fine, in_specs=in_specs, out_specs=out_specs, check_vma=False)
```

profile of v0, /device:TPU:8, one launch (start us, length us, event | category | flops | bytes accessed | tf_op | source)
XLA Modules:
  0.0 266.9 jit_solution(14809287437155235235)
XLA Ops:
  7.2 0.7 all-gather.5.cloned.1.call-update
  8.0 0.7 all-gather.3.cloned.1.call-update
  8.7 26.5 %all-gather.5.cloned.1.call-done = bf16[8,128,512]{2,1,0:T(8,128)(2,1)} async-done(((bf16[2,128,512]{2,1,0:T(8,128)(2,1)}), bf16[8,128,512]{2,1,0:T(8,128)(2,1)}) %all-gather.5.cloned.1.call-update) | async-done | bytes 1048592 | tf_op jit(solution)/shard_map/all_gather | solution.py:195
  35.2 3.4 %multiply_convert_fusion.1 = (bf16[8,128,512]{2,1,0:T(8,128)(2,1)S(1)}, f32[8,128,512]{2,1,0:T(8,128)}) fusion(f32[512]{0:T(512)} %param.10, bf16[8,128,512]{2,1,0:T(8,128)(2,1)} %all-gather.5.cloned.1.call-done, bf16[512,512]{1,0:T(8,128)(2,1)S(1)} %copy-done), kind=kOutput, calls=%fused_computation.121 | convolution fusion | flops 540016640 | bytes 4720640 | tf_op jit(solution)/shard_map/dot_general | solution.py:203
  38.6 3.4 %collective-permute-start = (bf16[2,128,512]{2,1,0:T(8,128)(2,1)S(1)}, bf16[2,128,512]{2,1,0:T(8,128)(2,1)S(1)}, u32[]{:S(2)}, u32[]{:S(2)}) collective-permute-start(bf16[2,128,512]{2,1,0:T(8,128)(2,1)S(1)} %get-tuple-element.40), channel_id=1, source_target_pairs={{0,4},{4,8},{8,12},{12,16},{16,20},{20,24},{24,28},{28,32},{32,36}... | collective-permute-start | bytes 786440 | tf_op jit(solution)/shard_map/ppermute | solution.py:161
  42.0 6.8 %collective-permute-start.1 = (bf16[2,128,512]{2,1,0:T(8,128)(2,1)S(1)}, bf16[2,128,512]{2,1,0:T(8,128)(2,1)S(1)}, u32[]{:S(2)}, u32[]{:S(2)}) collective-permute-start(bf16[2,128,512]{2,1,0:T(8,128)(2,1)S(1)} %get-tuple-element.41), channel_id=1, source_target_pairs={{4,0},{8,4},{12,8},{16,12},{20,16},{24,20},{28,24},{32,28},{36,32}... | collective-permute-start | bytes 786440 | tf_op jit(solution)/shard_map/ppermute | solution.py:164
  48.8 4.8 %collective-permute-done = bf16[2,128,512]{2,1,0:T(8,128)(2,1)S(1)} collective-permute-done((bf16[2,128,512]{2,1,0:T(8,128)(2,1)S(1)}, bf16[2,128,512]{2,1,0:T(8,128)(2,1)S(1)}, u32[]{:S(2)}, u32[]{:S(2)}) %collective-permute-start) | collective-permute-done | bytes 262176 | tf_op jit(solution)/shard_map/ppermute | solution.py:161
  53.6 1.1 collective-permute-done.1
  54.7 2.2 fusion.68
  56.9 27.2 %multiply_add_fusion = f32[8,128,512]{2,1,0:T(8,128)} fusion(f32[12,132,512]{2,1,0:T(8,128)} %fusion.68, f32[512]{0:T(512)S(1)} %bitcast.88, f32[512]{0:T(512)S(1)} %bitcast.90, f32[512]{0:T(512)S(1)} %bitcast.94, f32[512]{0:T(512)S(1)} %bitcast.96, f32[512]{0:T(512)S(1)} %bitcast.98, f32[512]{0:T(512)S(1)} %bitcast.100, f32[512]{0:T(512)S(1)} %bitcast.102, ...), kind=kLoop, calls=%fused_computation.120 | loop fusion | flops 26214400 | bytes 54579200 | tf_op jit(solution)/shard_map/add | solution.py:216
  84.1 8.8 %fusion.36 = (f32[512]{0:T(512)S(1)}, f32[512]{0:T(512)S(1)}, f32[512]{0:T(512)S(1)}, f32[512]{0:T(512)S(1)}, f32[512]{0:T(512)S(1)}, /*index=5*/f32[512]{0:T(51...) fusion(f32[12,132,512]{2,1,0:T(8,128)} %fusion.68, f32[8,128,512]{2,1,0:T(8,128)} %multiply_add_fusion, ...), kind=kOutput, calls=%fused_computation.66 | convolution fusion | flops 550498304 | bytes 19415040 | tf_op jit(solution)/shard_map/dot_general | solution.py:223
  93.0 1.9 collective-permute-start.2
  94.9 9.0 %collective-permute-start.3 = (bf16[2,128,512]{2,1,0:T(8,128)(2,1)S(1)}, bf16[2,128,512]{2,1,0:T(8,128)(2,1)S(1)}, u32[]{:S(2)}, u32[]{:S(2)}) collective-permute-start(bf16[2,128,512]{2,1,0:T(8,128)(2,1)S(1)} %get-tuple-element.39), channel_id=1, source_target_pairs={{4,0},{8,4},{12,8},{16,12},{20,16},{24,20},{28,24},{32,28},{36,32}... | collective-permute-start | bytes 786440 | tf_op jit(solution)/shard_map/ppermute | solution.py:164
  103.9 3.5 %collective-permute-done.2 = bf16[2,128,512]{2,1,0:T(8,128)(2,1)S(1)} collective-permute-done((bf16[2,128,512]{2,1,0:T(8,128)(2,1)S(1)}, bf16[2,128,512]{2,1,0:T(8,128)(2,1)S(1)}, u32[]{:S(2)}, u32[]{:S(2)}) %collective-permute-start.2) | collective-permute-done | bytes 262176 | tf_op jit(solution)/shard_map/ppermute | solution.py:161
  107.5 1.3 collective-permute-done.3
  108.8 0.5 fusion.62
  109.3 7.3 %convert_reduce_fusion.1 = (f32[512]{0:T(512)S(1)}, bf16[8,128,512]{2,1,0:T(8,128)(2,1)S(1)}) fusion(f32[8,128,512]{2,1,0:T(8,128)S(1)} %copy-done.1, f32[512]{0:T(512)S(1)} %copy-done.5, f32[12,132,512]{2,1,0:T(8,128)S(1)} %fusion.62, f32[512]{0:T(512)S(1)} %bitcast.89, f32[512]{0:T(512)S(1)} %bitcast.91, f32[512]{0:T(512)S(1)} %bitcast.95, ...), kind=kLoop, calls=%fused_computation.118 | loop fusion | flops 32505344 | bytes 55629824 | tf_op jit(solution)/shard_map/reduce_sum | solution.py:249
  116.6 2.1 fusion.69
  118.7 18.7 %fusion.37 = (f32[512]{0:T(512)S(1)}, f32[512]{0:T(512)S(1)}, f32[512]{0:T(512)S(1)}, f32[512]{0:T(512)S(1)}, f32[512]{0:T(512)S(1)}, /*index=5*/f32[512]{0:T(51...) fusion(bf16[8,128,512]{2,1,0:T(8,128)(2,1)S(1)} %get-tuple-elem, ...), kind=kLoop, calls=%fused_computation.67 | loop fusion | flops 19389440 | bytes 38834176 | tf_op jit(solution)/shard_map/reduce_sum | solution.py:236
  137.5 2.6 convolution_bitcast_fusion
  140.1 1.0 reshape.69
  141.2 2.0 convolution_bitcast_fusion.1
  143.1 0.3 copy.17
  143.5 1.0 reshape.67
  144.5 5.6 %concatenate.11 = f32[4204,128]{1,0:T(8,128)S(1)} concatenate(f32[2048,128]{1,0:T(8,128)} %reshape.67, f32[4,128]{1,0:T(4,128)S(1)} %bitcast.130, f32[100,128]{1,0:T(8,128)S(1)} %reshape.68, f32[4,128]{1,0:T(4,128)S(1)} %bitcast.149, f32[2048,128]{1,0:T(8,128)} %reshape.69), dimensions={0} | concatenate | bytes 4304896 | tf_op jit(solution)/shard_map/concatenate | solution.py:177
  150.3 100.8 %shard_map.118 = f32[4608,128]{1,0:T(8,128)S(1)} custom-call(f32[4608,128]{1,0:T(8,128)S(1)} %pad.13.data), custom_call_target="tpu_custom_call" | custom-call | tf_op jit(solution)/shard_map/pallas_call | solution.py:139
  251.1 1.5 fusion.75
  252.6 2.4 reshape.70
  255.0 2.4 reshape.72
  257.3 0.6 reshape.71
  258.0 0.6 slice_bitcast_fusion
  258.6 1.8 add_convert_fusion
  (28 shorter events, 0.6 us)
Async XLA Ops:
  7.2 28.0 %copy-start = (bf16[512,512]{1,0:T(8,128)(2,1)S(1)}, bf16[512,512]{1,0:T(8,128)(2,1)}, u32[]{:S(2)}) copy-start(bf16[512,512]{1,0:T(8,128)(2,1)} %param.9) | copy-start | bytes 1572868
  7.2 28.0 %all-gather.5.cloned.1.call-start = ((), (), s32[]{:S(2)}) async-start(), calls=%async_computation.2 | async-start | bytes 1310720 | tf_op jit(solution)/shard_map/all_gather | solution.py:195
  7.9 76.2 %all-gather.3.cloned.1.call-start = ((), (), s32[]{:S(2)}) async-start(), calls=%async_computation.1 | async-start | bytes 1310720 | tf_op jit(solution)/shard_map/all_gather | solution.py:196
  8.7 40.1 %copy-start.3 = (f32[25,512]{1,0:T(8,128)S(1)}, f32[25,512]{1,0:T(8,128)}, u32[]{:S(2)}) copy-start(f32[25,512]{1,0:T(8,128)} %param.11) | copy-start | bytes 153604
  8.7 249.9 %reduce-scatter.2.cloned.1.call-start = ((), (), s32[]{:S(2)}) async-start(), calls=%async_computation.3 | async-start | bytes 2621440 | tf_op jit(solution)/shard_map/reduce_scatter | solution.py:254
  38.6 15.0 %collective-permute-start = (bf16[2,128,512]{2,1,0:T(8,128)(2,1)S(1)}, bf16[2,128,512]{2,1,0:T(8,128)(2,1)S(1)}, u32[]{:S(2)}, u32[]{:S(2)}) collective-permute-start(bf16[2,128,512]{2,1,0:T(8,128)(2,1)S(1)} %get-tuple-element.40), channel_id=1, source_target_pairs={{0,4},{4,8},{8,12},{12,16},{16,20},{20,24},{24,28},{28,32},{32,36}... | collective-permute-start | bytes 786440 | tf_op jit(solution)/shard_map/ppermute | solution.py:161
  42.0 12.7 %collective-permute-start.1 = (bf16[2,128,512]{2,1,0:T(8,128)(2,1)S(1)}, bf16[2,128,512]{2,1,0:T(8,128)(2,1)S(1)}, u32[]{:S(2)}, u32[]{:S(2)}) collective-permute-start(bf16[2,128,512]{2,1,0:T(8,128)(2,1)S(1)} %get-tuple-element.41), channel_id=1, source_target_pairs={{4,0},{8,4},{12,8},{16,12},{20,16},{24,20},{28,24},{32,28},{36,32}... | collective-permute-start | bytes 786440 | tf_op jit(solution)/shard_map/ppermute | solution.py:164
  48.8 8.1 %copy-start.4 = (f32[512]{0:T(512)S(1)}, f32[512]{0:T(512)}, u32[]{:S(2)}) copy-start(f32[512]{0:T(512)} %param.12) | copy-start | bytes 6148
  56.9 27.2 %copy-start.6 = (bf16[512,512]{1,0:T(8,128)(2,1)S(1)}, bf16[512,512]{1,0:T(8,128)(2,1)}, u32[]{:S(2)}) copy-start(bf16[512,512]{1,0:T(8,128)(2,1)} %param.13) | copy-start | bytes 1572868
  93.0 14.5 %collective-permute-start.2 = (bf16[2,128,512]{2,1,0:T(8,128)(2,1)S(1)}, bf16[2,128,512]{2,1,0:T(8,128)(2,1)S(1)}, u32[]{:S(2)}, u32[]{:S(2)}) collective-permute-start(bf16[2,128,512]{2,1,0:T(8,128)(2,1)S(1)} %get-tuple-element.38), channel_id=1, source_target_pairs={{0,4},{4,8},{8,12},{12,16},{16,20},{20,24},{24,28},{28,32},{32,36}... | collective-permute-start | bytes 786440 | tf_op jit(solution)/shard_map/ppermute | solution.py:161
  94.9 14.4 %copy-start.1 = (f32[8,128,512]{2,1,0:T(8,128)S(1)}, f32[8,128,512]{2,1,0:T(8,128)}, u32[]{:S(2)}) copy-start(f32[8,128,512]{2,1,0:T(8,128)} %get-tuple-element.68) | copy-start | bytes 6291460
  94.9 14.4 %copy-start.5 = (f32[512]{0:T(512)S(1)}, f32[512]{0:T(512)}, u32[]{:S(2)}) copy-start(f32[512]{0:T(512)} %param.10) | copy-start | bytes 6148
  94.9 13.9 %collective-permute-start.3 = (bf16[2,128,512]{2,1,0:T(8,128)(2,1)S(1)}, bf16[2,128,512]{2,1,0:T(8,128)(2,1)S(1)}, u32[]{:S(2)}, u32[]{:S(2)}) collective-permute-start(bf16[2,128,512]{2,1,0:T(8,128)(2,1)S(1)} %get-tuple-element.39), channel_id=1, source_target_pairs={{4,0},{8,4},{12,8},{16,12},{20,16},{24,20},{28,24},{32,28},{36,32}... | collective-permute-start | bytes 786440 | tf_op jit(solution)/shard_map/ppermute | solution.py:164
  252.6 6.0 %copy-start.2 = (bf16[2,128,512]{2,1,0:T(8,128)(2,1)S(1)}, bf16[2,128,512]{2,1,0:T(8,128)(2,1)}, u32[]{:S(2)}) copy-start(bf16[2,128,512]{2,1,0:T(8,128)(2,1)} %param.8) | copy-start | bytes 786436
Sparse Core Ops, SparseCore 0:
  9.8 25.3 all-gather.4
  37.0 22.7 all-gather.2
  118.8 41.1 reduce-scatter.1
where the time goes:
time: 268 us; the launch traced here: 267 us
  Pallas kernels  101 us (38%)
  other arithmetic  57.6 us (21%)
  waiting for transfers between devices  38.6 us (14%)
  starting transfers between devices  21.2 us (8%)
  matrix products  18.8 us (7%)
  local copies, waits for them, and re-layouts  15.9 us (6%)
  between operations  14 us (5%)
    pallas_call x1, Pallas kernels, row_group_allreduce(): pl.pallas_call(body, out_shape=jax.ShapeDtypeStruct((rows, cols), jnp.flo...  101 us
    add x1, other arithmetic, shards(): pre_two + depth_k[5 * row_tap + col_tap] * padded[row_tap:row_tap + nrows...  27.2 us
    all_gather x1, waiting for transfers between devices, shards(): lax.all_gather(inputs, CHAN_AXES, axis=0, tiled=True)  26.5 us
    reduce_sum x1, other arithmetic, shards(): jnp.sum(padded[row_tap:row_tap + nrows, col_tap:col_tap + ncols] * grad_p...  18.7 us
    ppermute x2, starting transfers between devices, extended(): lax.ppermute(lax.slice_in_dim(block, 0, width, axis=dim), axis, backward)  15.8 us
    dot_general x1, matrix products, shards(): jnp.dot(flat_cotan, project_w.T, preferred_element_type=jnp.float32)  8.79 us
    ppermute x2, waiting for transfers between devices, extended(): lax.ppermute(lax.slice_in_dim(block, block.shape[dim] - width, None, axis...  8.28 us
    reduce_sum x1, other arithmetic, shards(): grad_b1 = jnp.sum(flat_act.astype(jnp.float32), axis=0)  7.26 us
  transfers between devices with their start and end apart: 7, of which 5 were waited for; matrix products, arithmetic and copies ran while one was open for 27% of the time, Pallas kernels for 38%

commit v1 on v0

--- a/solution.py
+++ b/solution.py
@@ -31,9 +31,13 @@
     partner = dev(y=1 - iy)
 
     barrier = pltpu.get_barrier_semaphore()
-    for d in (x_next[0], x_next[1], z_next[0], z_next[1], partner):
+    z_peer = [None] + [dev(z=lax.rem(iz + d, nz)) for d in range(1, nz)]
+    peers = [x_next[0], x_next[1], partner] + z_peer[1:]
+    if nx == 2:
+        peers = peers[1:]
+    for d in peers:
         pl.semaphore_signal(barrier, inc=1, device_id=d, device_id_type=MESH_ID)
-    pl.semaphore_wait(barrier, 5)
+    pl.semaphore_wait(barrier, len(peers))
 
     rows = data.shape[0]
     half = rows // 2
@@ -70,22 +74,25 @@
             xs[h, s] = xs[h, s] + data[xblock(h, ix - sg * (s + 2))]
             copies[h].wait_send()
     last = nx - 2
-    for s in range(nz - 1):
-        copies = []
-        for h in range(2):
-            sg = steps[h]
-            src = xs.at[h, last, zblock(iz - sg)] if s == 0 else zs.at[h, s - 1]
-            c = pltpu.make_async_remote_copy(
-                src_ref=src, dst_ref=zs.at[h, s], send_sem=zsend.at[h * nz + s],
-                recv_sem=zrecv.at[h * nz + s], device_id=z_next[h], device_id_type=MESH_ID)
-            c.start()
-            copies.append(c)
-        for h in range(2):
-            sg = steps[h]
-            copies[h].wait_recv()
-            zs[h, s] = zs[h, s] + xs[h, last, zblock(iz - sg * (s + 2))]
-            copies[h].wait_send()
-    zl = nz - 2
+    copies = []
+    for h in range(2):
+        for d in range(1, nz):
+            c = pltpu.make_async_remote_copy(
+                src_ref=xs.at[h, last, zblock(iz + d)], dst_ref=zs.at[h, d - 1],
+                send_sem=zsend.at[h * nz + d], recv_sem=zrecv.at[h * nz + d],
+                device_id=z_peer[d], device_id_type=MESH_ID)
+            c.start()
+            copies.append(c)
+    for c in copies:
+        c.wait_recv()
+    for h in range(2):
+        acc = xs[h, last, zblock(iz)]
+        for d in range(1, nz):
+            acc = acc + zs[h, d - 1]
+        zs[h, nz - 1] = acc
+    for c in copies:
+        c.wait_send()
+    zl = nz - 1
     c = pltpu.make_async_remote_copy(
         src_ref=zs.at[:, zl], dst_ref=ys, send_sem=ysend.at[0], recv_sem=yrecv.at[0],
         device_id=partner, device_id_type=MESH_ID)
@@ -94,19 +101,19 @@
     for h in range(2):
         out[oblock(h, ix, iz)] = zs[h, zl] + ys[h]
     c.wait_send()
-    for s in range(nz - 1):
-        copies = []
-        for h in range(2):
-            sg = steps[h]
-            loc = oblock(h, ix, iz - sg * s)
-            c = pltpu.make_async_remote_copy(
-                src_ref=out.at[loc], dst_ref=out.at[loc], send_sem=gzsend.at[h * nz + s],
-                recv_sem=gzrecv.at[h * nz + s], device_id=z_next[h], device_id_type=MESH_ID)
-            c.start()
-            copies.append(c)
-        for h in range(2):
-            copies[h].wait_recv()
-            copies[h].wait_send()
+    copies = []
+    for h in range(2):
+        loc = oblock(h, ix, iz)
+        for d in range(1, nz):
+            c = pltpu.make_async_remote_copy(
+                src_ref=out.at[loc], dst_ref=out.at[loc], send_sem=gzsend.at[h * nz + d],
+                recv_sem=gzrecv.at[h * nz + d], device_id=z_peer[d], device_id_type=MESH_ID)
+            c.start()
+            copies.append(c)
+    for c in copies:
+        c.wait_recv()
+    for c in copies:
+        c.wait_send()
     for s in range(nx - 1):
         copies = []
         for h in range(2):
@@ -143,7 +150,7 @@
         out_specs=pl.BlockSpec(memory_space=pltpu.VMEM),
         scratch_shapes=[
             pltpu.VMEM((2, nx - 1, bx, cols), jnp.float32),
-            pltpu.VMEM((2, nz - 1, bz, cols), jnp.float32),
+            pltpu.VMEM((2, nz, bz, cols), jnp.float32),
             pltpu.VMEM((2, bz, cols), jnp.float32),
         ] + sems,
         compiler_params=pltpu.CompilerParams(collective_id=0, has_side_effects=True,

time: 268 us -> 247 us (0.922)
  Pallas kernels: 101 us -> 78.1 us
    pallas_call x1, Pallas kernels: 101 us -> 78.1 us  [row_group_allreduce(): pl.pallas_call(body, out_shape=jax.ShapeDtypeStruct((rows, cols), jnp.flo...]
  transfers between devices with their start and end apart: 7 -> 7, of which waited for: 5 -> 5; matrix products, arithmetic and copies ran while one was open for 27% -> 29% of each run, Pallas kernels for 38% -> 32%
where the time goes in v1:
time: 247 us; the launch traced here: 244 us
  Pallas kernels  78.1 us (32%)
  other arithmetic  57.6 us (23%)
  waiting for transfers between devices  38.6 us (16%)
  starting transfers between devices  21.2 us (9%)
  matrix products  18.8 us (8%)
  local copies, waits for them, and re-layouts  15.9 us (6%)
  between operations  14 us (6%)
    pallas_call x1, Pallas kernels, row_group_allreduce(): pl.pallas_call(body, out_shape=jax.ShapeDtypeStruct((rows, cols), jnp.flo...  78.1 us
    add x1, other arithmetic, shards(): pre_two + depth_k[5 * row_tap + col_tap] * padded[row_tap:row_tap + nrows...  27.2 us
    all_gather x1, waiting for transfers between devices, shards(): lax.all_gather(inputs, CHAN_AXES, axis=0, tiled=True)  26.5 us
    reduce_sum x1, other arithmetic, shards(): jnp.sum(padded[row_tap:row_tap + nrows, col_tap:col_tap + ncols] * grad_p...  18.7 us
    ppermute x2, starting transfers between devices, extended(): lax.ppermute(lax.slice_in_dim(block, 0, width, axis=dim), axis, backward)  15.8 us
    dot_general x1, matrix products, shards(): jnp.dot(flat_cotan, project_w.T, preferred_element_type=jnp.float32)  8.79 us
    ppermute x2, waiting for transfers between devices, extended(): lax.ppermute(lax.slice_in_dim(block, block.shape[dim] - width, None, axis...  8.28 us
    reduce_sum x1, other arithmetic, shards(): grad_b1 = jnp.sum(flat_act.astype(jnp.float32), axis=0)  7.26 us
  transfers between devices with their start and end apart: 7, of which 5 were waited for; matrix products, arithmetic and copies ran while one was open for 29% of the time, Pallas kernels for 32%

profile of v1, /device:TPU:8, one launch (start us, length us, event | category | flops | bytes accessed | tf_op | source)
XLA Modules:
  0.0 244.2 jit_solution(1539073317169247700)
XLA Ops:
  7.2 0.7 all-gather.5.cloned.1.call-update
  8.0 0.7 all-gather.3.cloned.1.call-update
  8.7 26.5 %all-gather.5.cloned.1.call-done = bf16[8,128,512]{2,1,0:T(8,128)(2,1)} async-done(((bf16[2,128,512]{2,1,0:T(8,128)(2,1)}), bf16[8,128,512]{2,1,0:T(8,128)(2,1)}) %all-gather.5.cloned.1.call-update) | async-done | bytes 1048592 | tf_op jit(solution)/shard_map/all_gather | solution.py:202
  35.2 3.4 %multiply_convert_fusion.1 = (bf16[8,128,512]{2,1,0:T(8,128)(2,1)S(1)}, f32[8,128,512]{2,1,0:T(8,128)}) fusion(f32[512]{0:T(512)} %param.10, bf16[8,128,512]{2,1,0:T(8,128)(2,1)} %all-gather.5.cloned.1.call-done, bf16[512,512]{1,0:T(8,128)(2,1)S(1)} %copy-done), kind=kOutput, calls=%fused_computation.121 | convolution fusion | flops 540016640 | bytes 4720640 | tf_op jit(solution)/shard_map/dot_general | solution.py:210
  38.6 3.4 %collective-permute-start = (bf16[2,128,512]{2,1,0:T(8,128)(2,1)S(1)}, bf16[2,128,512]{2,1,0:T(8,128)(2,1)S(1)}, u32[]{:S(2)}, u32[]{:S(2)}) collective-permute-start(bf16[2,128,512]{2,1,0:T(8,128)(2,1)S(1)} %get-tuple-element.40), channel_id=1, source_target_pairs={{0,4},{4,8},{8,12},{12,16},{16,20},{20,24},{24,28},{28,32},{32,36}... | collective-permute-start | bytes 786440 | tf_op jit(solution)/shard_map/ppermute | solution.py:168
  42.0 6.8 %collective-permute-start.1 = (bf16[2,128,512]{2,1,0:T(8,128)(2,1)S(1)}, bf16[2,128,512]{2,1,0:T(8,128)(2,1)S(1)}, u32[]{:S(2)}, u32[]{:S(2)}) collective-permute-start(bf16[2,128,512]{2,1,0:T(8,128)(2,1)S(1)} %get-tuple-element.41), channel_id=1, source_target_pairs={{4,0},{8,4},{12,8},{16,12},{20,16},{24,20},{28,24},{32,28},{36,32}... | collective-permute-start | bytes 786440 | tf_op jit(solution)/shard_map/ppermute | solution.py:171
  48.8 4.8 %collective-permute-done = bf16[2,128,512]{2,1,0:T(8,128)(2,1)S(1)} collective-permute-done((bf16[2,128,512]{2,1,0:T(8,128)(2,1)S(1)}, bf16[2,128,512]{2,1,0:T(8,128)(2,1)S(1)}, u32[]{:S(2)}, u32[]{:S(2)}) %collective-permute-start) | collective-permute-done | bytes 262176 | tf_op jit(solution)/shard_map/ppermute | solution.py:168
  53.6 1.1 collective-permute-done.1
  54.7 2.2 fusion.68
  56.9 27.2 %multiply_add_fusion = f32[8,128,512]{2,1,0:T(8,128)} fusion(f32[12,132,512]{2,1,0:T(8,128)} %fusion.68, f32[512]{0:T(512)S(1)} %bitcast.88, f32[512]{0:T(512)S(1)} %bitcast.90, f32[512]{0:T(512)S(1)} %bitcast.94, f32[512]{0:T(512)S(1)} %bitcast.96, f32[512]{0:T(512)S(1)} %bitcast.98, f32[512]{0:T(512)S(1)} %bitcast.100, f32[512]{0:T(512)S(1)} %bitcast.102, ...), kind=kLoop, calls=%fused_computation.120 | loop fusion | flops 26214400 | bytes 54579200 | tf_op jit(solution)/shard_map/add | solution.py:223
  84.1 8.8 %fusion.36 = (f32[512]{0:T(512)S(1)}, f32[512]{0:T(512)S(1)}, f32[512]{0:T(512)S(1)}, f32[512]{0:T(512)S(1)}, f32[512]{0:T(512)S(1)}, /*index=5*/f32[512]{0:T(51...) fusion(f32[12,132,512]{2,1,0:T(8,128)} %fusion.68, f32[8,128,512]{2,1,0:T(8,128)} %multiply_add_fusion, ...), kind=kOutput, calls=%fused_computation.66 | convolution fusion | flops 550498304 | bytes 19415040 | tf_op jit(solution)/shard_map/dot_general | solution.py:230
  93.0 1.9 collective-permute-start.2
  94.9 9.0 %collective-permute-start.3 = (bf16[2,128,512]{2,1,0:T(8,128)(2,1)S(1)}, bf16[2,128,512]{2,1,0:T(8,128)(2,1)S(1)}, u32[]{:S(2)}, u32[]{:S(2)}) collective-permute-start(bf16[2,128,512]{2,1,0:T(8,128)(2,1)S(1)} %get-tuple-element.39), channel_id=1, source_target_pairs={{4,0},{8,4},{12,8},{16,12},{20,16},{24,20},{28,24},{32,28},{36,32}... | collective-permute-start | bytes 786440 | tf_op jit(solution)/shard_map/ppermute | solution.py:171
  103.9 3.5 %collective-permute-done.2 = bf16[2,128,512]{2,1,0:T(8,128)(2,1)S(1)} collective-permute-done((bf16[2,128,512]{2,1,0:T(8,128)(2,1)S(1)}, bf16[2,128,512]{2,1,0:T(8,128)(2,1)S(1)}, u32[]{:S(2)}, u32[]{:S(2)}) %collective-permute-start.2) | collective-permute-done | bytes 262176 | tf_op jit(solution)/shard_map/ppermute | solution.py:168
  107.5 1.3 collective-permute-done.3
  108.8 0.5 fusion.62
  109.3 7.3 %convert_reduce_fusion.1 = (f32[512]{0:T(512)S(1)}, bf16[8,128,512]{2,1,0:T(8,128)(2,1)S(1)}) fusion(f32[8,128,512]{2,1,0:T(8,128)S(1)} %copy-done.1, f32[512]{0:T(512)S(1)} %copy-done.5, f32[12,132,512]{2,1,0:T(8,128)S(1)} %fusion.62, f32[512]{0:T(512)S(1)} %bitcast.89, f32[512]{0:T(512)S(1)} %bitcast.91, f32[512]{0:T(512)S(1)} %bitcast.95, ...), kind=kLoop, calls=%fused_computation.118 | loop fusion | flops 32505344 | bytes 55629824 | tf_op jit(solution)/shard_map/reduce_sum | solution.py:256
  116.6 2.1 fusion.69
  118.7 18.7 %fusion.37 = (f32[512]{0:T(512)S(1)}, f32[512]{0:T(512)S(1)}, f32[512]{0:T(512)S(1)}, f32[512]{0:T(512)S(1)}, f32[512]{0:T(512)S(1)}, /*index=5*/f32[512]{0:T(51...) fusion(bf16[8,128,512]{2,1,0:T(8,128)(2,1)S(1)} %get-tuple-elem, ...), kind=kLoop, calls=%fused_computation.67 | loop fusion | flops 19389440 | bytes 38834176 | tf_op jit(solution)/shard_map/reduce_sum | solution.py:243
  137.5 2.6 %convolution_bitcast_fusion = f32[512,512]{1,0:T(8,128)S(1)} fusion(bf16[8,128,512]{2,1,0:T(8,128)(2,1)} %all-gather.3.cloned.1.call-done, f32[8,128,512]{2,1,0:T(8,128)} %multiply_add_fusion), kind=kOutput, calls=%fused_computation.132 | convolution fusion | flops 539492352 | bytes 4194304 | tf_op jit(solution)/shard_map/dot_general | solution.py:229
  140.1 1.0 reshape.69
  141.2 2.0 convolution_bitcast_fusion.1
  143.1 0.3 copy.17
  143.5 1.0 reshape.67
  144.5 5.6 %concatenate.11 = f32[4204,128]{1,0:T(8,128)S(1)} concatenate(f32[2048,128]{1,0:T(8,128)} %reshape.67, f32[4,128]{1,0:T(4,128)S(1)} %bitcast.130, f32[100,128]{1,0:T(8,128)S(1)} %reshape.68, f32[4,128]{1,0:T(4,128)S(1)} %bitcast.149, f32[2048,128]{1,0:T(8,128)} %reshape.69), dimensions={0} | concatenate | bytes 4304896 | tf_op jit(solution)/shard_map/concatenate | solution.py:184
  150.3 78.1 %shard_map.118 = f32[4608,128]{1,0:T(8,128)S(1)} custom-call(f32[4608,128]{1,0:T(8,128)S(1)} %pad.13.data), custom_call_target="tpu_custom_call" | custom-call | tf_op jit(solution)/shard_map/pallas_call | solution.py:146
  228.4 1.5 fusion.75
  229.9 2.4 reshape.70
  232.3 2.4 reshape.72
  234.6 0.6 reshape.71
  235.2 0.6 slice_bitcast_fusion
  235.8 1.8 add_convert_fusion
  (28 shorter events, 0.6 us)
Async XLA Ops:
  7.2 28.0 %copy-start = (bf16[512,512]{1,0:T(8,128)(2,1)S(1)}, bf16[512,512]{1,0:T(8,128)(2,1)}, u32[]{:S(2)}) copy-start(bf16[512,512]{1,0:T(8,128)(2,1)} %param.9) | copy-start | bytes 1572868
  7.2 28.0 %all-gather.5.cloned.1.call-start = ((), (), s32[]{:S(2)}) async-start(), calls=%async_computation.2 | async-start | bytes 1310720 | tf_op jit(solution)/shard_map/all_gather | solution.py:202
  7.9 76.2 %all-gather.3.cloned.1.call-start = ((), (), s32[]{:S(2)}) async-start(), calls=%async_computation.1 | async-start | bytes 1310720 | tf_op jit(solution)/shard_map/all_gather | solution.py:203
  8.7 40.1 %copy-start.3 = (f32[25,512]{1,0:T(8,128)S(1)}, f32[25,512]{1,0:T(8,128)}, u32[]{:S(2)}) copy-start(f32[25,512]{1,0:T(8,128)} %param.11) | copy-start | bytes 153604
  8.7 227.2 %reduce-scatter.2.cloned.1.call-start = ((), (), s32[]{:S(2)}) async-start(), calls=%async_computation.3 | async-start | bytes 2621440 | tf_op jit(solution)/shard_map/reduce_scatter | solution.py:261
  38.6 15.0 %collective-permute-start = (bf16[2,128,512]{2,1,0:T(8,128)(2,1)S(1)}, bf16[2,128,512]{2,1,0:T(8,128)(2,1)S(1)}, u32[]{:S(2)}, u32[]{:S(2)}) collective-permute-start(bf16[2,128,512]{2,1,0:T(8,128)(2,1)S(1)} %get-tuple-element.40), channel_id=1, source_target_pairs={{0,4},{4,8},{8,12},{12,16},{16,20},{20,24},{24,28},{28,32},{32,36}... | collective-permute-start | bytes 786440 | tf_op jit(solution)/shard_map/ppermute | solution.py:168
  42.0 12.7 %collective-permute-start.1 = (bf16[2,128,512]{2,1,0:T(8,128)(2,1)S(1)}, bf16[2,128,512]{2,1,0:T(8,128)(2,1)S(1)}, u32[]{:S(2)}, u32[]{:S(2)}) collective-permute-start(bf16[2,128,512]{2,1,0:T(8,128)(2,1)S(1)} %get-tuple-element.41), channel_id=1, source_target_pairs={{4,0},{8,4},{12,8},{16,12},{20,16},{24,20},{28,24},{32,28},{36,32}... | collective-permute-start | bytes 786440 | tf_op jit(solution)/shard_map/ppermute | solution.py:171
  48.8 8.1 %copy-start.4 = (f32[512]{0:T(512)S(1)}, f32[512]{0:T(512)}, u32[]{:S(2)}) copy-start(f32[512]{0:T(512)} %param.12) | copy-start | bytes 6148
  56.9 27.2 %copy-start.6 = (bf16[512,512]{1,0:T(8,128)(2,1)S(1)}, bf16[512,512]{1,0:T(8,128)(2,1)}, u32[]{:S(2)}) copy-start(bf16[512,512]{1,0:T(8,128)(2,1)} %param.13) | copy-start | bytes 1572868
  93.0 14.5 %collective-permute-start.2 = (bf16[2,128,512]{2,1,0:T(8,128)(2,1)S(1)}, bf16[2,128,512]{2,1,0:T(8,128)(2,1)S(1)}, u32[]{:S(2)}, u32[]{:S(2)}) collective-permute-start(bf16[2,128,512]{2,1,0:T(8,128)(2,1)S(1)} %get-tuple-element.38), channel_id=1, source_target_pairs={{0,4},{4,8},{8,12},{12,16},{16,20},{20,24},{24,28},{28,32},{32,36}... | collective-permute-start | bytes 786440 | tf_op jit(solution)/shard_map/ppermute | solution.py:168
  94.9 14.4 %copy-start.1 = (f32[8,128,512]{2,1,0:T(8,128)S(1)}, f32[8,128,512]{2,1,0:T(8,128)}, u32[]{:S(2)}) copy-start(f32[8,128,512]{2,1,0:T(8,128)} %get-tuple-element.68) | copy-start | bytes 6291460
  94.9 14.4 %copy-start.5 = (f32[512]{0:T(512)S(1)}, f32[512]{0:T(512)}, u32[]{:S(2)}) copy-start(f32[512]{0:T(512)} %param.10) | copy-start | bytes 6148
  94.9 13.9 %collective-permute-start.3 = (bf16[2,128,512]{2,1,0:T(8,128)(2,1)S(1)}, bf16[2,128,512]{2,1,0:T(8,128)(2,1)S(1)}, u32[]{:S(2)}, u32[]{:S(2)}) collective-permute-start(bf16[2,128,512]{2,1,0:T(8,128)(2,1)S(1)} %get-tuple-element.39), channel_id=1, source_target_pairs={{4,0},{8,4},{12,8},{16,12},{20,16},{24,20},{28,24},{32,28},{36,32}... | collective-permute-start | bytes 786440 | tf_op jit(solution)/shard_map/ppermute | solution.py:171
  229.9 6.0 %copy-start.2 = (bf16[2,128,512]{2,1,0:T(8,128)(2,1)S(1)}, bf16[2,128,512]{2,1,0:T(8,128)(2,1)}, u32[]{:S(2)}) copy-start(bf16[2,128,512]{2,1,0:T(8,128)(2,1)} %param.8) | copy-start | bytes 786436
Sparse Core Ops, SparseCore 0:
  9.8 25.3 all-gather.4
  37.0 22.7 all-gather.2
  118.8 41.1 reduce-scatter.1

commit v2 on v1

--- a/solution.py
+++ b/solution.py
@@ -158,6 +158,63 @@
     )(flat)
 
 
+def _chan_gather_kernel(first, second, out_first, out_second, sems):
+    coords = [lax.axis_index(a) for a in ALL_AXES]
+    hi, core = coords[3], coords[4]
+
+    def dev(h, c):
+        return (coords[0], coords[1], coords[2], h, c)
+
+    me = hi * 2 + core
+    across = hi * 2 + (1 - core)
+    over = (1 - hi) * 2 + core
+    pair, far = dev(hi, 1 - core), dev(1 - hi, core)
+
+    barrier = pltpu.get_barrier_semaphore()
+    for d in (pair, far):
+        pl.semaphore_signal(barrier, inc=1, device_id=d, device_id_type=MESH_ID)
+    pl.semaphore_wait(barrier, 2)
+
+    sources = (first, second)
+    outs = (out_first, out_second)
+    step_one = []
+    for k in range(2):
+        for j, target in enumerate((pair, far)):
+            c = pltpu.make_async_remote_copy(
+                src_ref=sources[k], dst_ref=outs[k].at[me], send_sem=sems.at[0, k, j],
+                recv_sem=sems.at[1, k, j], device_id=target, device_id_type=MESH_ID)
+            c.start()
+            step_one.append(c)
+    for k in range(2):
+        outs[k][me] = sources[k][...]
+    for c in step_one:
+        c.wait_recv()
+    relay = []
+    for k in range(2):
+        c = pltpu.make_async_remote_copy(
+            src_ref=outs[k].at[over], dst_ref=outs[k].at[over], send_sem=sems.at[0, k, 2],
+            recv_sem=sems.at[1, k, 2], device_id=pair, device_id_type=MESH_ID)
+        c.start()
+        relay.append(c)
+    for c in relay:
+        c.wait_recv()
+    for c in step_one + relay:
+        c.wait_send()
+
+
+def chan_gather(first, second):
+    shape = (4,) + first.shape
+    result = pl.pallas_call(
+        _chan_gather_kernel,
+        out_shape=(jax.ShapeDtypeStruct(shape, first.dtype), jax.ShapeDtypeStruct(shape, second.dtype)),
+        in_specs=[pl.BlockSpec(memory_space=pltpu.VMEM)] * 2,
+        out_specs=(pl.BlockSpec(memory_space=pltpu.VMEM),) * 2,
+        scratch_shapes=[pltpu.SemaphoreType.DMA((2, 2, 3))],
+        compiler_params=pltpu.CompilerParams(collective_id=1, has_side_effects=True),
+    )(first, second)
+    return tuple(r.reshape((-1,) + first.shape[1:]) for r in result)
+
+
 def extended(block, sides, width):
     for axis, dim in sides:
         count = 1
@@ -198,10 +255,7 @@
 
 
 def shards(inputs, cotangent, expand_w, expand_b, depth_k, depth_b, project_w):
-    rows_in, rows_cot = (
-        lax.all_gather(inputs, CHAN_AXES, axis=0, tiled=True),
-        lax.all_gather(cotangent, CHAN_AXES, axis=0, tiled=True),
-    )
+    rows_in, rows_cot = chan_gather(inputs, cotangent)
     nrows, ncols, cin = rows_in.shape
     hslice = expand_w.shape[1]
     flat_inputs = rows_in.reshape(nrows * ncols, cin)

time: 247 us -> 212 us (0.86)
  waiting for transfers between devices: 38.6 us -> 11.1 us
  other arithmetic: 57.6 us -> 36.1 us
  Pallas kernels: 78.1 us -> 96.7 us
  matrix products: 18.8 us -> 12.8 us
    add x1 -> x0, other arithmetic: 27.2 us -> none  [shards(): pre_two + depth_k[5 * row_tap + col_tap] * padded[row_tap:row_tap + nrows...]
    all_gather x2 -> x0, waiting for transfers between devices: 26.5 us -> none  [the longest x1 26.5 us: shards(): lax.all_gather(inputs, CHAN_AXES, axis=0, tiled=True)]
    pallas_call x0 -> x1, Pallas kernels: none -> 19.3 us  [chan_gather(): pl.pallas_call(_chan_gather_kernel, out_shape=(jax.ShapeDtypeStruct(shape...]
    convert_element_type x0 -> x1, other arithmetic: none -> 7.36 us  [shards(): mixed = mixed.astype(jnp.bfloat16).reshape(nrows * ncols, hslice)]
    dot_general x1, matrix products: 8.79 us -> 3.42 us  [shards(): jnp.dot(flat_cotan, project_w.T, preferred_element_type=jnp.float32)]
  transfers between devices with their start and end apart: 7 -> 5, of which waited for: 5 -> 4; matrix products, arithmetic and copies ran while one was open for 29% -> 19% of each run, Pallas kernels for 32% -> 37%
where the time goes in v2:
time: 212 us; the launch traced here: 211 us
  Pallas kernels  96.7 us (46%)
  other arithmetic  36.1 us (17%)
  starting transfers between devices  23.1 us (11%)
  local copies, waits for them, and re-layouts  16.7 us (8%)
  between operations  14.3 us (7%)
  matrix products  12.8 us (6%)
  waiting for transfers between devices  11.1 us (5%)
    pallas_call x1, Pallas kernels, row_group_allreduce(): pl.pallas_call(body, out_shape=jax.ShapeDtypeStruct((rows, cols), jnp.flo...  77.3 us
    pallas_call x1, Pallas kernels, chan_gather(): pl.pallas_call(_chan_gather_kernel, out_shape=(jax.ShapeDtypeStruct(shape...  19.3 us
    reduce_sum x1, other arithmetic, shards(): jnp.sum(padded[row_tap:row_tap + nrows, col_tap:col_tap + ncols] * grad_p...  18.6 us
    ppermute x2, starting transfers between devices, extended(): lax.ppermute(lax.slice_in_dim(block, 0, width, axis=dim), axis, backward)  17.7 us
    ppermute x2, waiting for transfers between devices, extended(): lax.ppermute(lax.slice_in_dim(block, block.shape[dim] - width, None, axis...  8.72 us
    convert_element_type x1, other arithmetic, shards(): mixed = mixed.astype(jnp.bfloat16).reshape(nrows * ncols, hslice)  7.36 us
    reduce_sum x1, other arithmetic, shards(): grad_b1 = jnp.sum(flat_act.astype(jnp.float32), axis=0)  7.26 us
    concatenate x1, local copies, waits for them, and re-layouts, row_group_sum(): flat = jnp.concatenate([t.reshape(-1, lanes) for t in terms], axis=0)  5.53 us
  transfers between devices with their start and end apart: 5, of which 4 were waited for; matrix products, arithmetic and copies ran while one was open for 19% of the time, Pallas kernels for 37%

profile of v2, /device:TPU:8, one launch (start us, length us, event | category | flops | bytes accessed | tf_op | source)
XLA Modules:
  0.0 210.9 jit_solution(11656415055161628340)
XLA Ops:
  7.2 0.0 reduce-scatter.2.cloned.1.call-start
  7.2 19.3 %shard_map.118 = (bf16[4,2,128,512]{3,2,1,0:T(8,128)(2,1)}, bf16[4,2,128,512]{3,2,1,0:T(8,128)(2,1)}) custom-call(bf16[2,128,512]{2,1,0:T(8,128)(2,1)} %first.1, bf16[2,128,512]{2,1,0:T(8,128)(2,1)} %second.1), custom_call_target="tpu_custom_call" | custom-call | tf_op jit(solution)/shard_map/pallas_call | solution.py:207
  26.6 2.1 %multiply_convert_fusion.1 = (bf16[8,128,512]{2,1,0:T(8,128)(2,1)S(1)}, f32[8,128,512]{2,1,0:T(8,128)S(1)}) fusion(f32[512]{0:T(512)} %param.10, bf16[8,128,512]{2,1,0:T(8,128)(2,1)} %bitcast.160, bf16[512,512]{1,0:T(8,128)(2,1)S(1)} %copy-done), kind=kOutput, calls=%fused_computation.121 | convolution fusion | flops 540016640 | bytes 4720640 | tf_op jit(solution)/shard_map/dot_general | solution.py:264
  28.8 3.4 %collective-permute-start = (bf16[2,128,512]{2,1,0:T(8,128)(2,1)S(1)}, bf16[2,128,512]{2,1,0:T(8,128)(2,1)S(1)}, u32[]{:S(2)}, u32[]{:S(2)}) collective-permute-start(bf16[2,128,512]{2,1,0:T(8,128)(2,1)S(1)} %get-tuple-element.46), channel_id=1, source_target_pairs={{0,4},{4,8},{8,12},{12,16},{16,20},{20,24},{24,28},{28,32},{32,36}... | collective-permute-start | bytes 786440 | tf_op jit(solution)/shard_map/ppermute | solution.py:225
  32.2 9.0 %collective-permute-start.1 = (bf16[2,128,512]{2,1,0:T(8,128)(2,1)S(1)}, bf16[2,128,512]{2,1,0:T(8,128)(2,1)S(1)}, u32[]{:S(2)}, u32[]{:S(2)}) collective-permute-start(bf16[2,128,512]{2,1,0:T(8,128)(2,1)S(1)} %get-tuple-element.47), channel_id=1, source_target_pairs={{4,0},{8,4},{12,8},{16,12},{20,16},{24,20},{28,24},{32,28},{36,32}... | collective-permute-start | bytes 786440 | tf_op jit(solution)/shard_map/ppermute | solution.py:228
  41.3 4.8 %collective-permute-done = bf16[2,128,512]{2,1,0:T(8,128)(2,1)S(1)} collective-permute-done((bf16[2,128,512]{2,1,0:T(8,128)(2,1)S(1)}, bf16[2,128,512]{2,1,0:T(8,128)(2,1)S(1)}, u32[]{:S(2)}, u32[]{:S(2)}) %collective-permute-start) | collective-permute-done | bytes 262176 | tf_op jit(solution)/shard_map/ppermute | solution.py:225
  46.1 1.2 collective-permute-done.1
  47.3 0.5 fusion.68
  47.8 7.4 %multiply_convert_fusion = (bf16[8,128,512]{2,1,0:T(8,128)(2,1)}, f32[8,128,512]{2,1,0:T(8,128)S(1)}) fusion(f32[12,132,512]{2,1,0:T(8,128)S(1)} %fusion.68, f32[512]{0:T(512)S(1)} %bitcast.91, f32[512]{0:T(512)S(1)} %bitcast.93, f32[512]{0:T(512)S(1)} %bitcast.97, f32[512]{0:T(512)S(1)} %bitcast.99, f32[512]{0:T(512)S(1)} %bitcast.101, ...), kind=kLoop, calls=%fused_computation.117 | loop fusion | flops 28835840 | bytes 55627776 | tf_op jit(solution)/shard_map/convert_element_type | solution.py:282
  55.2 3.4 %fusion.36 = (f32[512]{0:T(512)S(1)}, f32[512]{0:T(512)S(1)}, f32[512]{0:T(512)S(1)}, f32[512]{0:T(512)S(1)}, f32[512]{0:T(512)S(1)}, /*index=5*/f32[512]{0:T(51...) fusion(f32[12,132,512]{2,1,0:T(8,128)S(1)} %fusion.68, f32[8,128,512]{2,1,0:T(8,128)S(1)} %get-tuple-element.37, ...), kind=kOutput, calls=%fused_computation.66 | convolution fusion | flops 550498304 | bytes 19415040 | tf_op jit(solution)/shard_map/dot_general | solution.py:284
  58.7 1.9 collective-permute-start.2
  60.6 8.7 %collective-permute-start.3 = (bf16[2,128,512]{2,1,0:T(8,128)(2,1)S(1)}, bf16[2,128,512]{2,1,0:T(8,128)(2,1)S(1)}, u32[]{:S(2)}, u32[]{:S(2)}) collective-permute-start(bf16[2,128,512]{2,1,0:T(8,128)(2,1)S(1)} %get-tuple-element.45), channel_id=1, source_target_pairs={{4,0},{8,4},{12,8},{16,12},{20,16},{24,20},{28,24},{32,28},{36,32}... | collective-permute-start | bytes 786440 | tf_op jit(solution)/shard_map/ppermute | solution.py:228
  69.4 3.9 %collective-permute-done.2 = bf16[2,128,512]{2,1,0:T(8,128)(2,1)S(1)} collective-permute-done((bf16[2,128,512]{2,1,0:T(8,128)(2,1)S(1)}, bf16[2,128,512]{2,1,0:T(8,128)(2,1)S(1)}, u32[]{:S(2)}, u32[]{:S(2)}) %collective-permute-start.2) | collective-permute-done | bytes 262176 | tf_op jit(solution)/shard_map/ppermute | solution.py:225
  73.3 1.2 collective-permute-done.3
  74.5 0.5 fusion.62
  75.0 7.3 %convert_reduce_fusion.1 = (f32[512]{0:T(512)S(1)}, bf16[8,128,512]{2,1,0:T(8,128)(2,1)S(1)}) fusion(f32[8,128,512]{2,1,0:T(8,128)S(1)} %get-tuple-element.74, f32[512]{0:T(512)S(1)} %copy-done.5, f32[12,132,512]{2,1,0:T(8,128)S(1)} %fusion.62, f32[512]{0:T(512)S(1)} %bitcast.92, f32[512]{0:T(512)S(1)} %bitcast.94, f32[512]{0:T(512)S(1)} %bitcast.98, ...), kind=kLoop, calls=%fused_computation.118 | loop fusion | flops 32505344 | bytes 55629824 | tf_op jit(solution)/shard_map/reduce_sum | solution.py:310
  82.3 2.1 fusion.69
  84.4 3.2 %fusion.81 = f32[512,512]{1,0:T(8,128)} fusion(bf16[1024,512]{1,0:T(8,128)(2,1)} %bitcast.82, bf16[1024,512]{1,0:T(8,128)(2,1)} %bitcast.162), kind=kOutput, calls=%fused_computation.146 | convolution fusion | flops 536870912 | bytes 3145728 | tf_op jit(solution)/shard_map/dot_general | solution.py:283
  87.6 2.3 %reshape.73 = f32[2048,128]{1,0:T(8,128)} reshape(f32[512,512]{1,0:T(8,128)} %fusion.81) | data formatting | bytes 2097152 | tf_op jit(solution)/shard_map/reshape | solution.py:241
  89.9 18.6 %fusion.37 = (f32[512]{0:T(512)S(1)}, f32[512]{0:T(512)S(1)}, f32[512]{0:T(512)S(1)}, f32[512]{0:T(512)S(1)}, f32[512]{0:T(512)S(1)}, /*index=5*/f32[512]{0:T(51...) fusion(bf16[8,128,512]{2,1,0:T(8,128)(2,1)S(1)} %get-tuple-elem, ...), kind=kLoop, calls=%fused_computation.67 | loop fusion | flops 19389440 | bytes 38834176 | tf_op jit(solution)/shard_map/reduce_sum | solution.py:297
  108.6 0.1 stack.103
  108.7 2.0 fusion.80
  110.7 1.0 reshape.70
  111.7 5.5 %concatenate.11 = f32[4204,128]{1,0:T(8,128)S(1)} concatenate(f32[2048,128]{1,0:T(8,128)} %reshape.70, f32[4,128]{1,0:T(4,128)S(1)} %bitcast.133, f32[100,128]{1,0:T(8,128)S(1)} %reshape.71, f32[4,128]{1,0:T(4,128)S(1)} %bitcast.152, f32[2048,128]{1,0:T(8,128)} %reshape.73), dimensions={0} | concatenate | bytes 4304896 | tf_op jit(solution)/shard_map/concatenate | solution.py:241
  117.2 0.2 pad.13.data
  117.4 77.3 %shard_map.119 = f32[4608,128]{1,0:T(8,128)S(1)} custom-call(f32[4608,128]{1,0:T(8,128)S(1)} %pad.13.data), custom_call_target="tpu_custom_call" | custom-call | tf_op jit(solution)/shard_map/pallas_call | solution.py:146
  194.8 1.5 fusion.75
  196.2 2.4 %reshape.76 = f32[512,512]{1,0:T(8,128)} reshape(f32[2048,128]{1,0:T(8,128)} %get-tuple-element.40) | data formatting | bytes 2097152 | tf_op jit(solution)/shard_map/reshape | solution.py:252
  198.6 0.6 reshape.75
  199.3 2.4 %reshape.74 = f32[512,512]{1,0:T(8,128)} reshape(f32[2048,128]{1,0:T(8,128)} %get-tuple-element.41) | data formatting | bytes 2097152 | tf_op jit(solution)/shard_map/reshape | solution.py:252
  201.6 0.6 slice_bitcast_fusion
  202.2 1.8 add_convert_fusion
  (24 shorter events, 0.2 us)
Async XLA Ops:
  7.2 19.4 %copy-start = (bf16[512,512]{1,0:T(8,128)(2,1)S(1)}, bf16[512,512]{1,0:T(8,128)(2,1)}, u32[]{:S(2)}) copy-start(bf16[512,512]{1,0:T(8,128)(2,1)} %param.9) | copy-start | bytes 1572868
  7.2 195.0 %reduce-scatter.2.cloned.1.call-start = ((), (), s32[]{:S(2)}) async-start(), calls=%async_computation.1 | async-start | bytes 2621440 | tf_op jit(solution)/shard_map/reduce_scatter | solution.py:315
  26.6 14.6 %copy-start.3 = (f32[25,512]{1,0:T(8,128)S(1)}, f32[25,512]{1,0:T(8,128)}, u32[]{:S(2)}) copy-start(f32[25,512]{1,0:T(8,128)} %param.11) | copy-start | bytes 153604
  28.8 17.3 %collective-permute-start = (bf16[2,128,512]{2,1,0:T(8,128)(2,1)S(1)}, bf16[2,128,512]{2,1,0:T(8,128)(2,1)S(1)}, u32[]{:S(2)}, u32[]{:S(2)}) collective-permute-start(bf16[2,128,512]{2,1,0:T(8,128)(2,1)S(1)} %get-tuple-element.46), channel_id=1, source_target_pairs={{0,4},{4,8},{8,12},{12,16},{16,20},{20,24},{24,28},{28,32},{32,36}... | collective-permute-start | bytes 786440 | tf_op jit(solution)/shard_map/ppermute | solution.py:225
  32.2 15.1 %collective-permute-start.1 = (bf16[2,128,512]{2,1,0:T(8,128)(2,1)S(1)}, bf16[2,128,512]{2,1,0:T(8,128)(2,1)S(1)}, u32[]{:S(2)}, u32[]{:S(2)}) collective-permute-start(bf16[2,128,512]{2,1,0:T(8,128)(2,1)S(1)} %get-tuple-element.47), channel_id=1, source_target_pairs={{4,0},{8,4},{12,8},{16,12},{20,16},{24,20},{28,24},{32,28},{36,32}... | collective-permute-start | bytes 786440 | tf_op jit(solution)/shard_map/ppermute | solution.py:228
  41.3 6.5 %copy-start.4 = (f32[512]{0:T(512)S(1)}, f32[512]{0:T(512)}, u32[]{:S(2)}) copy-start(f32[512]{0:T(512)} %param.12) | copy-start | bytes 6148
  47.8 7.4 %copy-start.1 = (f32[12,132,512]{2,1,0:T(8,128)}, f32[12,132,512]{2,1,0:T(8,128)S(1)}, u32[]{:S(2)}) copy-start(f32[12,132,512]{2,1,0:T(8,128)S(1)} %fusion.68) | copy-start | bytes 9732100
  47.8 7.4 %copy-start.6 = (bf16[4,2,128,512]{3,2,1,0:T(8,128)(2,1)S(1)}, bf16[4,2,128,512]{3,2,1,0:T(8,128)(2,1)}, u32[]{:S(2)}) copy-start(bf16[4,2,128,512]{3,2,1,0:T(8,128)(2,1)} %get-tuple-element.8) | copy-start | bytes 3145732
  47.8 7.4 %copy-start.7 = (bf16[512,512]{1,0:T(8,128)(2,1)S(1)}, bf16[512,512]{1,0:T(8,128)(2,1)}, u32[]{:S(2)}) copy-start(bf16[512,512]{1,0:T(8,128)(2,1)} %param.13) | copy-start | bytes 1572868
  58.7 14.6 %collective-permute-start.2 = (bf16[2,128,512]{2,1,0:T(8,128)(2,1)S(1)}, bf16[2,128,512]{2,1,0:T(8,128)(2,1)S(1)}, u32[]{:S(2)}, u32[]{:S(2)}) collective-permute-start(bf16[2,128,512]{2,1,0:T(8,128)(2,1)S(1)} %get-tuple-element.44), channel_id=1, source_target_pairs={{0,4},{4,8},{8,12},{12,16},{16,20},{20,24},{24,28},{28,32},{32,36}... | collective-permute-start | bytes 786440 | tf_op jit(solution)/shard_map/ppermute | solution.py:225
  60.6 14.4 %copy-start.5 = (f32[512]{0:T(512)S(1)}, f32[512]{0:T(512)}, u32[]{:S(2)}) copy-start(f32[512]{0:T(512)} %param.10) | copy-start | bytes 6148
  60.6 13.9 %collective-permute-start.3 = (bf16[2,128,512]{2,1,0:T(8,128)(2,1)S(1)}, bf16[2,128,512]{2,1,0:T(8,128)(2,1)S(1)}, u32[]{:S(2)}, u32[]{:S(2)}) collective-permute-start(bf16[2,128,512]{2,1,0:T(8,128)(2,1)S(1)} %get-tuple-element.45), channel_id=1, source_target_pairs={{4,0},{8,4},{12,8},{16,12},{20,16},{24,20},{28,24},{32,28},{36,32}... | collective-permute-start | bytes 786440 | tf_op jit(solution)/shard_map/ppermute | solution.py:228
  196.2 6.0 %copy-start.2 = (bf16[2,128,512]{2,1,0:T(8,128)(2,1)S(1)}, bf16[2,128,512]{2,1,0:T(8,128)(2,1)}, u32[]{:S(2)}) copy-start(bf16[2,128,512]{2,1,0:T(8,128)(2,1)} %second.1) | copy-start | bytes 786436
Sparse Core Ops, SparseCore 0:
  84.5 41.9 reduce-scatter.1

commit v3 on v2

--- a/solution.py
+++ b/solution.py
@@ -1,3 +1,5 @@
+import functools
+
 import jax
 import jax.numpy as jnp
 from jax import lax
@@ -215,19 +217,53 @@
     return tuple(r.reshape((-1,) + first.shape[1:]) for r in result)
 
 
-def extended(block, sides, width):
-    for axis, dim in sides:
-        count = 1
-        for name in axis:
-            count *= lax.axis_size(name)
-        forward = [(i, i + 1) for i in range(count - 1)]
-        backward = [(target, source) for source, target in forward]
-        low = lax.ppermute(
-            lax.slice_in_dim(block, block.shape[dim] - width, None, axis=dim), axis, forward
-        )
-        high = lax.ppermute(lax.slice_in_dim(block, 0, width, axis=dim), axis, backward)
-        block = jnp.concatenate([low, block, high], axis=dim)
-    return block
+def _halo_kernel(width, block, low, high, sems):
+    coords = [lax.axis_index(a) for a in ALL_AXES]
+    ny, nz, nx = (lax.axis_size(a) for a in ROW_AXES)
+    count = ny * nz * nx
+    me = (coords[0] * nz + coords[1]) * nx + coords[2]
+
+    def dev(index):
+        index = lax.rem(index + count, count)
+        return (index // (nz * nx), lax.rem(index // nx, nz), lax.rem(index, nx), coords[3], coords[4])
+
+    up, down = dev(me + 1), dev(me - 1)
+    barrier = pltpu.get_barrier_semaphore()
+    for d in (up, down):
+        pl.semaphore_signal(barrier, inc=1, device_id=d, device_id_type=MESH_ID)
+    pl.semaphore_wait(barrier, 2)
+    rows = block.shape[0]
+    copies = [
+        pltpu.make_async_remote_copy(
+            src_ref=block.at[pl.ds(rows - width, width)], dst_ref=low, send_sem=sems.at[0, 0],
+            recv_sem=sems.at[1, 0], device_id=up, device_id_type=MESH_ID),
+        pltpu.make_async_remote_copy(
+            src_ref=block.at[pl.ds(0, width)], dst_ref=high, send_sem=sems.at[0, 1],
+            recv_sem=sems.at[1, 1], device_id=down, device_id_type=MESH_ID),
+    ]
+    for c in copies:
+        c.start()
+    for c in copies:
+        c.wait_recv()
+    for c in copies:
+        c.wait_send()
+
+
+def with_halo(block, width):
+    edge = jax.ShapeDtypeStruct((width,) + block.shape[1:], block.dtype)
+    low, high = pl.pallas_call(
+        functools.partial(_halo_kernel, width),
+        out_shape=(edge, edge),
+        in_specs=[pl.BlockSpec(memory_space=pl.ANY)],
+        out_specs=(pl.BlockSpec(memory_space=pltpu.VMEM),) * 2,
+        scratch_shapes=[pltpu.SemaphoreType.DMA((2, 2))],
+        compiler_params=pltpu.CompilerParams(collective_id=2, has_side_effects=True),
+    )(block)
+    ny, nz, nx = (lax.axis_size(a) for a in ROW_AXES)
+    me = (lax.axis_index("y_lo") * nz + lax.axis_index("z")) * nx + lax.axis_index("x")
+    low = jnp.where(me == 0, jnp.zeros_like(low), low)
+    high = jnp.where(me == ny * nz * nx - 1, jnp.zeros_like(high), high)
+    return jnp.concatenate([low, block, high], axis=0)
 
 
 def gelu_parts(pre):
@@ -268,7 +304,7 @@
     )
     hidden, slope_one = gelu_parts(pre_one)
     hidden = hidden.astype(jnp.bfloat16)
-    rimmed = extended(hidden, ((ROW_AXES, 0),), 2)
+    rimmed = with_halo(hidden, 2)
     padded = jnp.pad(rimmed, ((0, 0), (2, 2), (0, 0))).astype(jnp.float32)
     pre_two = jnp.zeros((nrows, ncols, hslice), jnp.float32) + depth_b
     for row_tap in range(5):
@@ -287,7 +323,7 @@
     grad_pre = (grad_mixed * slope_two).astype(jnp.bfloat16)
     grad_pre_f = grad_pre.astype(jnp.float32)
     grad_bd = jnp.sum(grad_pre_f, axis=(0, 1))
-    grad_rimmed = extended(grad_pre, ((ROW_AXES, 0),), 2)
+    grad_rimmed = with_halo(grad_pre, 2)
     grad_pad = jnp.pad(grad_rimmed, ((0, 0), (2, 2), (0, 0))).astype(jnp.float32)
     taps = []
     grad_hidden = jnp.zeros((nrows, ncols, hslice), jnp.float32)

time: 212 us -> 216 us (1.019)
  Pallas kernels: 96.7 us -> 126 us
  starting transfers between devices: 23.1 us -> 0.04 us
  waiting for transfers between devices: 11.1 us -> 0.02 us
  local copies, waits for them, and re-layouts: 16.7 us -> 19.9 us
  other arithmetic: 36.1 us -> 39 us
  matrix products: 12.8 us -> 15.1 us
    pallas_call x0 -> x2, Pallas kernels: none -> 30 us  [with_halo(): pl.pallas_call(functools.partial(_halo_kernel, width), out_shape=(edge, e...]
    ppermute x4 -> x0, starting transfers between devices: 23.1 us -> none  [the longest x2 17.7 us: extended(): lax.ppermute(lax.slice_in_dim(block, 0, width, axis=dim), axis, backward)]
    ppermute x4 -> x0, waiting for transfers between devices: 11.1 us -> none  [the longest x2 8.72 us: extended(): lax.ppermute(lax.slice_in_dim(block, block.shape[dim] - width, None, axis...]
    select_n x0 -> x3, other arithmetic: none -> 3.04 us  [the longest x2 2.06 us: with_halo(): high = jnp.where(me == ny * nz * nx - 1, jnp.zeros_like(high), high)]
  transfers between devices with their start and end apart: 5 -> 1, of which waited for: 4 -> 0; matrix products, arithmetic and copies ran while one was open for 19% -> 19% of each run, Pallas kernels for 37% -> 36%
where the time goes in v3:
time: 216 us; the launch traced here: 214 us
  Pallas kernels  126 us (58%)
  other arithmetic  39 us (18%)
  local copies, waits for them, and re-layouts  19.9 us (9%)
  matrix products  15.1 us (7%)
  between operations  14.2 us (7%)
    pallas_call x1, Pallas kernels, row_group_allreduce(): pl.pallas_call(body, out_shape=jax.ShapeDtypeStruct((rows, cols), jnp.flo...  76.5 us
    pallas_call x2, Pallas kernels, with_halo(): pl.pallas_call(functools.partial(_halo_kernel, width), out_shape=(edge, e...  30 us
    pallas_call x1, Pallas kernels, chan_gather(): pl.pallas_call(_chan_gather_kernel, out_shape=(jax.ShapeDtypeStruct(shape...  19.3 us
    reduce_sum x1, other arithmetic, shards(): jnp.sum(padded[row_tap:row_tap + nrows, col_tap:col_tap + ncols] * grad_p...  18.6 us
    convert_element_type x1, other arithmetic, shards(): mixed = mixed.astype(jnp.bfloat16).reshape(nrows * ncols, hslice)  7.31 us
    reduce_sum x1, other arithmetic, shards(): grad_b1 = jnp.sum(flat_act.astype(jnp.float32), axis=0)  7.19 us
    concatenate x1, local copies, waits for them, and re-layouts, row_group_sum(): flat = jnp.concatenate([t.reshape(-1, lanes) for t in terms], axis=0)  5.49 us
    reshape x3, local copies, waits for them, and re-layouts, row_group_sum(): out.append(flat[at:at + size].reshape(t.shape))  5.38 us
  transfers between devices with their start and end apart: 1, of which 0 were waited for; matrix products, arithmetic and copies ran while one was open for 19% of the time, Pallas kernels for 36%

profile of v3, /device:TPU:8, one launch (start us, length us, event | category | flops | bytes accessed | tf_op | source)
XLA Modules:
  0.0 214.1 jit_solution(1430040513751044514)
XLA Ops:
  7.2 0.9 fusion.77
  8.1 1.2 fusion.76
  9.4 19.3 %shard_map.118 = (bf16[4,2,128,512]{3,2,1,0:T(8,128)(2,1)}, bf16[4,2,128,512]{3,2,1,0:T(8,128)(2,1)}) custom-call(bf16[2,128,512]{2,1,0:T(8,128)(2,1)} %first.1, bf16[2,128,512]{2,1,0:T(8,128)(2,1)} %second.1), custom_call_target="tpu_custom_call" | custom-call | tf_op jit(solution)/shard_map/pallas_call | solution.py:209
  28.7 3.7 %multiply_convert_fusion.1 = (bf16[8,128,512]{2,1,0:T(8,128)(2,1)}, f32[8,128,512]{2,1,0:T(8,128)}) fusion(f32[512]{0:T(512)} %param.10, bf16[8,128,512]{2,1,0:T(8,128)(2,1)} %bitcast.160, bf16[512,512]{1,0:T(8,128)(2,1)S(1)} %copy-done), kind=kOutput, calls=%fused_computation.121 | convolution fusion | flops 540016640 | bytes 4720640 | tf_op jit(solution)/shard_map/dot_general | solution.py:300
  32.4 17.0 %shard_map.119 = (bf16[2,128,512]{2,1,0:T(8,128)(2,1)}, bf16[2,128,512]{2,1,0:T(8,128)(2,1)}) custom-call(bf16[8,128,512]{2,1,0:T(8,128)(2,1)} %get-tuple-element.77.block), custom_call_target="tpu_custom_call" | custom-call | tf_op jit(solution)/shard_map/pallas_call | solution.py:254
  49.4 1.1 broadcast_select_fusion.1
  50.5 0.5 fusion.68
  51.0 0.1 copy-done.6
  51.2 7.3 %multiply_convert_fusion = (bf16[8,128,512]{2,1,0:T(8,128)(2,1)}, f32[8,128,512]{2,1,0:T(8,128)S(1)}) fusion(f32[12,132,512]{2,1,0:T(8,128)S(1)} %fusion.68, f32[512]{0:T(512)S(1)} %bitcast.91, f32[512]{0:T(512)S(1)} %bitcast.93, f32[512]{0:T(512)S(1)} %bitcast.97, f32[512]{0:T(512)S(1)} %bitcast.99, f32[512]{0:T(512)S(1)} %bitcast.101, ...), kind=kLoop, calls=%fused_computation.117 | loop fusion | flops 28835840 | bytes 55627776 | tf_op jit(solution)/shard_map/convert_element_type | solution.py:318
  58.5 4.1 %fusion.36 = (f32[512]{0:T(512)S(1)}, f32[512]{0:T(512)S(1)}, f32[512]{0:T(512)S(1)}, f32[512]{0:T(512)S(1)}, f32[512]{0:T(512)S(1)}, /*index=5*/f32[512]{0:T(51...) fusion(f32[12,132,512]{2,1,0:T(8,128)S(1)} %fusion.68, f32[8,128,512]{2,1,0:T(8,128)S(1)} %get-tuple-element.45, ...), kind=kOutput, calls=%fused_computation.66 | convolution fusion | flops 550498304 | bytes 19415040 | tf_op jit(solution)/shard_map/dot_general | solution.py:320
  62.6 13.0 %shard_map.120 = (bf16[2,128,512]{2,1,0:T(8,128)(2,1)}, bf16[2,128,512]{2,1,0:T(8,128)(2,1)}) custom-call(bf16[8,128,512]{2,1,0:T(8,128)(2,1)} %get-tuple-element.79.block), custom_call_target="tpu_custom_call" | custom-call | tf_op jit(solution)/shard_map/pallas_call | solution.py:254
  75.7 1.0 broadcast_select_fusion.2
  76.6 1.0 broadcast_select_fusion
  77.7 0.5 fusion.62
  78.2 1.1 copy-done.4
  79.2 7.2 %convert_reduce_fusion.1 = (f32[512]{0:T(512)S(1)}, bf16[8,128,512]{2,1,0:T(8,128)(2,1)S(1)}) fusion(f32[8,128,512]{2,1,0:T(8,128)S(1)} %copy-done.4, f32[512]{0:T(512)S(1)} %copy-done.7, f32[12,132,512]{2,1,0:T(8,128)S(1)} %fusion.62, f32[512]{0:T(512)S(1)} %bitcast.92, f32[512]{0:T(512)S(1)} %bitcast.94, f32[512]{0:T(512)S(1)} %bitcast.98, ...), kind=kLoop, calls=%fused_computation.118 | loop fusion | flops 32505344 | bytes 55629824 | tf_op jit(solution)/shard_map/reduce_sum | solution.py:346
  86.4 2.1 fusion.69
  88.5 3.2 %fusion.79 = f32[512,512]{1,0:T(8,128)} fusion(bf16[1024,512]{1,0:T(8,128)(2,1)} %bitcast.82, bf16[1024,512]{1,0:T(8,128)(2,1)} %bitcast.162), kind=kOutput, calls=%fused_computation.148 | convolution fusion | flops 536870912 | bytes 3145728 | tf_op jit(solution)/shard_map/dot_general | solution.py:319
  91.8 2.3 %reshape.73 = f32[2048,128]{1,0:T(8,128)} reshape(f32[512,512]{1,0:T(8,128)} %fusion.79) | data formatting | bytes 2097152 | tf_op jit(solution)/shard_map/reshape | solution.py:277
  94.1 18.6 %fusion.37 = (f32[512]{0:T(512)S(1)}, f32[512]{0:T(512)S(1)}, f32[512]{0:T(512)S(1)}, f32[512]{0:T(512)S(1)}, f32[512]{0:T(512)S(1)}, /*index=5*/f32[512]{0:T(51...) fusion(bf16[8,128,512]{2,1,0:T(8,128)(2,1)S(1)} %copy-done.2, ...), kind=kLoop, calls=%fused_computation.67 | loop fusion | flops 19389440 | bytes 38834176 | tf_op jit(solution)/shard_map/reduce_sum | solution.py:333
  112.7 0.1 stack.103
  112.9 1.9 fusion.78
  114.8 1.0 reshape.70
  115.9 5.5 %concatenate.11 = f32[4204,128]{1,0:T(8,128)S(1)} concatenate(f32[2048,128]{1,0:T(8,128)} %reshape.70, f32[4,128]{1,0:T(4,128)S(1)} %bitcast.133, f32[100,128]{1,0:T(8,128)S(1)} %reshape.71, f32[4,128]{1,0:T(4,128)S(1)} %bitcast.152, f32[2048,128]{1,0:T(8,128)} %reshape.73), dimensions={0} | concatenate | bytes 4304896 | tf_op jit(solution)/shard_map/concatenate | solution.py:277
  121.4 0.2 pad.13.data
  121.5 76.5 %shard_map.121 = f32[4608,128]{1,0:T(8,128)S(1)} custom-call(f32[4608,128]{1,0:T(8,128)S(1)} %pad.13.data), custom_call_target="tpu_custom_call" | custom-call | tf_op jit(solution)/shard_map/pallas_call | solution.py:148
  198.0 1.5 fusion.75
  199.5 2.4 %reshape.76 = f32[512,512]{1,0:T(8,128)} reshape(f32[2048,128]{1,0:T(8,128)} %get-tuple-element.48) | data formatting | bytes 2097152 | tf_op jit(solution)/shard_map/reshape | solution.py:288
  201.9 0.6 reshape.75
  202.5 2.4 %reshape.74 = f32[512,512]{1,0:T(8,128)} reshape(f32[2048,128]{1,0:T(8,128)} %get-tuple-element.49) | data formatting | bytes 2097152 | tf_op jit(solution)/shard_map/reshape | solution.py:288
  204.9 0.6 slice_bitcast_fusion
  205.4 1.8 add_convert_fusion
  (23 shorter events, 0.1 us)
Async XLA Ops:
  7.2 21.5 %copy-start = (bf16[512,512]{1,0:T(8,128)(2,1)S(1)}, bf16[512,512]{1,0:T(8,128)(2,1)}, u32[]{:S(2)}) copy-start(bf16[512,512]{1,0:T(8,128)(2,1)} %param.9) | copy-start | bytes 1572868
  7.2 198.3 %reduce-scatter.2.cloned.1.call-start = ((), (), s32[]{:S(2)}) async-start(), calls=%async_computation.1 | async-start | bytes 2621440 | tf_op jit(solution)/shard_map/reduce_scatter | solution.py:351
  32.4 18.1 %copy-start.3 = (bf16[8,128,512]{2,1,0:T(8,128)(2,1)S(1)}, bf16[8,128,512]{2,1,0:T(8,128)(2,1)}, u32[]{:S(2)}) copy-start(bf16[8,128,512]{2,1,0:T(8,128)(2,1)} %get-tuple-element.77.block) | copy-start | bytes 3145732
  50.5 0.7 copy-start.6
  51.0 7.5 %copy-start.1 = (f32[12,132,512]{2,1,0:T(8,128)}, f32[12,132,512]{2,1,0:T(8,128)S(1)}, u32[]{:S(2)}) copy-start(f32[12,132,512]{2,1,0:T(8,128)S(1)} %fusion.68) | copy-start | bytes 9732100
  51.2 7.3 %copy-start.8 = (bf16[4,2,128,512]{3,2,1,0:T(8,128)(2,1)S(1)}, bf16[4,2,128,512]{3,2,1,0:T(8,128)(2,1)}, u32[]{:S(2)}) copy-start(bf16[4,2,128,512]{3,2,1,0:T(8,128)(2,1)} %get-tuple-element.12) | copy-start | bytes 3145732
  51.2 7.3 %copy-start.9 = (bf16[512,512]{1,0:T(8,128)(2,1)S(1)}, bf16[512,512]{1,0:T(8,128)(2,1)}, u32[]{:S(2)}) copy-start(bf16[512,512]{1,0:T(8,128)(2,1)} %param.13) | copy-start | bytes 1572868
  62.6 15.0 %copy-start.2 = (bf16[8,128,512]{2,1,0:T(8,128)(2,1)S(1)}, bf16[8,128,512]{2,1,0:T(8,128)(2,1)}, u32[]{:S(2)}) copy-start(bf16[8,128,512]{2,1,0:T(8,128)(2,1)} %get-tuple-element.79.block) | copy-start | bytes 3145732
  77.6 1.6 copy-start.4
  77.6 1.6 copy-start.7
  199.5 6.0 %copy-start.5 = (bf16[2,128,512]{2,1,0:T(8,128)(2,1)S(1)}, bf16[2,128,512]{2,1,0:T(8,128)(2,1)}, u32[]{:S(2)}) copy-start(bf16[2,128,512]{2,1,0:T(8,128)(2,1)} %second.1) | copy-start | bytes 786436
Sparse Core Ops, SparseCore 0:
  88.7 40.7 reduce-scatter.1

commit v4 on v2

--- a/solution.py
+++ b/solution.py
@@ -11,10 +11,18 @@
 CHAN_AXES = ("y_hi", "core")
 
 
-def _sum_kernel(nx, nz, data, out, xs, zs, ys, sems):
-    (xsend, xrecv, zsend, zrecv, ysend, yrecv, gzsend, gzrecv, gxsend, gxrecv) = sems
+def _sum_kernel(nx, nz, layout, terms, part, cot, term_outs, grad_out, data, out, xs, zs, ys, from_pair, from_far,
+                relay, sems):
+    (xsend, xrecv, zsend, zrecv, ysend, yrecv, gzsend, gzrecv, gxsend, gxrecv, csems) = sems
     coords = [lax.axis_index(a) for a in ALL_AXES]
     iy, iz, ix = coords[0], coords[1], coords[2]
+    hi, core = coords[3], coords[4]
+    me = hi * 2 + core
+    pair_at = hi * 2 + (1 - core)
+    far_at = (1 - hi) * 2 + core
+    diag_at = (1 - hi) * 2 + (1 - core)
+    pair = (iy, iz, ix, hi, 1 - core)
+    far = (iy, iz, ix, 1 - hi, core)
 
     def dev(y=None, z=None, x=None):
         c = list(coords)
@@ -32,12 +40,26 @@
 
     barrier = pltpu.get_barrier_semaphore()
     z_peer = [None] + [dev(z=lax.rem(iz + d, nz)) for d in range(1, nz)]
-    peers = [x_next[0], x_next[1], partner] + z_peer[1:]
+    peers = [x_next[0], x_next[1], partner, pair, far] + z_peer[1:]
     if nx == 2:
         peers = peers[1:]
     for d in peers:
         pl.semaphore_signal(barrier, inc=1, device_id=d, device_id_type=MESH_ID)
     pl.semaphore_wait(barrier, len(peers))
+
+    filled = 0
+    for ref, (at, size) in zip(terms, layout):
+        data[at : at + size] = ref[...]
+        filled = at + size
+    data[filled:] = jnp.zeros((data.shape[0] - filled, data.shape[1]), data.dtype)
+
+    chan_one = []
+    for j, src in enumerate((part.at[pair_at], part.at[diag_at])):
+        c = pltpu.make_async_remote_copy(
+            src_ref=src, dst_ref=from_pair.at[j], send_sem=csems.at[0, j],
+            recv_sem=csems.at[1, j], device_id=pair, device_id_type=MESH_ID)
+        c.start()
+        chan_one.append(c)
 
     rows = data.shape[0]
     half = rows // 2
@@ -74,6 +96,13 @@
             xs[h, s] = xs[h, s] + data[xblock(h, ix - sg * (s + 2))]
             copies[h].wait_send()
     last = nx - 2
+    for c in chan_one:
+        c.wait_recv()
+    relay[...] = part[far_at] + from_pair[1]
+    chan_two = pltpu.make_async_remote_copy(
+        src_ref=relay, dst_ref=from_far, send_sem=csems.at[0, 2],
+        recv_sem=csems.at[1, 2], device_id=far, device_id_type=MESH_ID)
+    chan_two.start()
     copies = []
     for h in range(2):
         for d in range(1, nz):
@@ -128,9 +157,24 @@
             copies[h].wait_recv()
             copies[h].wait_send()
 
-
-def row_group_allreduce(flat, nx, nz):
-    rows, cols = flat.shape
+    for ref, (at, size) in zip(term_outs, layout):
+        ref[...] = out[at : at + size]
+    chan_two.wait_recv()
+    total = part[me] + from_pair[0] + from_far[...]
+    grad_out[...] = (cot[...].astype(jnp.float32) + total).astype(grad_out.dtype)
+    for c in chan_one:
+        c.wait_send()
+    chan_two.wait_send()
+
+def row_group_allreduce(terms, nx, nz, part, cot):
+    cols = terms[0].shape[-1]
+    layout = []
+    at = 0
+    for t in terms:
+        layout.append((at, t.shape[0]))
+        at += t.shape[0]
+    quantum = 2 * nx * nz * 8
+    rows = -(-at // quantum) * quantum
     half = rows // 2
     bx = half // nx
     bz = bx // nz
@@ -138,24 +182,35 @@
             pltpu.SemaphoreType.DMA((2 * nz,)), pltpu.SemaphoreType.DMA((2 * nz,)),
             pltpu.SemaphoreType.DMA((1,)), pltpu.SemaphoreType.DMA((1,)),
             pltpu.SemaphoreType.DMA((2 * nz,)), pltpu.SemaphoreType.DMA((2 * nz,)),
-            pltpu.SemaphoreType.DMA((2 * nx,)), pltpu.SemaphoreType.DMA((2 * nx,))]
-
-    def body(data, out, xs, zs, ys, *s):
-        _sum_kernel(nx, nz, data, out, xs, zs, ys, s)
+            pltpu.SemaphoreType.DMA((2 * nx,)), pltpu.SemaphoreType.DMA((2 * nx,)),
+            pltpu.SemaphoreType.DMA((2, 3))]
+    block = part.shape[1:]
+    count = len(terms)
+
+    def body(*refs):
+        ins, outs, scratch = refs[: count + 2], refs[count + 2 : 2 * count + 3], refs[2 * count + 3 :]
+        _sum_kernel(nx, nz, layout, ins[:count], ins[count], ins[count + 1], outs[:count], outs[count],
+                    *scratch[:8], scratch[8:])
 
     return pl.pallas_call(
         body,
-        out_shape=jax.ShapeDtypeStruct((rows, cols), jnp.float32),
-        in_specs=[pl.BlockSpec(memory_space=pltpu.VMEM)],
-        out_specs=pl.BlockSpec(memory_space=pltpu.VMEM),
+        out_shape=tuple(jax.ShapeDtypeStruct(t.shape, jnp.float32) for t in terms)
+        + (jax.ShapeDtypeStruct(cot.shape, cot.dtype),),
+        in_specs=[pl.BlockSpec(memory_space=pltpu.VMEM)] * (count + 2),
+        out_specs=(pl.BlockSpec(memory_space=pltpu.VMEM),) * (count + 1),
         scratch_shapes=[
+            pltpu.VMEM((rows, cols), jnp.float32),
+            pltpu.VMEM((rows, cols), jnp.float32),
             pltpu.VMEM((2, nx - 1, bx, cols), jnp.float32),
             pltpu.VMEM((2, nz, bz, cols), jnp.float32),
             pltpu.VMEM((2, bz, cols), jnp.float32),
+            pltpu.VMEM((2,) + block, jnp.float32),
+            pltpu.VMEM(block, jnp.float32),
+            pltpu.VMEM(block, jnp.float32),
         ] + sems,
         compiler_params=pltpu.CompilerParams(collective_id=0, has_side_effects=True,
                                              vmem_limit_bytes=48 * 1024 * 1024),
-    )(flat)
+    )(*terms, part, cot)
 
 
 def _chan_gather_kernel(first, second, out_first, out_second, sems):
@@ -234,24 +289,6 @@
     cdf = 0.5 * (1.0 + lax.erf(pre * 0.7071067811865476))
     dens = jnp.exp(-0.5 * pre * pre) * 0.3989422804014327
     return (pre * cdf, cdf + pre * dens)
-
-
-def row_group_sum(terms):
-    lanes = 128
-    flat = jnp.concatenate([t.reshape(-1, lanes) for t in terms], axis=0)
-    rows = flat.shape[0]
-    nx, nz = lax.axis_size("x"), lax.axis_size("z")
-    quantum = 16 * nx * nz
-    padded_rows = -(-rows // quantum) * quantum
-    flat = jnp.pad(flat, ((0, padded_rows - rows), (0, 0)))
-    flat = row_group_allreduce(flat, nx, nz)
-    out = []
-    at = 0
-    for t in terms:
-        size = t.size // lanes
-        out.append(flat[at : at + size].reshape(t.shape))
-        at += size
-    return out
 
 
 def shards(inputs, cotangent, expand_w, expand_b, depth_k, depth_b, project_w):
@@ -309,17 +346,13 @@
     flat_act = grad_act.reshape(nrows * ncols, hslice)
     grad_b1 = jnp.sum(flat_act.astype(jnp.float32), axis=0)
     grad_w1 = jnp.dot(flat_inputs.T, flat_act, preferred_element_type=jnp.float32)
-    summed = row_group_sum([grad_w1, grad_b1[None], grad_k, grad_bd[None], grad_w2])
-    summed[1] = summed[1][0]
-    summed[3] = summed[3][0]
-    own_part = lax.psum_scatter(
-        jnp.einsum("rwh,ch->rwc", grad_act, expand_w, preferred_element_type=jnp.float32),
-        CHAN_AXES,
-        scatter_dimension=0,
-        tiled=True,
-    )
-    input_grad = (cotangent.astype(jnp.float32) + own_part).astype(jnp.bfloat16)
-    return (input_grad, summed[0], summed[1], summed[2], summed[3], summed[4])
+    part = jnp.einsum("rwh,ch->rwc", grad_act, expand_w, preferred_element_type=jnp.float32)
+    part = part.reshape((4, -1) + part.shape[1:])
+    nx, nz = lax.axis_size("x"), lax.axis_size("z")
+    w1, w2, k, b1, bd, input_grad = row_group_allreduce(
+        [grad_w1, grad_w2, grad_k, grad_b1[None], grad_bd[None]], nx, nz, part, cotangent
+    )
+    return (input_grad, w1, b1[0], k, bd[0], w2)
 
 
 def solution(mesh):

time: 212 us -> 192 us (0.906)
  Pallas kernels: 96.7 us -> 119 us
  other arithmetic: 36.1 us -> 20.3 us
  between operations: 14.3 us -> 1.03 us
  local copies, waits for them, and re-layouts: 16.7 us -> 9.27 us
  waiting for transfers between devices: 11.1 us -> 6.16 us
    pallas_call x1, Pallas kernels: 77.3 us -> 100 us  [row_group_allreduce(): pl.pallas_call(body, out_shape=tuple((jax.ShapeDtypeStruct(t.shape, jnp.f...]
    reduce_sum x1, other arithmetic: 18.6 us -> 5.3 us  [shards(): jnp.sum(padded[row_tap:row_tap + nrows, col_tap:col_tap + ncols] * grad_p...]
    reshape x6 -> x0, local copies, waits for them, and re-layouts: 8.72 us -> none  [the longest x3 5.38 us: row_group_sum(): out.append(flat[at:at + size].reshape(t.shape))]
    concatenate x1 -> x0, local copies, waits for them, and re-layouts: 5.53 us -> none  [row_group_sum(): flat = jnp.concatenate([t.reshape(-1, lanes) for t in terms], axis=0)]
    unnamed x16 -> x48, local copies, waits for them, and re-layouts: 0.05 us -> 5.49 us
    ppermute x2, waiting for transfers between devices: 8.72 us -> 4.75 us  [extended(): lax.ppermute(lax.slice_in_dim(block, block.shape[dim] - width, None, axis...]
    another operation x1, local copies, waits for them, and re-layouts: 0.13 us -> 2.96 us  [shards(): grad_k = jnp.stack(taps, axis=0)]
  transfers between devices with their start and end apart: 5 -> 4, of which waited for: 4 -> 3; matrix products, arithmetic and copies ran while one was open for 19% -> 3% of each run, Pallas kernels for 37% -> 0%
where the time goes in v4:
time: 192 us; the launch traced here: 191 us
  Pallas kernels  119 us (62%)
  starting transfers between devices  22.9 us (12%)
  other arithmetic  20.3 us (11%)
  matrix products  12.2 us (6%)
  local copies, waits for them, and re-layouts  9.27 us (5%)
  waiting for transfers between devices  6.16 us (3%)
    pallas_call x1, Pallas kernels, row_group_allreduce(): pl.pallas_call(body, out_shape=tuple((jax.ShapeDtypeStruct(t.shape, jnp.f...  100 us
    pallas_call x1, Pallas kernels, chan_gather(): pl.pallas_call(_chan_gather_kernel, out_shape=(jax.ShapeDtypeStruct(shape...  19.3 us
    ppermute x2, starting transfers between devices, extended(): lax.ppermute(lax.slice_in_dim(block, 0, width, axis=dim), axis, backward)  17.6 us
    reduce_sum x1, other arithmetic, shards(): grad_b1 = jnp.sum(flat_act.astype(jnp.float32), axis=0)  7.26 us
    convert_element_type x1, other arithmetic, shards(): mixed = mixed.astype(jnp.bfloat16).reshape(nrows * ncols, hslice)  6.69 us
    unnamed x48, local copies, waits for them, and re-layouts  5.49 us
    ppermute x2, starting transfers between devices, extended(): lax.ppermute(lax.slice_in_dim(block, block.shape[dim] - width, None, axis...  5.33 us
    reduce_sum x1, other arithmetic, shards(): jnp.sum(padded[row_tap:row_tap + nrows, col_tap:col_tap + ncols] * grad_p...  5.3 us
  transfers between devices with their start and end apart: 4, of which 3 were waited for; matrix products, arithmetic and copies ran while one was open for 3% of the time, Pallas kernels for 0%

profile of v4, /device:TPU:8, one launch (start us, length us, event | category | flops | bytes accessed | tf_op | source)
XLA Modules:
  0.0 191.2 jit_solution(2454072799248268379)
XLA Ops:
  0.6 0.0 copy-start
  0.6 19.3 %shard_map.118 = (bf16[4,2,128,512]{3,2,1,0:T(8,128)(2,1)}, bf16[4,2,128,512]{3,2,1,0:T(8,128)(2,1)}) custom-call(bf16[2,128,512]{2,1,0:T(8,128)(2,1)} %first.1, bf16[2,128,512]{2,1,0:T(8,128)(2,1)} %refs_6_.1), custom_call_target="tpu_custom_call" | custom-call | tf_op jit(solution)/shard_map/pallas_call | solution.py:262
  20.0 3.4 %multiply_convert_fusion.1 = (bf16[8,128,512]{2,1,0:T(8,128)(2,1)S(1)}, f32[8,128,512]{2,1,0:T(8,128)}) fusion(f32[512]{0:T(512)} %param.10, bf16[8,128,512]{2,1,0:T(8,128)(2,1)} %bitcast.162, bf16[512,512]{1,0:T(8,128)(2,1)S(1)} %copy-done), kind=kOutput, calls=%fused_computation.121 | convolution fusion | flops 540016640 | bytes 4720640 | tf_op jit(solution)/shard_map/dot_general | solution.py:301
  23.4 3.4 %collective-permute-start = (bf16[2,128,512]{2,1,0:T(8,128)(2,1)S(1)}, bf16[2,128,512]{2,1,0:T(8,128)(2,1)S(1)}, u32[]{:S(2)}, u32[]{:S(2)}) collective-permute-start(bf16[2,128,512]{2,1,0:T(8,128)(2,1)S(1)} %get-tuple-element.54), channel_id=1, source_target_pairs={{0,4},{4,8},{8,12},{12,16},{16,20},{20,24},{24,28},{28,32},{32,36}... | collective-permute-start | bytes 786440 | tf_op jit(solution)/shard_map/ppermute | solution.py:280
  26.9 9.0 %collective-permute-start.1 = (bf16[2,128,512]{2,1,0:T(8,128)(2,1)S(1)}, bf16[2,128,512]{2,1,0:T(8,128)(2,1)S(1)}, u32[]{:S(2)}, u32[]{:S(2)}) collective-permute-start(bf16[2,128,512]{2,1,0:T(8,128)(2,1)S(1)} %get-tuple-element.55), channel_id=1, source_target_pairs={{4,0},{8,4},{12,8},{16,12},{20,16},{24,20},{28,24},{32,28},{36,32}... | collective-permute-start | bytes 786440 | tf_op jit(solution)/shard_map/ppermute | solution.py:283
  36.0 0.0 copy-start.16
  36.0 4.7 %collective-permute-done = bf16[2,128,512]{2,1,0:T(8,128)(2,1)S(1)} collective-permute-done((bf16[2,128,512]{2,1,0:T(8,128)(2,1)S(1)}, bf16[2,128,512]{2,1,0:T(8,128)(2,1)S(1)}, u32[]{:S(2)}, u32[]{:S(2)}) %collective-permute-start) | collective-permute-done | bytes 262176 | tf_op jit(solution)/shard_map/ppermute | solution.py:280
  40.7 1.2 collective-permute-done.1
  41.9 0.5 fusion.68
  42.5 0.0 copy-start.20
  42.5 6.7 %multiply_convert_fusion = (bf16[8,128,512]{2,1,0:T(8,128)(2,1)S(1)}, f32[8,128,512]{2,1,0:T(8,128)S(1)}) fusion(f32[12,132,512]{2,1,0:T(8,128)S(1)} %fusion.68, f32[512]{0:T(512)S(1)} %bitcast.95, f32[512]{0:T(512)S(1)} %bitcast.97, f32[512]{0:T(512)S(1)} %bitcast.101, f32[512]{0:T(512)S(1)} %bitcast.103, f32[512]{0:T(512)S(1)} %bitcast.105, ...), kind=kLoop, calls=%fused_computation.118 | loop fusion | flops 28835840 | bytes 55627776 | tf_op jit(solution)/shard_map/convert_element_type | solution.py:319
  49.3 4.0 %fusion.36 = (f32[512]{0:T(512)}, f32[512]{0:T(512)}, f32[512]{0:T(512)}, f32[512]{0:T(512)}, f32[512]{0:T(512)}, /*index=5*/f32[512]{0:T(512)}, f32[512]{0:T(512)}, f32[512]{0:T(512)S(1)}, bf16[8,128,512]{2,1,0:T(8,128)(2,1)S(1)}) fusion(f32[12,132,512]{2,1,0:T(8,128)S(1)} %fusion.68, f32[8,128,512]{2,1,0:T(8,128)S(1)} %get-tuple-element.51, ...), kind=kOutput, calls=%fused_computation.66 | convolution fusion | flops 550498304 | bytes 19415040 | tf_op jit(solution)/shard_map/dot_general | solution.py:321
  53.3 5.3 %fusion.37 = (f32[512]{0:T(512)}, f32[512]{0:T(512)}, f32[512]{0:T(512)}, f32[512]{0:T(512)}, f32[512]{0:T(512)}, /*index=5*/f32[512]{0:T(512)}, f32[512]{0:T(51...) fusion(bf16[8,128,512]{2,1,0:T(8,128)(2,1)S(1)} %get-tuple-elem, ...), kind=kLoop, calls=%fused_computation.67 | loop fusion | flops 19389440 | bytes 38834176 | tf_op jit(solution)/shard_map/reduce_sum | solution.py:334
  58.6 0.7 fusion.75
  59.3 1.9 collective-permute-start.2
  61.2 8.6 %collective-permute-start.3 = (bf16[2,128,512]{2,1,0:T(8,128)(2,1)S(1)}, bf16[2,128,512]{2,1,0:T(8,128)(2,1)S(1)}, u32[]{:S(2)}, u32[]{:S(2)}) collective-permute-start(bf16[2,128,512]{2,1,0:T(8,128)(2,1)S(1)} %get-tuple-element.53), channel_id=1, source_target_pairs={{4,0},{8,4},{12,8},{16,12},{20,16},{24,20},{28,24},{32,28},{36,32}... | collective-permute-start | bytes 786440 | tf_op jit(solution)/shard_map/ppermute | solution.py:283
  69.9 3.0 %stack.103.refs_2_ = f32[25,512]{1,0:T(8,128)S(1)} concatenate(f32[1,512]{1,0:T(1,128)} %bitcast.161, f32[1,512]{1,0:T(1,128)} %bitcast.138, f32[1,512]{1,0:T(1,128)} %bitcast.139, f32[1,512]{1,0:T(1,128)} %bitcast.140, f32[1,512]{1,0:T(1,128)} %bitcast.141, f32[1,512]{1,0:T(1,128)} %bitcast.142, f32[1,512]{1,0:T(1,128)} %bitcast.143, f32[1,512]{1,0:T(1,128)} %bitcast.144, ...), dimensions={0} | concatenate | bytes 102400 | tf_op jit(solution)/shard_map/stack | solution.py:344
  72.8 2.0 %fusion.80.refs_1_ = f32[512,512]{1,0:T(8,128)S(1)} fusion(bf16[1024,512]{1,0:T(8,128)(2,1)S(1)} %bitcast.86, bf16[1024,512]{1,0:T(8,128)(2,1)} %bitcast.164), kind=kOutput, calls=%fused_computation.142 | convolution fusion | flops 536870912 | bytes 3145728 | tf_op jit(solution)/shard_map/dot_general | solution.py:320
  74.9 0.2 collective-permute-done.3
  75.1 0.5 fusion.62
  75.6 0.7 copy-done.2
  76.4 7.3 %convert_reduce_fusion.1 = (f32[512]{0:T(512)S(1)}, bf16[8,128,512]{2,1,0:T(8,128)(2,1)S(1)}) fusion(f32[8,128,512]{2,1,0:T(8,128)S(1)} %copy-done.2, f32[512]{0:T(512)S(1)} %copy-done.17, f32[12,132,512]{2,1,0:T(8,128)S(1)} %fusion.62, f32[512]{0:T(512)S(1)} %bitcast.96, f32[512]{0:T(512)S(1)} %bitcast.98, f32[512]{0:T(512)S(1)} %bitcast.102, ...), kind=kLoop, calls=%fused_computation.117 | loop fusion | flops 32505344 | bytes 55629824 | tf_op jit(solution)/shard_map/reduce_sum | solution.py:347
  83.7 2.1 %fusion.69 = f32[8,128,512]{2,1,0:T(8,128)} fusion(bf16[8,128,512]{2,1,0:T(8,128)(2,1)S(1)} %get-tuple-element.49, bf16[512,512]{1,0:T(8,128)(2,1)S(1)} %copy-done), kind=kOutput, calls=%fused_computation.132 | convolution fusion | flops 536870912 | bytes 3670016 | tf_op jit(solution)/shard_map/rwh,ch->rwc/dot_general | solution.py:349
  85.8 0.7 fusion.79.refs_0_
  86.5 0.2 copy-done.1
  86.8 100.0 %shard_map.119 = (f32[512,512]{1,0:T(8,128)S(1)}, f32[512,512]{1,0:T(8,128)S(1)}, f32[25,512]{1,0:T(8,128)S(1)}, f32[1,512]{1,0:T(1,128)S(1)}, f32[1,512]{1,0:T(1,128)S(1)}, /*index=5*/bf16[2,128,512]{2,1,0:T(8,128)(2,1)S(1)}) custom-call(f32[512,512]{1,0:T(8,128)S(1)} %fusion.79.refs_0_, f32[512,512]{1,0:T(8,128)S(1)} %fusion.80.refs_1_, ...), custom_call_target="tpu_custom_call" | custom-call | tf_op jit(solution)/shard_map/pallas_call | solution.py:195
  186.8 0.7 copy.19
  187.5 1.0 copy.20
  188.4 0.6 copy.21
  189.0 0.6 copy.22
  189.6 0.6 copy.23
  190.2 1.0 copy.24
  (41 shorter events, 0.2 us)
Async XLA Ops:
  0.6 19.3 %copy-start = (bf16[512,512]{1,0:T(8,128)(2,1)S(1)}, bf16[512,512]{1,0:T(8,128)(2,1)}, u32[]{:S(2)}) copy-start(bf16[512,512]{1,0:T(8,128)(2,1)} %param.9) | copy-start | bytes 1572868
  20.0 15.9 %copy-start.3 = (f32[25,512]{1,0:T(8,128)S(1)}, f32[25,512]{1,0:T(8,128)}, u32[]{:S(2)}) copy-start(f32[25,512]{1,0:T(8,128)} %param.11) | copy-start | bytes 153604
  23.4 17.3 %collective-permute-start = (bf16[2,128,512]{2,1,0:T(8,128)(2,1)S(1)}, bf16[2,128,512]{2,1,0:T(8,128)(2,1)S(1)}, u32[]{:S(2)}, u32[]{:S(2)}) collective-permute-start(bf16[2,128,512]{2,1,0:T(8,128)(2,1)S(1)} %get-tuple-element.54), channel_id=1, source_target_pairs={{0,4},{4,8},{8,12},{12,16},{16,20},{20,24},{24,28},{28,32},{32,36}... | collective-permute-start | bytes 786440 | tf_op jit(solution)/shard_map/ppermute | solution.py:280
  26.9 15.1 %collective-permute-start.1 = (bf16[2,128,512]{2,1,0:T(8,128)(2,1)S(1)}, bf16[2,128,512]{2,1,0:T(8,128)(2,1)S(1)}, u32[]{:S(2)}, u32[]{:S(2)}) collective-permute-start(bf16[2,128,512]{2,1,0:T(8,128)(2,1)S(1)} %get-tuple-element.55), channel_id=1, source_target_pairs={{4,0},{8,4},{12,8},{16,12},{20,16},{24,20},{28,24},{32,28},{36,32}... | collective-permute-start | bytes 786440 | tf_op jit(solution)/shard_map/ppermute | solution.py:283
  35.9 6.5 %copy-start.4 = (f32[1,512]{1,0:T(1,128)}, f32[1,512]{1,0:T(1,128)S(1)}, u32[]{:S(2)}) copy-start(f32[1,512]{1,0:T(1,128)S(1)} %get-tuple-element.69) | copy-start | bytes 6148
  35.9 6.5 %copy-start.6 = (f32[1,512]{1,0:T(1,128)}, f32[1,512]{1,0:T(1,128)S(1)}, u32[]{:S(2)}) copy-start(f32[1,512]{1,0:T(1,128)S(1)} %get-tuple-element.70) | copy-start | bytes 6148
  35.9 6.5 %copy-start.8 = (f32[1,512]{1,0:T(1,128)}, f32[1,512]{1,0:T(1,128)S(1)}, u32[]{:S(2)}) copy-start(f32[1,512]{1,0:T(1,128)S(1)} %get-tuple-element.71) | copy-start | bytes 6148
  36.0 6.5 %copy-start.10 = (f32[1,512]{1,0:T(1,128)}, f32[1,512]{1,0:T(1,128)S(1)}, u32[]{:S(2)}) copy-start(f32[1,512]{1,0:T(1,128)S(1)} %get-tuple-element.72) | copy-start | bytes 6148
  36.0 6.5 %copy-start.12 = (f32[1,512]{1,0:T(1,128)}, f32[1,512]{1,0:T(1,128)S(1)}, u32[]{:S(2)}) copy-start(f32[1,512]{1,0:T(1,128)S(1)} %get-tuple-element.73) | copy-start | bytes 6148
  36.0 6.5 %copy-start.14 = (f32[1,512]{1,0:T(1,128)}, f32[1,512]{1,0:T(1,128)S(1)}, u32[]{:S(2)}) copy-start(f32[1,512]{1,0:T(1,128)S(1)} %get-tuple-element.74) | copy-start | bytes 6148
  36.0 6.5 %copy-start.16 = (f32[512]{0:T(512)S(1)}, f32[512]{0:T(512)}, u32[]{:S(2)}) copy-start(f32[512]{0:T(512)} %param.12) | copy-start | bytes 6148
  42.5 6.7 %copy-start.19 = (bf16[4,2,128,512]{3,2,1,0:T(8,128)(2,1)S(1)}, bf16[4,2,128,512]{3,2,1,0:T(8,128)(2,1)}, u32[]{:S(2)}) copy-start(bf16[4,2,128,512]{3,2,1,0:T(8,128)(2,1)} %get-tuple-element.15) | copy-start | bytes 3145732
  42.5 6.7 %copy-start.20 = (bf16[512,512]{1,0:T(8,128)(2,1)S(1)}, bf16[512,512]{1,0:T(8,128)(2,1)}, u32[]{:S(2)}) copy-start(bf16[512,512]{1,0:T(8,128)(2,1)} %param.13) | copy-start | bytes 1572868
  59.3 15.6 %collective-permute-start.2 = (bf16[2,128,512]{2,1,0:T(8,128)(2,1)}, bf16[2,128,512]{2,1,0:T(8,128)(2,1)S(1)}, u32[]{:S(2)}, u32[]{:S(2)}) collective-permute-start(bf16[2,128,512]{2,1,0:T(8,128)(2,1)} %get-tuple-element.52), channel_id=1, source_target_pairs={{0,4},{4,8},{8,12},{12,16},{16,20},{20,24},{24,28},{28,32},{32,36}... | collective-permute-start | bytes 786440 | tf_op jit(solution)/shard_map/ppermute | solution.py:280
  61.2 13.9 %collective-permute-start.3 = (bf16[2,128,512]{2,1,0:T(8,128)(2,1)S(1)}, bf16[2,128,512]{2,1,0:T(8,128)(2,1)S(1)}, u32[]{:S(2)}, u32[]{:S(2)}) collective-permute-start(bf16[2,128,512]{2,1,0:T(8,128)(2,1)S(1)} %get-tuple-element.53), channel_id=1, source_target_pairs={{4,0},{8,4},{12,8},{16,12},{20,16},{24,20},{28,24},{32,28},{36,32}... | collective-permute-start | bytes 786440 | tf_op jit(solution)/shard_map/ppermute | solution.py:283
  74.8 1.6 copy-start.2
  74.8 1.6 copy-start.5
  74.8 1.6 copy-start.7
  74.8 1.6 copy-start.9
  74.8 1.6 copy-start.11
  74.8 1.6 copy-start.13
  74.8 1.6 copy-start.15
  74.9 1.6 copy-start.17
  83.7 2.1 %copy-start.18 = (bf16[4,2,128,512]{3,2,1,0:T(8,128)(2,1)S(1)}, bf16[4,2,128,512]{3,2,1,0:T(8,128)(2,1)}, u32[]{:S(2)}) copy-start(bf16[4,2,128,512]{3,2,1,0:T(8,128)(2,1)} %get-tuple-element.14) | copy-start | bytes 3145732
  85.8 1.0 copy-start.1

commit v5 on v4

--- a/solution.py
+++ b/solution.py
@@ -11,9 +11,8 @@
 CHAN_AXES = ("y_hi", "core")
 
 
-def _sum_kernel(nx, nz, layout, terms, part, cot, term_outs, grad_out, data, out, xs, zs, ys, from_pair, from_far,
-                relay, sems):
-    (xsend, xrecv, zsend, zrecv, ysend, yrecv, gzsend, gzrecv, gxsend, gxrecv, csems) = sems
+def _sum_kernel(nx, nz, data, part, cot, out, grad_out, xs, zs, ys, fin, from_pair, from_far, relay, sems):
+    (xsend, xrecv, zsend, zrecv, ysend, yrecv, gzsend, gzrecv, gxsend, gxrecv, csems, local) = sems
     coords = [lax.axis_index(a) for a in ALL_AXES]
     iy, iz, ix = coords[0], coords[1], coords[2]
     hi, core = coords[3], coords[4]
@@ -47,12 +46,6 @@
         pl.semaphore_signal(barrier, inc=1, device_id=d, device_id_type=MESH_ID)
     pl.semaphore_wait(barrier, len(peers))
 
-    filled = 0
-    for ref, (at, size) in zip(terms, layout):
-        data[at : at + size] = ref[...]
-        filled = at + size
-    data[filled:] = jnp.zeros((data.shape[0] - filled, data.shape[1]), data.dtype)
-
     chan_one = []
     for j, src in enumerate((part.at[pair_at], part.at[diag_at])):
         c = pltpu.make_async_remote_copy(
@@ -61,24 +54,27 @@
         c.start()
         chan_one.append(c)
 
-    rows = data.shape[0]
-    half = rows // 2
-    bx = half // nx
-    bz = bx // nz
+    rows, cols = data.shape
+    half = cols // 2
+    bx = rows // nx
+    bz = bx // (nz // 2)
+    lanes = half // 2
     steps = (1, -1)
 
     def xblock(h, k):
-        return pl.ds(pl.multiple_of(h * half + lax.rem(k + 4 * nx, nx) * bx, 8), bx)
+        return (pl.ds(pl.multiple_of(lax.rem(k + 4 * nx, nx) * bx, 8), bx), pl.ds(h * half, half))
 
     def zblock(k):
-        return pl.ds(pl.multiple_of(lax.rem(k + 4 * nz, nz) * bz, 8), bz)
+        k = lax.rem(k + 4 * nz, nz)
+        return (pl.ds(pl.multiple_of((k // 2) * bz, 8), bz), pl.ds(pl.multiple_of(lax.rem(k, 2) * lanes, 128), lanes))
 
     def oblock(h, kx, kz):
-        at = h * half + lax.rem(kx + 4 * nx, nx) * bx + lax.rem(kz + 4 * nz, nz) * bz
-        return pl.ds(pl.multiple_of(at, 8), bz)
+        r, c = zblock(kz)
+        start = pl.multiple_of(lax.rem(kx + 4 * nx, nx) * bx + r.start, 8)
+        return (pl.ds(start, bz), pl.ds(pl.multiple_of(h * half + c.start, 128), lanes))
 
     def obig(h, kx):
-        return pl.ds(pl.multiple_of(h * half + lax.rem(kx + 4 * nx, nx) * bx, 8), bx)
+        return xblock(h, kx)
 
     for s in range(nx - 1):
         copies = []
@@ -93,7 +89,8 @@
         for h in range(2):
             sg = steps[h]
             copies[h].wait_recv()
-            xs[h, s] = xs[h, s] + data[xblock(h, ix - sg * (s + 2))]
+            r, c = xblock(h, ix - sg * (s + 2))
+            xs[h, s] = xs[h, s] + data[r, c]
             copies[h].wait_send()
     last = nx - 2
     for c in chan_one:
@@ -107,28 +104,38 @@
     for h in range(2):
         for d in range(1, nz):
             c = pltpu.make_async_remote_copy(
-                src_ref=xs.at[h, last, zblock(iz + d)], dst_ref=zs.at[h, d - 1],
+                src_ref=xs.at[(h, last) + zblock(iz + d)], dst_ref=zs.at[h, d - 1],
                 send_sem=zsend.at[h * nz + d], recv_sem=zrecv.at[h * nz + d],
                 device_id=z_peer[d], device_id_type=MESH_ID)
             c.start()
             copies.append(c)
+    own = [pltpu.make_async_copy(xs.at[(h, last) + zblock(iz)], zs.at[h, nz - 1], local.at[h]) for h in range(2)]
+    for c in own:
+        c.start()
+    for c in own:
+        c.wait()
     for c in copies:
         c.wait_recv()
     for h in range(2):
-        acc = xs[h, last, zblock(iz)]
+        acc = zs[h, nz - 1]
         for d in range(1, nz):
             acc = acc + zs[h, d - 1]
-        zs[h, nz - 1] = acc
+        zs[h, nz] = acc
     for c in copies:
         c.wait_send()
-    zl = nz - 1
+    zl = nz
     c = pltpu.make_async_remote_copy(
         src_ref=zs.at[:, zl], dst_ref=ys, send_sem=ysend.at[0], recv_sem=yrecv.at[0],
         device_id=partner, device_id_type=MESH_ID)
     c.start()
     c.wait_recv()
     for h in range(2):
-        out[oblock(h, ix, iz)] = zs[h, zl] + ys[h]
+        fin[h] = zs[h, zl] + ys[h]
+    placed = [pltpu.make_async_copy(fin.at[h], out.at[oblock(h, ix, iz)], local.at[2 + h]) for h in range(2)]
+    for p in placed:
+        p.start()
+    for p in placed:
+        p.wait()
     c.wait_send()
     copies = []
     for h in range(2):
@@ -157,8 +164,6 @@
             copies[h].wait_recv()
             copies[h].wait_send()
 
-    for ref, (at, size) in zip(term_outs, layout):
-        ref[...] = out[at : at + size]
     chan_two.wait_recv()
     total = part[me] + from_pair[0] + from_far[...]
     grad_out[...] = (cot[...].astype(jnp.float32) + total).astype(grad_out.dtype)
@@ -166,51 +171,70 @@
         c.wait_send()
     chan_two.wait_send()
 
-def row_group_allreduce(terms, nx, nz, part, cot):
-    cols = terms[0].shape[-1]
+def row_group_allreduce(pieces, nx, nz, part, cot):
+    cols = pieces[0].shape[-1]
     layout = []
     at = 0
-    for t in terms:
-        layout.append((at, t.shape[0]))
-        at += t.shape[0]
-    quantum = 2 * nx * nz * 8
+    for piece in pieces:
+        layout.append((at, piece.shape[0]))
+        at += piece.shape[0]
+    quantum = 8 * nx * (nz // 2)
     rows = -(-at // quantum) * quantum
-    half = rows // 2
-    bx = half // nx
-    bz = bx // nz
+    used = at
+    count = len(pieces)
+    half = cols // 2
+    bx = rows // nx
+    bz = bx // (nz // 2)
     sems = [pltpu.SemaphoreType.DMA((2 * nx,)), pltpu.SemaphoreType.DMA((2 * nx,)),
             pltpu.SemaphoreType.DMA((2 * nz,)), pltpu.SemaphoreType.DMA((2 * nz,)),
             pltpu.SemaphoreType.DMA((1,)), pltpu.SemaphoreType.DMA((1,)),
             pltpu.SemaphoreType.DMA((2 * nz,)), pltpu.SemaphoreType.DMA((2 * nz,)),
             pltpu.SemaphoreType.DMA((2 * nx,)), pltpu.SemaphoreType.DMA((2 * nx,)),
-            pltpu.SemaphoreType.DMA((2, 3))]
+            pltpu.SemaphoreType.DMA((2, 3)), pltpu.SemaphoreType.DMA((4,)),
+            pltpu.SemaphoreType.DMA((2 * count,))]
     block = part.shape[1:]
-    count = len(terms)
 
     def body(*refs):
-        ins, outs, scratch = refs[: count + 2], refs[count + 2 : 2 * count + 3], refs[2 * count + 3 :]
-        _sum_kernel(nx, nz, layout, ins[:count], ins[count], ins[count + 1], outs[:count], outs[count],
-                    *scratch[:8], scratch[8:])
+        ins, outs = refs[:count], refs[count + 2 : 2 * count + 2]
+        part, cot, grad_out = refs[count], refs[count + 1], refs[2 * count + 2]
+        data, out, xs, zs, ys, fin, from_pair, from_far, relay = refs[2 * count + 3 : 2 * count + 12]
+        s = refs[2 * count + 12 :]
+        moves = s[-1]
+        packs = [pltpu.make_async_copy(ref, data.at[pl.ds(at, size)], moves.at[i])
+                 for i, (ref, (at, size)) in enumerate(zip(ins, layout))]
+        for c in packs:
+            c.start()
+        data[used:] = jnp.zeros((rows - used, cols), jnp.float32)
+        for c in packs:
+            c.wait()
+        _sum_kernel(nx, nz, data, part, cot, out, grad_out, xs, zs, ys, fin, from_pair, from_far, relay, s[:-1])
+        unpacks = [pltpu.make_async_copy(out.at[pl.ds(at, size)], ref, moves.at[count + i])
+                   for i, (ref, (at, size)) in enumerate(zip(outs, layout))]
+        for c in unpacks:
+            c.start()
+        for c in unpacks:
+            c.wait()
 
     return pl.pallas_call(
         body,
-        out_shape=tuple(jax.ShapeDtypeStruct(t.shape, jnp.float32) for t in terms)
+        out_shape=tuple(jax.ShapeDtypeStruct(p.shape, jnp.float32) for p in pieces)
         + (jax.ShapeDtypeStruct(cot.shape, cot.dtype),),
         in_specs=[pl.BlockSpec(memory_space=pltpu.VMEM)] * (count + 2),
         out_specs=(pl.BlockSpec(memory_space=pltpu.VMEM),) * (count + 1),
         scratch_shapes=[
             pltpu.VMEM((rows, cols), jnp.float32),
             pltpu.VMEM((rows, cols), jnp.float32),
-            pltpu.VMEM((2, nx - 1, bx, cols), jnp.float32),
-            pltpu.VMEM((2, nz, bz, cols), jnp.float32),
-            pltpu.VMEM((2, bz, cols), jnp.float32),
+            pltpu.VMEM((2, nx - 1, bx, half), jnp.float32),
+            pltpu.VMEM((2, nz + 1, bz, half // 2), jnp.float32),
+            pltpu.VMEM((2, bz, half // 2), jnp.float32),
+            pltpu.VMEM((2, bz, half // 2), jnp.float32),
             pltpu.VMEM((2,) + block, jnp.float32),
             pltpu.VMEM(block, jnp.float32),
             pltpu.VMEM(block, jnp.float32),
         ] + sems,
         compiler_params=pltpu.CompilerParams(collective_id=0, has_side_effects=True,
                                              vmem_limit_bytes=48 * 1024 * 1024),
-    )(*terms, part, cot)
+    )(*pieces, part, cot)
 
 
 def _chan_gather_kernel(first, second, out_first, out_second, sems):
@@ -348,11 +372,13 @@
     grad_w1 = jnp.dot(flat_inputs.T, flat_act, preferred_element_type=jnp.float32)
     part = jnp.einsum("rwh,ch->rwc", grad_act, expand_w, preferred_element_type=jnp.float32)
     part = part.reshape((4, -1) + part.shape[1:])
+    small = jnp.concatenate([grad_k, grad_b1[None], grad_bd[None]], axis=0)
+    taps_count = grad_k.shape[0]
+    small = jnp.pad(small, ((0, -small.shape[0] % 8), (0, 0)))
     nx, nz = lax.axis_size("x"), lax.axis_size("z")
-    w1, w2, k, b1, bd, input_grad = row_group_allreduce(
-        [grad_w1, grad_w2, grad_k, grad_b1[None], grad_bd[None]], nx, nz, part, cotangent
-    )
-    return (input_grad, w1, b1[0], k, bd[0], w2)
+    w1, w2, small, input_grad = row_group_allreduce([grad_w1, grad_w2, small], nx, nz, part, cotangent)
+    summed = [w1, small[taps_count], small[:taps_count], small[taps_count + 1], w2]
+    return (input_grad, summed[0], summed[1], summed[2], summed[3], summed[4])
 
 
 def solution(mesh):

time: 192 us -> 168 us (0.88)
  Pallas kernels: 119 us -> 98.7 us
  local copies, waits for them, and re-layouts: 9.27 us -> 4.23 us
  waiting for transfers between devices: 6.16 us -> 10.5 us
  matrix products: 12.2 us -> 9.06 us
    pallas_call x1, Pallas kernels: 100 us -> 79.4 us  [row_group_allreduce(): pl.pallas_call(body, out_shape=tuple((jax.ShapeDtypeStruct(p.shape, jnp.f...]
    ppermute x2, waiting for transfers between devices: 4.75 us -> 8.16 us  [extended(): lax.ppermute(lax.slice_in_dim(block, block.shape[dim] - width, None, axis...]
    another operation x1 -> x0, local copies, waits for them, and re-layouts: 2.96 us -> none  [shards(): grad_k = jnp.stack(taps, axis=0)]
    unnamed x48 -> x20, local copies, waits for them, and re-layouts: 5.49 us -> 3.37 us
  transfers between devices with their start and end apart: 4 -> 4, of which waited for: 3 -> 4; matrix products, arithmetic and copies ran while one was open for 3% -> 0% of each run, Pallas kernels for 0% -> 0%
where the time goes in v5:
time: 168 us; the launch traced here: 166 us
  Pallas kernels  98.7 us (59%)
  starting transfers between devices  23 us (14%)
  other arithmetic  19.7 us (12%)
  waiting for transfers between devices  10.5 us (6%)
  matrix products  9.06 us (5%)
  local copies, waits for them, and re-layouts  4.23 us (3%)
    pallas_call x1, Pallas kernels, row_group_allreduce(): pl.pallas_call(body, out_shape=tuple((jax.ShapeDtypeStruct(p.shape, jnp.f...  79.4 us
    pallas_call x1, Pallas kernels, chan_gather(): pl.pallas_call(_chan_gather_kernel, out_shape=(jax.ShapeDtypeStruct(shape...  19.3 us
    ppermute x2, starting transfers between devices, extended(): lax.ppermute(lax.slice_in_dim(block, 0, width, axis=dim), axis, backward)  17.6 us
    ppermute x2, waiting for transfers between devices, extended(): lax.ppermute(lax.slice_in_dim(block, block.shape[dim] - width, None, axis...  8.16 us
    reduce_sum x1, other arithmetic, shards(): grad_b1 = jnp.sum(flat_act.astype(jnp.float32), axis=0)  7.26 us
    convert_element_type x1, other arithmetic, shards(): mixed = mixed.astype(jnp.bfloat16).reshape(nrows * ncols, hslice)  6.69 us
    ppermute x2, starting transfers between devices, extended(): lax.ppermute(lax.slice_in_dim(block, block.shape[dim] - width, None, axis...  5.34 us
    reduce_sum x1, other arithmetic, shards(): jnp.sum(padded[row_tap:row_tap + nrows, col_tap:col_tap + ncols] * grad_p...  4.67 us
  transfers between devices with their start and end apart: 4, of which 4 were waited for; matrix products, arithmetic and copies ran while one was open for 0% of the time, Pallas kernels for 0%

profile of v5, /device:TPU:8, one launch (start us, length us, event | category | flops | bytes accessed | tf_op | source)
XLA Modules:
  0.0 166.0 jit_solution(1183453692399025641)
XLA Ops:
  0.6 0.0 copy-start
  0.6 19.3 %shard_map.118 = (bf16[4,2,128,512]{3,2,1,0:T(8,128)(2,1)}, bf16[4,2,128,512]{3,2,1,0:T(8,128)(2,1)}) custom-call(bf16[2,128,512]{2,1,0:T(8,128)(2,1)} %first.1, bf16[2,128,512]{2,1,0:T(8,128)(2,1)} %refs_4_.1), custom_call_target="tpu_custom_call" | custom-call | tf_op jit(solution)/shard_map/pallas_call | solution.py:286
  20.0 0.0 copy-start.2
  20.0 2.1 %multiply_convert_fusion.1 = (bf16[8,128,512]{2,1,0:T(8,128)(2,1)S(1)}, f32[8,128,512]{2,1,0:T(8,128)S(1)}) fusion(f32[512]{0:T(512)} %param.10, bf16[8,128,512]{2,1,0:T(8,128)(2,1)} %bitcast.164, bf16[512,512]{1,0:T(8,128)(2,1)S(1)} %copy-done), kind=kOutput, calls=%fused_computation.121 | convolution fusion | flops 540016640 | bytes 4720640 | tf_op jit(solution)/shard_map/dot_general | solution.py:325
  22.2 3.4 %collective-permute-start = (bf16[2,128,512]{2,1,0:T(8,128)(2,1)S(1)}, bf16[2,128,512]{2,1,0:T(8,128)(2,1)S(1)}, u32[]{:S(2)}, u32[]{:S(2)}) collective-permute-start(bf16[2,128,512]{2,1,0:T(8,128)(2,1)S(1)} %get-tuple-element.50), channel_id=1, source_target_pairs={{0,4},{4,8},{8,12},{12,16},{16,20},{20,24},{24,28},{28,32},{32,36}... | collective-permute-start | bytes 786440 | tf_op jit(solution)/shard_map/ppermute | solution.py:304
  25.6 9.0 %collective-permute-start.1 = (bf16[2,128,512]{2,1,0:T(8,128)(2,1)S(1)}, bf16[2,128,512]{2,1,0:T(8,128)(2,1)S(1)}, u32[]{:S(2)}, u32[]{:S(2)}) collective-permute-start(bf16[2,128,512]{2,1,0:T(8,128)(2,1)S(1)} %get-tuple-element.51), channel_id=1, source_target_pairs={{4,0},{8,4},{12,8},{16,12},{20,16},{24,20},{28,24},{32,28},{36,32}... | collective-permute-start | bytes 786440 | tf_op jit(solution)/shard_map/ppermute | solution.py:307
  34.7 0.0 copy-start.3
  34.7 4.8 %collective-permute-done = bf16[2,128,512]{2,1,0:T(8,128)(2,1)S(1)} collective-permute-done((bf16[2,128,512]{2,1,0:T(8,128)(2,1)S(1)}, bf16[2,128,512]{2,1,0:T(8,128)(2,1)S(1)}, u32[]{:S(2)}, u32[]{:S(2)}) %collective-permute-start) | collective-permute-done | bytes 262176 | tf_op jit(solution)/shard_map/ppermute | solution.py:304
  39.5 1.2 collective-permute-done.1
  40.7 0.5 fusion.68
  41.2 0.0 copy-start.7
  41.3 6.7 %multiply_convert_fusion = (bf16[8,128,512]{2,1,0:T(8,128)(2,1)S(1)}, f32[8,128,512]{2,1,0:T(8,128)S(1)}) fusion(f32[12,132,512]{2,1,0:T(8,128)S(1)} %fusion.68, f32[512]{0:T(512)S(1)} %bitcast.93, f32[512]{0:T(512)S(1)} %bitcast.95, f32[512]{0:T(512)S(1)} %bitcast.99, f32[512]{0:T(512)S(1)} %bitcast.101, f32[512]{0:T(512)S(1)} %bitcast.103, ...), kind=kLoop, calls=%fused_computation.118 | loop fusion | flops 28835840 | bytes 55627776 | tf_op jit(solution)/shard_map/convert_element_type | solution.py:343
  48.0 3.4 %fusion.36 = (f32[512]{0:T(512)S(1)}, f32[512]{0:T(512)S(1)}, f32[512]{0:T(512)S(1)}, f32[512]{0:T(512)S(1)}, f32[512]{0:T(512)S(1)}, /*index=5*/f32[512]{0:T(51...) fusion(f32[12,132,512]{2,1,0:T(8,128)S(1)} %fusion.68, f32[8,128,512]{2,1,0:T(8,128)S(1)} %get-tuple-element.47, ...), kind=kOutput, calls=%fused_computation.66 | convolution fusion | flops 550498304 | bytes 19415040 | tf_op jit(solution)/shard_map/dot_general | solution.py:345
  51.4 4.7 %fusion.37 = (f32[512]{0:T(512)S(1)}, f32[512]{0:T(512)S(1)}, f32[512]{0:T(512)S(1)}, f32[512]{0:T(512)S(1)}, f32[512]{0:T(512)S(1)}, /*index=5*/f32[512]{0:T(51...) fusion(bf16[8,128,512]{2,1,0:T(8,128)(2,1)S(1)} %get-tuple-elem, ...), kind=kLoop, calls=%fused_computation.67 | loop fusion | flops 19389440 | bytes 38834176 | tf_op jit(solution)/shard_map/reduce_sum | solution.py:358
  56.1 1.9 %collective-permute-start.2 = (bf16[2,128,512]{2,1,0:T(8,128)(2,1)S(1)}, bf16[2,128,512]{2,1,0:T(8,128)(2,1)S(1)}, u32[]{:S(2)}, u32[]{:S(2)}) collective-permute-start(bf16[2,128,512]{2,1,0:T(8,128)(2,1)S(1)} %get-tuple-element.48), channel_id=1, source_target_pairs={{0,4},{4,8},{8,12},{12,16},{16,20},{20,24},{24,28},{28,32},{32,36}... | collective-permute-start | bytes 786440 | tf_op jit(solution)/shard_map/ppermute | solution.py:304
  58.0 8.6 %collective-permute-start.3 = (bf16[2,128,512]{2,1,0:T(8,128)(2,1)S(1)}, bf16[2,128,512]{2,1,0:T(8,128)(2,1)S(1)}, u32[]{:S(2)}, u32[]{:S(2)}) collective-permute-start(bf16[2,128,512]{2,1,0:T(8,128)(2,1)S(1)} %get-tuple-element.49), channel_id=1, source_target_pairs={{4,0},{8,4},{12,8},{16,12},{20,16},{24,20},{28,24},{32,28},{36,32}... | collective-permute-start | bytes 786440 | tf_op jit(solution)/shard_map/ppermute | solution.py:307
  66.6 0.7 fusion.81.refs_1_
  67.4 0.0 copy-start.4
  67.4 3.4 %collective-permute-done.2 = bf16[2,128,512]{2,1,0:T(8,128)(2,1)S(1)} collective-permute-done((bf16[2,128,512]{2,1,0:T(8,128)(2,1)S(1)}, bf16[2,128,512]{2,1,0:T(8,128)(2,1)S(1)}, u32[]{:S(2)}, u32[]{:S(2)}) %collective-permute-start.2) | collective-permute-done | bytes 262176 | tf_op jit(solution)/shard_map/ppermute | solution.py:304
  70.8 1.2 collective-permute-done.3
  71.9 0.5 fusion.62
  72.5 7.3 %convert_reduce_fusion.1 = (f32[512]{0:T(512)S(1)}, bf16[8,128,512]{2,1,0:T(8,128)(2,1)S(1)}) fusion(f32[8,128,512]{2,1,0:T(8,128)S(1)} %get-tuple-element.80, f32[512]{0:T(512)S(1)} %copy-done.4, f32[12,132,512]{2,1,0:T(8,128)S(1)} %fusion.62, f32[512]{0:T(512)S(1)} %bitcast.94, f32[512]{0:T(512)S(1)} %bitcast.96, f32[512]{0:T(512)S(1)} %bitcast.100, ...), kind=kLoop, calls=%fused_computation.117 | loop fusion | flops 32505344 | bytes 55629824 | tf_op jit(solution)/shard_map/reduce_sum | solution.py:371
  79.7 2.1 %fusion.69 = f32[8,128,512]{2,1,0:T(8,128)} fusion(bf16[8,128,512]{2,1,0:T(8,128)(2,1)S(1)} %get-tuple-element.45, bf16[512,512]{1,0:T(8,128)(2,1)S(1)} %copy-done), kind=kOutput, calls=%fused_computation.132 | convolution fusion | flops 536870912 | bytes 3670016 | tf_op jit(solution)/shard_map/rwh,ch->rwc/dot_general | solution.py:373
  81.8 0.7 fusion.80.refs_0_
  82.6 0.1 concatenate.11
  82.7 0.1 copy-done.1
  82.8 79.4 %shard_map.119 = (f32[512,512]{1,0:T(8,128)S(1)}, f32[512,512]{1,0:T(8,128)S(1)}, f32[32,512]{1,0:T(8,128)S(1)}, bf16[2,128,512]{2,1,0:T(8,128)(2,1)S(1)}) custom-call(f32[512,512]{1,0:T(8,128)S(1)} %fusion.80.refs_0_, f32[512,512]{1,0:T(8,128)S(1)} %fusion.81.refs_1_, f32[32,512]{1,0:T(8,128)S(1)} %pad.13.refs_2_, f32[4,2,128,512]{3,2,1,0:T(8,128)} %bitcast.82, ...), custom_call_target="tpu_custom_call" | custom-call | tf_op jit(solution)/shard_map/pallas_call | solution.py:218
  162.2 0.6 fusion.77
  162.8 0.7 copy.17
  163.5 1.0 copy.18
  164.4 0.6 copy.19
  165.1 1.0 copy.20
  (15 shorter events, 0.1 us)
Async XLA Ops:
  0.6 19.4 %copy-start = (bf16[512,512]{1,0:T(8,128)(2,1)S(1)}, bf16[512,512]{1,0:T(8,128)(2,1)}, u32[]{:S(2)}) copy-start(bf16[512,512]{1,0:T(8,128)(2,1)} %param.9) | copy-start | bytes 1572868
  20.0 14.6 %copy-start.2 = (f32[25,512]{1,0:T(8,128)S(1)}, f32[25,512]{1,0:T(8,128)}, u32[]{:S(2)}) copy-start(f32[25,512]{1,0:T(8,128)} %param.11) | copy-start | bytes 153604
  22.2 17.3 %collective-permute-start = (bf16[2,128,512]{2,1,0:T(8,128)(2,1)S(1)}, bf16[2,128,512]{2,1,0:T(8,128)(2,1)S(1)}, u32[]{:S(2)}, u32[]{:S(2)}) collective-permute-start(bf16[2,128,512]{2,1,0:T(8,128)(2,1)S(1)} %get-tuple-element.50), channel_id=1, source_target_pairs={{0,4},{4,8},{8,12},{12,16},{16,20},{20,24},{24,28},{28,32},{32,36}... | collective-permute-start | bytes 786440 | tf_op jit(solution)/shard_map/ppermute | solution.py:304
  25.6 15.1 %collective-permute-start.1 = (bf16[2,128,512]{2,1,0:T(8,128)(2,1)S(1)}, bf16[2,128,512]{2,1,0:T(8,128)(2,1)S(1)}, u32[]{:S(2)}, u32[]{:S(2)}) collective-permute-start(bf16[2,128,512]{2,1,0:T(8,128)(2,1)S(1)} %get-tuple-element.51), channel_id=1, source_target_pairs={{4,0},{8,4},{12,8},{16,12},{20,16},{24,20},{28,24},{32,28},{36,32}... | collective-permute-start | bytes 786440 | tf_op jit(solution)/shard_map/ppermute | solution.py:307
  34.7 6.5 %copy-start.3 = (f32[512]{0:T(512)S(1)}, f32[512]{0:T(512)}, u32[]{:S(2)}) copy-start(f32[512]{0:T(512)} %param.12) | copy-start | bytes 6148
  41.2 6.7 %copy-start.6 = (bf16[4,2,128,512]{3,2,1,0:T(8,128)(2,1)S(1)}, bf16[4,2,128,512]{3,2,1,0:T(8,128)(2,1)}, u32[]{:S(2)}) copy-start(bf16[4,2,128,512]{3,2,1,0:T(8,128)(2,1)} %get-tuple-element.13) | copy-start | bytes 3145732
  41.2 6.7 %copy-start.7 = (bf16[512,512]{1,0:T(8,128)(2,1)S(1)}, bf16[512,512]{1,0:T(8,128)(2,1)}, u32[]{:S(2)}) copy-start(bf16[512,512]{1,0:T(8,128)(2,1)} %param.13) | copy-start | bytes 1572868
  56.1 14.7 %collective-permute-start.2 = (bf16[2,128,512]{2,1,0:T(8,128)(2,1)S(1)}, bf16[2,128,512]{2,1,0:T(8,128)(2,1)S(1)}, u32[]{:S(2)}, u32[]{:S(2)}) collective-permute-start(bf16[2,128,512]{2,1,0:T(8,128)(2,1)S(1)} %get-tuple-element.48), channel_id=1, source_target_pairs={{0,4},{4,8},{8,12},{12,16},{16,20},{20,24},{24,28},{28,32},{32,36}... | collective-permute-start | bytes 786440 | tf_op jit(solution)/shard_map/ppermute | solution.py:304
  58.0 13.9 %collective-permute-start.3 = (bf16[2,128,512]{2,1,0:T(8,128)(2,1)S(1)}, bf16[2,128,512]{2,1,0:T(8,128)(2,1)S(1)}, u32[]{:S(2)}, u32[]{:S(2)}) collective-permute-start(bf16[2,128,512]{2,1,0:T(8,128)(2,1)S(1)} %get-tuple-element.49), channel_id=1, source_target_pairs={{4,0},{8,4},{12,8},{16,12},{20,16},{24,20},{28,24},{32,28},{36,32}... | collective-permute-start | bytes 786440 | tf_op jit(solution)/shard_map/ppermute | solution.py:307
  67.4 5.1 %copy-start.4 = (f32[512]{0:T(512)S(1)}, f32[512]{0:T(512)}, u32[]{:S(2)}) copy-start(f32[512]{0:T(512)} %param.10) | copy-start | bytes 6148
  79.7 2.1 %copy-start.5 = (bf16[4,2,128,512]{3,2,1,0:T(8,128)(2,1)S(1)}, bf16[4,2,128,512]{3,2,1,0:T(8,128)(2,1)}, u32[]{:S(2)}) copy-start(bf16[4,2,128,512]{3,2,1,0:T(8,128)(2,1)} %get-tuple-element.12) | copy-start | bytes 3145732
  81.8 1.0 copy-start.1

commit v6 on v5

--- a/solution.py
+++ b/solution.py
@@ -245,39 +245,28 @@
         return (coords[0], coords[1], coords[2], h, c)
 
     me = hi * 2 + core
-    across = hi * 2 + (1 - core)
-    over = (1 - hi) * 2 + core
-    pair, far = dev(hi, 1 - core), dev(1 - hi, core)
+    targets = (dev(hi, 1 - core), dev(1 - hi, core), dev(1 - hi, 1 - core))
 
     barrier = pltpu.get_barrier_semaphore()
-    for d in (pair, far):
+    for d in targets:
         pl.semaphore_signal(barrier, inc=1, device_id=d, device_id_type=MESH_ID)
-    pl.semaphore_wait(barrier, 2)
+    pl.semaphore_wait(barrier, len(targets))
 
     sources = (first, second)
     outs = (out_first, out_second)
-    step_one = []
+    copies = []
     for k in range(2):
-        for j, target in enumerate((pair, far)):
+        for j, target in enumerate(targets):
             c = pltpu.make_async_remote_copy(
                 src_ref=sources[k], dst_ref=outs[k].at[me], send_sem=sems.at[0, k, j],
                 recv_sem=sems.at[1, k, j], device_id=target, device_id_type=MESH_ID)
             c.start()
-            step_one.append(c)
+            copies.append(c)
     for k in range(2):
         outs[k][me] = sources[k][...]
-    for c in step_one:
+    for c in copies:
         c.wait_recv()
-    relay = []
-    for k in range(2):
-        c = pltpu.make_async_remote_copy(
-            src_ref=outs[k].at[over], dst_ref=outs[k].at[over], send_sem=sems.at[0, k, 2],
-            recv_sem=sems.at[1, k, 2], device_id=pair, device_id_type=MESH_ID)
-        c.start()
-        relay.append(c)
-    for c in relay:
-        c.wait_recv()
-    for c in step_one + relay:
+    for c in copies:
         c.wait_send()
 
 

time: 168 us -> 179 us (1.065); the launches traced: 166 us -> 179 us
  Pallas kernels: 98.7 us -> 112 us
    pallas_call x1, Pallas kernels: 19.3 us -> 29.2 us  [chan_gather(): pl.pallas_call(_chan_gather_kernel, out_shape=(jax.ShapeDtypeStruct(shape...]
    pallas_call x1, Pallas kernels: 79.4 us -> 83.2 us  [row_group_allreduce(): pl.pallas_call(body, out_shape=tuple((jax.ShapeDtypeStruct(p.shape, jnp.f...]
where the time goes in v6:
time: 179 us
  Pallas kernels  112 us (63%)
  starting transfers between devices  22.4 us (13%)
  other arithmetic  19.6 us (11%)
  waiting for transfers between devices  10.3 us (6%)
  matrix products  9.07 us (5%)
  local copies, waits for them, and re-layouts  4.23 us (2%)
    pallas_call x1, Pallas kernels, row_group_allreduce(): pl.pallas_call(body, out_shape=tuple((jax.ShapeDtypeStruct(p.shape, jnp.f...  83.2 us
    pallas_call x1, Pallas kernels, chan_gather(): pl.pallas_call(_chan_gather_kernel, out_shape=(jax.ShapeDtypeStruct(shape...  29.2 us
    ppermute x2, starting transfers between devices, extended(): lax.ppermute(lax.slice_in_dim(block, 0, width, axis=dim), axis, backward)  17 us
    ppermute x2, waiting for transfers between devices, extended(): lax.ppermute(lax.slice_in_dim(block, block.shape[dim] - width, None, axis...  7.94 us
    reduce_sum x1, other arithmetic, shards(): grad_b1 = jnp.sum(flat_act.astype(jnp.float32), axis=0)  7.26 us
    convert_element_type x1, other arithmetic, shards(): mixed = mixed.astype(jnp.bfloat16).reshape(nrows * ncols, hslice)  6.69 us
    ppermute x2, starting transfers between devices, extended(): lax.ppermute(lax.slice_in_dim(block, block.shape[dim] - width, None, axis...  5.32 us
    reduce_sum x1, other arithmetic, shards(): jnp.sum(padded[row_tap:row_tap + nrows, col_tap:col_tap + ncols] * grad_p...  4.67 us
  transfers between devices with their start and end apart: 4, of which 4 were waited for; matrix products, arithmetic and copies ran while one was open for 0% of the time, Pallas kernels for 0%

profile of v6, /device:TPU:8, one launch (start us, length us, event | category | flops | bytes accessed | tf_op | source)
XLA Modules:
  0.0 178.9 jit_solution(783933350178269889)
XLA Ops:
  0.6 0.0 copy-start
  0.6 29.2 %shard_map.118 = (bf16[4,2,128,512]{3,2,1,0:T(8,128)(2,1)}, bf16[4,2,128,512]{3,2,1,0:T(8,128)(2,1)}) custom-call(bf16[2,128,512]{2,1,0:T(8,128)(2,1)} %first.1, bf16[2,128,512]{2,1,0:T(8,128)(2,1)} %refs_4_.1), custom_call_target="tpu_custom_call" | custom-call | tf_op jit(solution)/shard_map/pallas_call | solution.py:275
  29.8 0.0 copy-start.2
  29.8 2.1 %multiply_convert_fusion.1 = (bf16[8,128,512]{2,1,0:T(8,128)(2,1)S(1)}, f32[8,128,512]{2,1,0:T(8,128)S(1)}) fusion(f32[512]{0:T(512)} %param.10, bf16[8,128,512]{2,1,0:T(8,128)(2,1)} %bitcast.164, bf16[512,512]{1,0:T(8,128)(2,1)S(1)} %copy-done), kind=kOutput, calls=%fused_computation.121 | convolution fusion | flops 540016640 | bytes 4720640 | tf_op jit(solution)/shard_map/dot_general | solution.py:314
  32.0 3.4 %collective-permute-start = (bf16[2,128,512]{2,1,0:T(8,128)(2,1)S(1)}, bf16[2,128,512]{2,1,0:T(8,128)(2,1)S(1)}, u32[]{:S(2)}, u32[]{:S(2)}) collective-permute-start(bf16[2,128,512]{2,1,0:T(8,128)(2,1)S(1)} %get-tuple-element.50), channel_id=1, source_target_pairs={{0,4},{4,8},{8,12},{12,16},{16,20},{20,24},{24,28},{28,32},{32,36}... | collective-permute-start | bytes 786440 | tf_op jit(solution)/shard_map/ppermute | solution.py:293
  35.4 8.4 %collective-permute-start.1 = (bf16[2,128,512]{2,1,0:T(8,128)(2,1)S(1)}, bf16[2,128,512]{2,1,0:T(8,128)(2,1)S(1)}, u32[]{:S(2)}, u32[]{:S(2)}) collective-permute-start(bf16[2,128,512]{2,1,0:T(8,128)(2,1)S(1)} %get-tuple-element.51), channel_id=1, source_target_pairs={{4,0},{8,4},{12,8},{16,12},{20,16},{24,20},{28,24},{32,28},{36,32}... | collective-permute-start | bytes 786440 | tf_op jit(solution)/shard_map/ppermute | solution.py:296
  43.9 0.0 copy-start.3
  43.9 4.7 %collective-permute-done = bf16[2,128,512]{2,1,0:T(8,128)(2,1)S(1)} collective-permute-done((bf16[2,128,512]{2,1,0:T(8,128)(2,1)S(1)}, bf16[2,128,512]{2,1,0:T(8,128)(2,1)S(1)}, u32[]{:S(2)}, u32[]{:S(2)}) %collective-permute-start) | collective-permute-done | bytes 262176 | tf_op jit(solution)/shard_map/ppermute | solution.py:293
  48.7 1.2 collective-permute-done.1
  49.8 0.5 fusion.68
  50.4 0.0 copy-start.7
  50.4 6.7 %multiply_convert_fusion = (bf16[8,128,512]{2,1,0:T(8,128)(2,1)S(1)}, f32[8,128,512]{2,1,0:T(8,128)S(1)}) fusion(f32[12,132,512]{2,1,0:T(8,128)S(1)} %fusion.68, f32[512]{0:T(512)S(1)} %bitcast.93, f32[512]{0:T(512)S(1)} %bitcast.95, f32[512]{0:T(512)S(1)} %bitcast.99, f32[512]{0:T(512)S(1)} %bitcast.101, f32[512]{0:T(512)S(1)} %bitcast.103, ...), kind=kLoop, calls=%fused_computation.118 | loop fusion | flops 28835840 | bytes 55627776 | tf_op jit(solution)/shard_map/convert_element_type | solution.py:332
  57.1 3.4 %fusion.36 = (f32[512]{0:T(512)S(1)}, f32[512]{0:T(512)S(1)}, f32[512]{0:T(512)S(1)}, f32[512]{0:T(512)S(1)}, f32[512]{0:T(512)S(1)}, /*index=5*/f32[512]{0:T(51...) fusion(f32[12,132,512]{2,1,0:T(8,128)S(1)} %fusion.68, f32[8,128,512]{2,1,0:T(8,128)S(1)} %get-tuple-element.47, ...), kind=kOutput, calls=%fused_computation.66 | convolution fusion | flops 550498304 | bytes 19415040 | tf_op jit(solution)/shard_map/dot_general | solution.py:334
  60.5 4.7 %fusion.37 = (f32[512]{0:T(512)S(1)}, f32[512]{0:T(512)S(1)}, f32[512]{0:T(512)S(1)}, f32[512]{0:T(512)S(1)}, f32[512]{0:T(512)S(1)}, /*index=5*/f32[512]{0:T(51...) fusion(bf16[8,128,512]{2,1,0:T(8,128)(2,1)S(1)} %get-tuple-elem, ...), kind=kLoop, calls=%fused_computation.67 | loop fusion | flops 19389440 | bytes 38834176 | tf_op jit(solution)/shard_map/reduce_sum | solution.py:347
  65.2 1.9 %collective-permute-start.2 = (bf16[2,128,512]{2,1,0:T(8,128)(2,1)S(1)}, bf16[2,128,512]{2,1,0:T(8,128)(2,1)S(1)}, u32[]{:S(2)}, u32[]{:S(2)}) collective-permute-start(bf16[2,128,512]{2,1,0:T(8,128)(2,1)S(1)} %get-tuple-element.48), channel_id=1, source_target_pairs={{0,4},{4,8},{8,12},{12,16},{16,20},{20,24},{24,28},{28,32},{32,36}... | collective-permute-start | bytes 786440 | tf_op jit(solution)/shard_map/ppermute | solution.py:293
  67.1 8.6 %collective-permute-start.3 = (bf16[2,128,512]{2,1,0:T(8,128)(2,1)S(1)}, bf16[2,128,512]{2,1,0:T(8,128)(2,1)S(1)}, u32[]{:S(2)}, u32[]{:S(2)}) collective-permute-start(bf16[2,128,512]{2,1,0:T(8,128)(2,1)S(1)} %get-tuple-element.49), channel_id=1, source_target_pairs={{4,0},{8,4},{12,8},{16,12},{20,16},{24,20},{28,24},{32,28},{36,32}... | collective-permute-start | bytes 786440 | tf_op jit(solution)/shard_map/ppermute | solution.py:296
  75.8 0.7 fusion.81.refs_1_
  76.5 0.0 copy-start.4
  76.5 3.2 %collective-permute-done.2 = bf16[2,128,512]{2,1,0:T(8,128)(2,1)S(1)} collective-permute-done((bf16[2,128,512]{2,1,0:T(8,128)(2,1)S(1)}, bf16[2,128,512]{2,1,0:T(8,128)(2,1)S(1)}, u32[]{:S(2)}, u32[]{:S(2)}) %collective-permute-start.2) | collective-permute-done | bytes 262176 | tf_op jit(solution)/shard_map/ppermute | solution.py:293
  79.8 1.2 collective-permute-done.3
  80.9 0.5 fusion.62
  81.5 7.3 %convert_reduce_fusion.1 = (f32[512]{0:T(512)S(1)}, bf16[8,128,512]{2,1,0:T(8,128)(2,1)S(1)}) fusion(f32[8,128,512]{2,1,0:T(8,128)S(1)} %get-tuple-element.80, f32[512]{0:T(512)S(1)} %copy-done.4, f32[12,132,512]{2,1,0:T(8,128)S(1)} %fusion.62, f32[512]{0:T(512)S(1)} %bitcast.94, f32[512]{0:T(512)S(1)} %bitcast.96, f32[512]{0:T(512)S(1)} %bitcast.100, ...), kind=kLoop, calls=%fused_computation.117 | loop fusion | flops 32505344 | bytes 55629824 | tf_op jit(solution)/shard_map/reduce_sum | solution.py:360
  88.7 2.1 %fusion.69 = f32[8,128,512]{2,1,0:T(8,128)} fusion(bf16[8,128,512]{2,1,0:T(8,128)(2,1)S(1)} %get-tuple-element.45, bf16[512,512]{1,0:T(8,128)(2,1)S(1)} %copy-done), kind=kOutput, calls=%fused_computation.132 | convolution fusion | flops 536870912 | bytes 3670016 | tf_op jit(solution)/shard_map/rwh,ch->rwc/dot_general | solution.py:362
  90.8 0.7 fusion.80.refs_0_
  91.6 0.1 concatenate.11
  91.7 0.1 copy-done.1
  91.8 83.2 %shard_map.119 = (f32[512,512]{1,0:T(8,128)S(1)}, f32[512,512]{1,0:T(8,128)S(1)}, f32[32,512]{1,0:T(8,128)S(1)}, bf16[2,128,512]{2,1,0:T(8,128)(2,1)S(1)}) custom-call(f32[512,512]{1,0:T(8,128)S(1)} %fusion.80.refs_0_, f32[512,512]{1,0:T(8,128)S(1)} %fusion.81.refs_1_, f32[32,512]{1,0:T(8,128)S(1)} %pad.13.refs_2_, f32[4,2,128,512]{3,2,1,0:T(8,128)} %bitcast.82, ...), custom_call_target="tpu_custom_call" | custom-call | tf_op jit(solution)/shard_map/pallas_call | solution.py:218
  175.0 0.6 fusion.77
  175.6 0.7 copy.17
  176.3 1.0 copy.18
  177.3 0.6 copy.19
  177.9 1.0 copy.20
  (15 shorter events, 0.1 us)
Async XLA Ops:
  0.6 29.2 %copy-start = (bf16[512,512]{1,0:T(8,128)(2,1)S(1)}, bf16[512,512]{1,0:T(8,128)(2,1)}, u32[]{:S(2)}) copy-start(bf16[512,512]{1,0:T(8,128)(2,1)} %param.9) | copy-start | bytes 1572868
  29.8 14.0 %copy-start.2 = (f32[25,512]{1,0:T(8,128)S(1)}, f32[25,512]{1,0:T(8,128)}, u32[]{:S(2)}) copy-start(f32[25,512]{1,0:T(8,128)} %param.11) | copy-start | bytes 153604
  32.0 16.6 %collective-permute-start = (bf16[2,128,512]{2,1,0:T(8,128)(2,1)S(1)}, bf16[2,128,512]{2,1,0:T(8,128)(2,1)S(1)}, u32[]{:S(2)}, u32[]{:S(2)}) collective-permute-start(bf16[2,128,512]{2,1,0:T(8,128)(2,1)S(1)} %get-tuple-element.50), channel_id=1, source_target_pairs={{0,4},{4,8},{8,12},{12,16},{16,20},{20,24},{24,28},{28,32},{32,36}... | collective-permute-start | bytes 786440 | tf_op jit(solution)/shard_map/ppermute | solution.py:293
  35.4 14.4 %collective-permute-start.1 = (bf16[2,128,512]{2,1,0:T(8,128)(2,1)S(1)}, bf16[2,128,512]{2,1,0:T(8,128)(2,1)S(1)}, u32[]{:S(2)}, u32[]{:S(2)}) collective-permute-start(bf16[2,128,512]{2,1,0:T(8,128)(2,1)S(1)} %get-tuple-element.51), channel_id=1, source_target_pairs={{4,0},{8,4},{12,8},{16,12},{20,16},{24,20},{28,24},{32,28},{36,32}... | collective-permute-start | bytes 786440 | tf_op jit(solution)/shard_map/ppermute | solution.py:296
  43.9 6.4 %copy-start.3 = (f32[512]{0:T(512)S(1)}, f32[512]{0:T(512)}, u32[]{:S(2)}) copy-start(f32[512]{0:T(512)} %param.12) | copy-start | bytes 6148
  50.4 6.7 %copy-start.6 = (bf16[4,2,128,512]{3,2,1,0:T(8,128)(2,1)S(1)}, bf16[4,2,128,512]{3,2,1,0:T(8,128)(2,1)}, u32[]{:S(2)}) copy-start(bf16[4,2,128,512]{3,2,1,0:T(8,128)(2,1)} %get-tuple-element.13) | copy-start | bytes 3145732
  50.4 6.7 %copy-start.7 = (bf16[512,512]{1,0:T(8,128)(2,1)S(1)}, bf16[512,512]{1,0:T(8,128)(2,1)}, u32[]{:S(2)}) copy-start(bf16[512,512]{1,0:T(8,128)(2,1)} %param.13) | copy-start | bytes 1572868
  65.2 14.5 %collective-permute-start.2 = (bf16[2,128,512]{2,1,0:T(8,128)(2,1)S(1)}, bf16[2,128,512]{2,1,0:T(8,128)(2,1)S(1)}, u32[]{:S(2)}, u32[]{:S(2)}) collective-permute-start(bf16[2,128,512]{2,1,0:T(8,128)(2,1)S(1)} %get-tuple-element.48), channel_id=1, source_target_pairs={{0,4},{4,8},{8,12},{12,16},{16,20},{20,24},{24,28},{28,32},{32,36}... | collective-permute-start | bytes 786440 | tf_op jit(solution)/shard_map/ppermute | solution.py:293
  67.1 13.8 %collective-permute-start.3 = (bf16[2,128,512]{2,1,0:T(8,128)(2,1)S(1)}, bf16[2,128,512]{2,1,0:T(8,128)(2,1)S(1)}, u32[]{:S(2)}, u32[]{:S(2)}) collective-permute-start(bf16[2,128,512]{2,1,0:T(8,128)(2,1)S(1)} %get-tuple-element.49), channel_id=1, source_target_pairs={{4,0},{8,4},{12,8},{16,12},{20,16},{24,20},{28,24},{32,28},{36,32}... | collective-permute-start | bytes 786440 | tf_op jit(solution)/shard_map/ppermute | solution.py:296
  76.5 4.9 %copy-start.4 = (f32[512]{0:T(512)S(1)}, f32[512]{0:T(512)}, u32[]{:S(2)}) copy-start(f32[512]{0:T(512)} %param.10) | copy-start | bytes 6148
  88.7 2.1 %copy-start.5 = (bf16[4,2,128,512]{3,2,1,0:T(8,128)(2,1)S(1)}, bf16[4,2,128,512]{3,2,1,0:T(8,128)(2,1)}, u32[]{:S(2)}) copy-start(bf16[4,2,128,512]{3,2,1,0:T(8,128)(2,1)} %get-tuple-element.12) | copy-start | bytes 3145732
  90.8 1.0 copy-start.1

commit v7 on v5

--- a/solution.py
+++ b/solution.py
@@ -329,26 +329,35 @@
     )
     hidden, slope_one = gelu_parts(pre_one)
     hidden = hidden.astype(jnp.bfloat16)
-    rimmed = extended(hidden, ((ROW_AXES, 0),), 2)
-    padded = jnp.pad(rimmed, ((0, 0), (2, 2), (0, 0))).astype(jnp.float32)
-    pre_two = jnp.zeros((nrows, ncols, hslice), jnp.float32) + depth_b
+    count = 1
+    for name in ROW_AXES:
+        count *= lax.axis_size(name)
+    forward = [(i, i + 1) for i in range(count - 1)]
+    backward = [(t, f) for f, t in forward]
+    low = lax.ppermute(jnp.concatenate([hidden[nrows - 4 :], rows_cot[nrows - 2 :]], axis=0), ROW_AXES, forward)
+    high = lax.ppermute(jnp.concatenate([hidden[:4], rows_cot[:2]], axis=0), ROW_AXES, backward)
+    hidden_ext = jnp.concatenate([low[:4], hidden, high[:4]], axis=0)
+    cot_ext = jnp.concatenate([low[4:], rows_cot, high[4:]], axis=0)
+    wide = nrows + 4
+    padded_ext = jnp.pad(hidden_ext, ((0, 0), (2, 2), (0, 0))).astype(jnp.float32)
+    padded = padded_ext[2 : 2 + wide]
+    pre_two = jnp.zeros((wide, ncols, hslice), jnp.float32) + depth_b
     for row_tap in range(5):
         for col_tap in range(5):
             pre_two = (
                 pre_two
                 + depth_k[5 * row_tap + col_tap]
-                * padded[row_tap : row_tap + nrows, col_tap : col_tap + ncols]
+                * padded_ext[row_tap : row_tap + wide, col_tap : col_tap + ncols]
             )
     mixed, slope_two = gelu_parts(pre_two)
-    mixed = mixed.astype(jnp.bfloat16).reshape(nrows * ncols, hslice)
+    mixed = mixed[2 : 2 + nrows].astype(jnp.bfloat16).reshape(nrows * ncols, hslice)
     grad_w2 = jnp.dot(mixed.T, flat_cotan, preferred_element_type=jnp.float32)
-    grad_mixed = jnp.dot(flat_cotan, project_w.T, preferred_element_type=jnp.float32).reshape(
-        nrows, ncols, hslice
-    )
-    grad_pre = (grad_mixed * slope_two).astype(jnp.bfloat16)
-    grad_pre_f = grad_pre.astype(jnp.float32)
+    grad_mixed = jnp.dot(
+        cot_ext.reshape(wide * ncols, cin), project_w.T, preferred_element_type=jnp.float32
+    ).reshape(wide, ncols, hslice)
+    grad_rimmed = (grad_mixed * slope_two).astype(jnp.bfloat16)
+    grad_pre_f = grad_rimmed[2 : 2 + nrows].astype(jnp.float32)
     grad_bd = jnp.sum(grad_pre_f, axis=(0, 1))
-    grad_rimmed = extended(grad_pre, ((ROW_AXES, 0),), 2)
     grad_pad = jnp.pad(grad_rimmed, ((0, 0), (2, 2), (0, 0))).astype(jnp.float32)
     taps = []
     grad_hidden = jnp.zeros((nrows, ncols, hslice), jnp.float32)

time: 168 us -> 183 us (1.089)
  starting transfers between devices: 23 us -> 12.4 us
  other arithmetic: 19.7 us -> 26.4 us
  waiting for transfers between devices: 10.5 us -> 17.2 us
  Pallas kernels: 98.7 us -> 105 us
  local copies, waits for them, and re-layouts: 4.23 us -> 9.07 us
  matrix products: 9.06 us -> 11.2 us
    ppermute x4 -> x2, starting transfers between devices: 23 us -> 12.4 us  [the longest x1 8.98 us: shards(): lax.ppermute(jnp.concatenate([hidden[:4], rows_cot[:2]], axis=0), ROW_AXE...]
    mul x0 -> x1, other arithmetic: none -> 9.93 us  [gelu_parts(): cdf = 0.5 * (1.0 + lax.erf(pre * 0.7071067811865476))]
    ppermute x4 -> x2, waiting for transfers between devices: 10.5 us -> 17.2 us  [the longest x1 16 us: shards(): lax.ppermute(jnp.concatenate([hidden[nrows - 4:], rows_cot[nrows - 2:]],...]
    pallas_call x1, Pallas kernels: 79.4 us -> 85.8 us  [row_group_allreduce(): pl.pallas_call(body, out_shape=tuple((jax.ShapeDtypeStruct(p.shape, jnp.f...]
    convert_element_type x2 -> x1, other arithmetic: 7.2 us -> 0.79 us  [shards(): jnp.pad(hidden_ext, ((0, 0), (2, 2), (0, 0))).astype(jnp.float32)]
    unnamed x20 -> x26, local copies, waits for them, and re-layouts: 3.37 us -> 6.18 us
    slice x2 -> x6, local copies, waits for them, and re-layouts: 0.07 us -> 2.11 us  [the longest x2 1.94 us: shards(): cot_ext = jnp.concatenate([low[4:], rows_cot, high[4:]], axis=0)]
    reduce_sum x1 -> x2, other arithmetic: 4.67 us -> 6.52 us  [shards(): jnp.sum(padded[row_tap:row_tap + nrows, col_tap:col_tap + ncols] * grad_p...]
  transfers between devices with their start and end apart: 4 -> 2, of which waited for: 4 -> 2; matrix products, arithmetic and copies ran while one was open for 0% -> 0% of each run, Pallas kernels for 0% -> 0%
where the time goes in v7:
time: 183 us; the launch traced here: 182 us
  Pallas kernels  105 us (57%)
  other arithmetic  26.4 us (14%)
  waiting for transfers between devices  17.2 us (9%)
  starting transfers between devices  12.4 us (7%)
  matrix products  11.2 us (6%)
  local copies, waits for them, and re-layouts  9.07 us (5%)
    pallas_call x1, Pallas kernels, row_group_allreduce(): pl.pallas_call(body, out_shape=tuple((jax.ShapeDtypeStruct(p.shape, jnp.f...  85.8 us
    pallas_call x1, Pallas kernels, chan_gather(): pl.pallas_call(_chan_gather_kernel, out_shape=(jax.ShapeDtypeStruct(shape...  19.3 us
    ppermute x1, waiting for transfers between devices, shards(): lax.ppermute(jnp.concatenate([hidden[nrows - 4:], rows_cot[nrows - 2:]],...  16 us
    mul x1, other arithmetic, gelu_parts(): cdf = 0.5 * (1.0 + lax.erf(pre * 0.7071067811865476))  9.93 us
    ppermute x1, starting transfers between devices, shards(): lax.ppermute(jnp.concatenate([hidden[:4], rows_cot[:2]], axis=0), ROW_AXE...  8.98 us
    reduce_sum x1, other arithmetic, shards(): grad_b1 = jnp.sum(flat_act.astype(jnp.float32), axis=0)  7.19 us
    reduce_sum x2, other arithmetic, shards(): jnp.sum(padded[row_tap:row_tap + nrows, col_tap:col_tap + ncols] * grad_p...  6.52 us
    unnamed x26, local copies, waits for them, and re-layouts  6.18 us
  transfers between devices with their start and end apart: 2, of which 2 were waited for; matrix products, arithmetic and copies ran while one was open for 0% of the time, Pallas kernels for 0%

profile of v7, /device:TPU:8, one launch (start us, length us, event | category | flops | bytes accessed | tf_op | source)
XLA Modules:
  0.0 182.2 jit_solution(15123944766919757317)
XLA Ops:
  0.6 19.3 %shard_map.118 = (bf16[4,2,128,512]{3,2,1,0:T(8,128)(2,1)}, bf16[4,2,128,512]{3,2,1,0:T(8,128)(2,1)}) custom-call(bf16[2,128,512]{2,1,0:T(8,128)(2,1)} %first.1, bf16[2,128,512]{2,1,0:T(8,128)(2,1)} %refs_4_.1), custom_call_target="tpu_custom_call" | custom-call | tf_op jit(solution)/shard_map/pallas_call | solution.py:286
  20.0 3.4 %multiply_convert_fusion = (bf16[8,128,512]{2,1,0:T(8,128)(2,1)S(1)}, f32[8,128,512]{2,1,0:T(8,128)}) fusion(f32[512]{0:T(512)} %param.10, bf16[8,128,512]{2,1,0:T(8,128)(2,1)} %bitcast.167, bf16[512,512]{1,0:T(8,128)(2,1)S(1)} %copy-done), kind=kOutput, calls=%fused_computation.177 | convolution fusion | flops 540016640 | bytes 4720640 | tf_op jit(solution)/shard_map/dot_general | solution.py:325
  23.4 1.2 copy-done.6
  24.6 0.1 pad_maximum_fusion
  24.7 3.4 %collective-permute-start = (bf16[6,128,512]{2,1,0:T(8,128)(2,1)S(1)}, bf16[6,128,512]{2,1,0:T(8,128)(2,1)S(1)}, u32[]{:S(2)}, u32[]{:S(2)}) collective-permute-start(bf16[6,128,512]{2,1,0:T(8,128)(2,1)S(1)} %pad_maximum_fusion), channel_id=1, source_target_pairs={{0,4},{4,8},{8,12},{12,16},{16,20},{20,24},{24,28},{28,32},{32,36}... | collective-permute-start | bytes 2359304 | tf_op jit(solution)/shard_map/ppermute | solution.py:337
  28.1 0.1 pad_maximum_fusion.1
  28.2 9.0 %collective-permute-start.1 = (bf16[6,128,512]{2,1,0:T(8,128)(2,1)S(1)}, bf16[6,128,512]{2,1,0:T(8,128)(2,1)S(1)}, u32[]{:S(2)}, u32[]{:S(2)}) collective-permute-start(bf16[6,128,512]{2,1,0:T(8,128)(2,1)S(1)} %pad_maximum_fusion.1), channel_id=1, source_target_pairs={{4,0},{8,4},{12,8},{16,12},{20,16},{24,20},{28,24},{32,28},{36,32}... | collective-permute-start | bytes 2359304 | tf_op jit(solution)/shard_map/ppermute | solution.py:338
  37.3 16.0 %collective-permute-done = bf16[6,128,512]{2,1,0:T(8,128)(2,1)S(1)} collective-permute-done((bf16[6,128,512]{2,1,0:T(8,128)(2,1)S(1)}, bf16[6,128,512]{2,1,0:T(8,128)(2,1)S(1)}, u32[]{:S(2)}, u32[]{:S(2)}) %collective-permute-start) | collective-permute-done | bytes 786464 | tf_op jit(solution)/shard_map/ppermute | solution.py:337
  53.3 1.2 collective-permute-done.1
  54.5 0.9 copy-done.5
  55.4 0.8 fusion.37
  56.2 9.9 %add_multiply_fusion = (f32[12,128,512]{2,1,0:T(8,128)S(1)}, f32[12,128,512]{2,1,0:T(8,128)S(1)}) fusion(f32[16,132,512]{2,1,0:T(8,128)S(1)} %fusion.37, f32[512]{0:T(512)S(1)} %bitcast.96, f32[512]{0:T(512)S(1)} %bitcast.98, f32[512]{0:T(512)S(1)} %bitcast.102, f32[512]{0:T(512)S(1)} %bitcast.104, f32[512]{0:T(512)S(1)} %bitcast.106, f32[512]{0:T(512)S(1)} %bitcast.108, ...), kind=kLoop, calls=%fused_computation.87 | loop fusion | flops 41680896 | bytes 84987904 | tf_op jit(solution)/shard_map/mul | solution.py:313
  66.2 1.0 slice.513
  67.2 1.0 slice.515
  68.1 2.9 %fusion.6 = bf16[12,128,512]{2,1,0:T(8,128)(2,1)S(1)} fusion(f32[12,128,512]{2,1,0:T(8,128)S(1)} %get-tuple-element.46, f32[12,128,512]{2,1,0:T(8,128)S(1)} %get-tuple-element.47, bf16[2,128,512]{2,1,0:T(8,128)(2,1)S(1)} %slice.515, bf16[8,128,512]{2,1,0:T(8,128)(2,1)} %bitcast.86, bf16[2,128,512]{2,1,0:T(8,128)(2,1)S(1)} %slice.513, ...), kind=kOutput, calls=%fused_computation.35 | convolution fusion | flops 812384256 | bytes 9961472 | tf_op jit(solution)/shard_map/dot_general | solution.py:355
  71.1 4.1 %fusion.60 = (f32[512]{0:T(512)S(1)}, f32[512]{0:T(512)S(1)}, f32[512]{0:T(512)S(1)}, f32[512]{0:T(512)S(1)}, f32[512]{0:T(512)S(1)}, /*index=5*/f32[512]{0:T(51...) fusion(f32[16,132,512]{2,1,0:T(8,128)S(1)} %fusion.37, ...), kind=kLoop, calls=%fused_computation.116 | loop fusion | flops 17293312 | bytes 34635776 | tf_op jit(solution)/shard_map/reduce_sum | solution.py:367
  75.2 2.4 %fusion.68 = (f32[512]{0:T(512)S(1)}, f32[512]{0:T(512)S(1)}, f32[512]{0:T(512)S(1)}, f32[512]{0:T(512)S(1)}, f32[512]{0:T(512)S(1)}, /*index=5*/f32[512]{0:T(51...) fusion(f32[16,132,512]{2,1,0:T(8,128)S(1)} %fusion.37, bf16[12,128,512]{2,1,0:T(8,128)(2,1)S(1)} %fusion.6), kind=kLoop, calls=%fused_computation.124 | loop fusion | flops 10480640 | bytes 19943424 | tf_op jit(solution)/shard_map/reduce_sum | solution.py:367
  77.6 0.5 pad_convert_fusion
  78.1 1.3 fusion.69
  79.4 0.6 copy-done.2
  80.1 7.2 %convert_reduce_fusion.1 = (f32[512]{0:T(512)S(1)}, bf16[8,128,512]{2,1,0:T(8,128)(2,1)S(1)}) fusion(f32[8,128,512]{2,1,0:T(8,128)S(1)} %copy-done.2, f32[512]{0:T(512)S(1)} %copy-done.9, f32[12,132,512]{2,1,0:T(8,128)S(1)} %pad_convert_fusion, f32[512]{0:T(512)S(1)} %bitcast.97, f32[512]{0:T(512)S(1)} %bitcast.99, f32[512]{0:T(512)S(1)} %bitcast.103, ...), kind=kLoop, calls=%fused_computation.176 | loop fusion | flops 32505344 | bytes 55629824 | tf_op jit(solution)/shard_map/reduce_sum | solution.py:380
  87.3 2.1 %fusion.100 = f32[8,128,512]{2,1,0:T(8,128)} fusion(bf16[8,128,512]{2,1,0:T(8,128)(2,1)S(1)} %get-tuple-element.45, bf16[512,512]{1,0:T(8,128)(2,1)S(1)} %copy-done), kind=kOutput, calls=%fused_computation.188 | convolution fusion | flops 536870912 | bytes 3670016 | tf_op jit(solution)/shard_map/rwh,ch->rwc/dot_general | solution.py:382
  89.3 0.1 concatenate.19
  89.5 2.0 %fusion.112.refs_1_ = f32[512,512]{1,0:T(8,128)S(1)} fusion(bf16[1024,512]{1,0:T(8,128)(2,1)S(1)} %bitcast.85, bf16[1024,512]{1,0:T(8,128)(2,1)} %bitcast.87), kind=kOutput, calls=%fused_computation.200 | convolution fusion | flops 536870912 | bytes 3145728 | tf_op jit(solution)/shard_map/dot_general | solution.py:354
  91.6 0.7 fusion.111.refs_0_
  92.3 0.2 copy-done.1
  92.5 85.8 %shard_map.119 = (f32[512,512]{1,0:T(8,128)S(1)}, f32[512,512]{1,0:T(8,128)S(1)}, f32[32,512]{1,0:T(8,128)S(1)}, bf16[2,128,512]{2,1,0:T(8,128)(2,1)S(1)}) custom-call(f32[512,512]{1,0:T(8,128)S(1)} %fusion.111.refs_0_, f32[512,512]{1,0:T(8,128)S(1)} %fusion.112.refs_1_, f32[32,512]{1,0:T(8,128)S(1)} %pad.14.refs_2_, f32[4,2,128,512]{3,2,1,0:T(8,128)} %bitcast.83, ...), custom_call_target="tpu_custom_call" | custom-call | tf_op jit(solution)/shard_map/pallas_call | solution.py:218
  178.4 0.6 fusion.108
  178.9 0.7 copy.17
  179.6 1.0 copy.18
  180.6 0.6 copy.19
  181.2 1.0 copy.20
  (25 shorter events, 0.3 us)
Async XLA Ops:
  0.6 19.3 %copy-start = (bf16[512,512]{1,0:T(8,128)(2,1)S(1)}, bf16[512,512]{1,0:T(8,128)(2,1)}, u32[]{:S(2)}) copy-start(bf16[512,512]{1,0:T(8,128)(2,1)} %param.9) | copy-start | bytes 1572868
  23.4 1.2 copy-start.6
  24.6 12.6 %copy-start.7 = (f32[25,512]{1,0:T(8,128)S(1)}, f32[25,512]{1,0:T(8,128)}, u32[]{:S(2)}) copy-start(f32[25,512]{1,0:T(8,128)} %param.11) | copy-start | bytes 153604
  24.7 28.5 %collective-permute-start = (bf16[6,128,512]{2,1,0:T(8,128)(2,1)S(1)}, bf16[6,128,512]{2,1,0:T(8,128)(2,1)S(1)}, u32[]{:S(2)}, u32[]{:S(2)}) collective-permute-start(bf16[6,128,512]{2,1,0:T(8,128)(2,1)S(1)} %pad_maximum_fusion), channel_id=1, source_target_pairs={{0,4},{4,8},{8,12},{12,16},{16,20},{20,24},{24,28},{28,32},{32,36}... | collective-permute-start | bytes 2359304 | tf_op jit(solution)/shard_map/ppermute | solution.py:337
  28.2 26.3 %collective-permute-start.1 = (bf16[6,128,512]{2,1,0:T(8,128)(2,1)S(1)}, bf16[6,128,512]{2,1,0:T(8,128)(2,1)S(1)}, u32[]{:S(2)}, u32[]{:S(2)}) collective-permute-start(bf16[6,128,512]{2,1,0:T(8,128)(2,1)S(1)} %pad_maximum_fusion.1), channel_id=1, source_target_pairs={{4,0},{8,4},{12,8},{16,12},{20,16},{24,20},{28,24},{32,28},{36,32}... | collective-permute-start | bytes 2359304 | tf_op jit(solution)/shard_map/ppermute | solution.py:338
  53.2 1.3 copy-start.4
  54.5 0.9 copy-start.5
  55.4 0.8 copy-start.8
  78.1 2.0 %copy-start.2 = (f32[8,128,512]{2,1,0:T(8,128)S(1)}, f32[8,128,512]{2,1,0:T(8,128)}, u32[]{:S(2)}) copy-start(f32[8,128,512]{2,1,0:T(8,128)} %get-tuple-element.87) | copy-start | bytes 6291460
  78.1 2.0 %copy-start.9 = (f32[512]{0:T(512)S(1)}, f32[512]{0:T(512)}, u32[]{:S(2)}) copy-start(f32[512]{0:T(512)} %param.10) | copy-start | bytes 6148
  87.2 2.3 %copy-start.3 = (bf16[8,128,512]{2,1,0:T(8,128)(2,1)S(1)}, bf16[8,128,512]{2,1,0:T(8,128)(2,1)}, u32[]{:S(2)}) copy-start(bf16[8,128,512]{2,1,0:T(8,128)(2,1)} %fusion.69) | copy-start | bytes 3145732
  89.5 2.1 %copy-start.10 = (bf16[4,2,128,512]{3,2,1,0:T(8,128)(2,1)S(1)}, bf16[4,2,128,512]{3,2,1,0:T(8,128)(2,1)}, u32[]{:S(2)}) copy-start(bf16[4,2,128,512]{3,2,1,0:T(8,128)(2,1)} %get-tuple-element.12) | copy-start | bytes 3145732
  91.6 1.0 copy-start.1

commit v8 on v5

--- a/solution.py
+++ b/solution.py
@@ -191,14 +191,14 @@
             pltpu.SemaphoreType.DMA((2 * nz,)), pltpu.SemaphoreType.DMA((2 * nz,)),
             pltpu.SemaphoreType.DMA((2 * nx,)), pltpu.SemaphoreType.DMA((2 * nx,)),
             pltpu.SemaphoreType.DMA((2, 3)), pltpu.SemaphoreType.DMA((4,)),
-            pltpu.SemaphoreType.DMA((2 * count,))]
+            pltpu.SemaphoreType.DMA((2 * count + 1,))]
     block = part.shape[1:]
 
     def body(*refs):
         ins, outs = refs[:count], refs[count + 2 : 2 * count + 2]
         part, cot, grad_out = refs[count], refs[count + 1], refs[2 * count + 2]
-        data, out, xs, zs, ys, fin, from_pair, from_far, relay = refs[2 * count + 3 : 2 * count + 12]
-        s = refs[2 * count + 12 :]
+        data, out, xs, zs, ys, fin, from_pair, from_far, relay, staged = refs[2 * count + 3 : 2 * count + 13]
+        s = refs[2 * count + 13 :]
         moves = s[-1]
         packs = [pltpu.make_async_copy(ref, data.at[pl.ds(at, size)], moves.at[i])
                  for i, (ref, (at, size)) in enumerate(zip(ins, layout))]
@@ -207,9 +207,10 @@
         data[used:] = jnp.zeros((rows - used, cols), jnp.float32)
         for c in packs:
             c.wait()
-        _sum_kernel(nx, nz, data, part, cot, out, grad_out, xs, zs, ys, fin, from_pair, from_far, relay, s[:-1])
+        _sum_kernel(nx, nz, data, part, cot, out, staged, xs, zs, ys, fin, from_pair, from_far, relay, s[:-1])
         unpacks = [pltpu.make_async_copy(out.at[pl.ds(at, size)], ref, moves.at[count + i])
                    for i, (ref, (at, size)) in enumerate(zip(outs, layout))]
+        unpacks.append(pltpu.make_async_copy(staged, grad_out, moves.at[2 * count]))
         for c in unpacks:
             c.start()
         for c in unpacks:
@@ -220,7 +221,8 @@
         out_shape=tuple(jax.ShapeDtypeStruct(p.shape, jnp.float32) for p in pieces)
         + (jax.ShapeDtypeStruct(cot.shape, cot.dtype),),
         in_specs=[pl.BlockSpec(memory_space=pltpu.VMEM)] * (count + 2),
-        out_specs=(pl.BlockSpec(memory_space=pltpu.VMEM),) * (count + 1),
+        out_specs=tuple(pl.BlockSpec(memory_space=pl.ANY if p.shape[0] >= 256 else pltpu.VMEM) for p in pieces)
+        + (pl.BlockSpec(memory_space=pl.ANY),),
         scratch_shapes=[
             pltpu.VMEM((rows, cols), jnp.float32),
             pltpu.VMEM((rows, cols), jnp.float32),
@@ -231,6 +233,7 @@
             pltpu.VMEM((2,) + block, jnp.float32),
             pltpu.VMEM(block, jnp.float32),
             pltpu.VMEM(block, jnp.float32),
+            pltpu.VMEM(cot.shape, cot.dtype),
         ] + sems,
         compiler_params=pltpu.CompilerParams(collective_id=0, has_side_effects=True,
                                              vmem_limit_bytes=48 * 1024 * 1024),

time: 168 us -> 168 us (level)
  no operation moved by 1% of the time
where the time goes in v8:
time: 168 us; the launch traced here: 166 us
  Pallas kernels  98.7 us (59%)
  starting transfers between devices  23 us (14%)
  other arithmetic  19.7 us (12%)
  waiting for transfers between devices  10.5 us (6%)
  matrix products  9.06 us (5%)
  local copies, waits for them, and re-layouts  4.23 us (3%)
    pallas_call x1, Pallas kernels, row_group_allreduce(): pl.pallas_call(body, out_shape=tuple((jax.ShapeDtypeStruct(p.shape, jnp.f...  79.4 us
    pallas_call x1, Pallas kernels, chan_gather(): pl.pallas_call(_chan_gather_kernel, out_shape=(jax.ShapeDtypeStruct(shape...  19.3 us
    ppermute x2, starting transfers between devices, extended(): lax.ppermute(lax.slice_in_dim(block, 0, width, axis=dim), axis, backward)  17.6 us
    ppermute x2, waiting for transfers between devices, extended(): lax.ppermute(lax.slice_in_dim(block, block.shape[dim] - width, None, axis...  8.16 us
    reduce_sum x1, other arithmetic, shards(): grad_b1 = jnp.sum(flat_act.astype(jnp.float32), axis=0)  7.26 us
    convert_element_type x1, other arithmetic, shards(): mixed = mixed.astype(jnp.bfloat16).reshape(nrows * ncols, hslice)  6.69 us
    ppermute x2, starting transfers between devices, extended(): lax.ppermute(lax.slice_in_dim(block, block.shape[dim] - width, None, axis...  5.34 us
    reduce_sum x1, other arithmetic, shards(): jnp.sum(padded[row_tap:row_tap + nrows, col_tap:col_tap + ncols] * grad_p...  4.67 us
  transfers between devices with their start and end apart: 4, of which 4 were waited for; matrix products, arithmetic and copies ran while one was open for 0% of the time, Pallas kernels for 0%

profile of v8, /device:TPU:8, one launch (start us, length us, event | category | flops | bytes accessed | tf_op | source)
XLA Modules:
  0.0 166.1 jit_solution(13075193427334897988)
XLA Ops:
  0.6 0.0 copy-start
  0.6 19.3 %shard_map.118 = (bf16[4,2,128,512]{3,2,1,0:T(8,128)(2,1)}, bf16[4,2,128,512]{3,2,1,0:T(8,128)(2,1)}) custom-call(bf16[2,128,512]{2,1,0:T(8,128)(2,1)} %first.1, bf16[2,128,512]{2,1,0:T(8,128)(2,1)} %refs_4_.1), custom_call_target="tpu_custom_call" | custom-call | tf_op jit(solution)/shard_map/pallas_call | solution.py:289
  20.0 0.0 copy-start.2
  20.0 2.1 %multiply_convert_fusion.1 = (bf16[8,128,512]{2,1,0:T(8,128)(2,1)S(1)}, f32[8,128,512]{2,1,0:T(8,128)S(1)}) fusion(f32[512]{0:T(512)} %param.10, bf16[8,128,512]{2,1,0:T(8,128)(2,1)} %bitcast.164, bf16[512,512]{1,0:T(8,128)(2,1)S(1)} %copy-done), kind=kOutput, calls=%fused_computation.121 | convolution fusion | flops 540016640 | bytes 4720640 | tf_op jit(solution)/shard_map/dot_general | solution.py:328
  22.2 3.4 %collective-permute-start = (bf16[2,128,512]{2,1,0:T(8,128)(2,1)S(1)}, bf16[2,128,512]{2,1,0:T(8,128)(2,1)S(1)}, u32[]{:S(2)}, u32[]{:S(2)}) collective-permute-start(bf16[2,128,512]{2,1,0:T(8,128)(2,1)S(1)} %get-tuple-element.50), channel_id=1, source_target_pairs={{0,4},{4,8},{8,12},{12,16},{16,20},{20,24},{24,28},{28,32},{32,36}... | collective-permute-start | bytes 786440 | tf_op jit(solution)/shard_map/ppermute | solution.py:307
  25.6 9.0 %collective-permute-start.1 = (bf16[2,128,512]{2,1,0:T(8,128)(2,1)S(1)}, bf16[2,128,512]{2,1,0:T(8,128)(2,1)S(1)}, u32[]{:S(2)}, u32[]{:S(2)}) collective-permute-start(bf16[2,128,512]{2,1,0:T(8,128)(2,1)S(1)} %get-tuple-element.51), channel_id=1, source_target_pairs={{4,0},{8,4},{12,8},{16,12},{20,16},{24,20},{28,24},{32,28},{36,32}... | collective-permute-start | bytes 786440 | tf_op jit(solution)/shard_map/ppermute | solution.py:310
  34.7 0.0 copy-start.3
  34.7 4.8 %collective-permute-done = bf16[2,128,512]{2,1,0:T(8,128)(2,1)S(1)} collective-permute-done((bf16[2,128,512]{2,1,0:T(8,128)(2,1)S(1)}, bf16[2,128,512]{2,1,0:T(8,128)(2,1)S(1)}, u32[]{:S(2)}, u32[]{:S(2)}) %collective-permute-start) | collective-permute-done | bytes 262176 | tf_op jit(solution)/shard_map/ppermute | solution.py:307
  39.5 1.2 collective-permute-done.1
  40.7 0.5 fusion.68
  41.2 0.0 copy-start.7
  41.3 6.7 %multiply_convert_fusion = (bf16[8,128,512]{2,1,0:T(8,128)(2,1)S(1)}, f32[8,128,512]{2,1,0:T(8,128)S(1)}) fusion(f32[12,132,512]{2,1,0:T(8,128)S(1)} %fusion.68, f32[512]{0:T(512)S(1)} %bitcast.93, f32[512]{0:T(512)S(1)} %bitcast.95, f32[512]{0:T(512)S(1)} %bitcast.99, f32[512]{0:T(512)S(1)} %bitcast.101, f32[512]{0:T(512)S(1)} %bitcast.103, ...), kind=kLoop, calls=%fused_computation.118 | loop fusion | flops 28835840 | bytes 55627776 | tf_op jit(solution)/shard_map/convert_element_type | solution.py:346
  48.0 3.4 %fusion.36 = (f32[512]{0:T(512)S(1)}, f32[512]{0:T(512)S(1)}, f32[512]{0:T(512)S(1)}, f32[512]{0:T(512)S(1)}, f32[512]{0:T(512)S(1)}, /*index=5*/f32[512]{0:T(51...) fusion(f32[12,132,512]{2,1,0:T(8,128)S(1)} %fusion.68, f32[8,128,512]{2,1,0:T(8,128)S(1)} %get-tuple-element.47, ...), kind=kOutput, calls=%fused_computation.66 | convolution fusion | flops 550498304 | bytes 19415040 | tf_op jit(solution)/shard_map/dot_general | solution.py:348
  51.4 4.7 %fusion.37 = (f32[512]{0:T(512)S(1)}, f32[512]{0:T(512)S(1)}, f32[512]{0:T(512)S(1)}, f32[512]{0:T(512)S(1)}, f32[512]{0:T(512)S(1)}, /*index=5*/f32[512]{0:T(51...) fusion(bf16[8,128,512]{2,1,0:T(8,128)(2,1)S(1)} %get-tuple-elem, ...), kind=kLoop, calls=%fused_computation.67 | loop fusion | flops 19389440 | bytes 38834176 | tf_op jit(solution)/shard_map/reduce_sum | solution.py:361
  56.1 1.9 %collective-permute-start.2 = (bf16[2,128,512]{2,1,0:T(8,128)(2,1)S(1)}, bf16[2,128,512]{2,1,0:T(8,128)(2,1)S(1)}, u32[]{:S(2)}, u32[]{:S(2)}) collective-permute-start(bf16[2,128,512]{2,1,0:T(8,128)(2,1)S(1)} %get-tuple-element.48), channel_id=1, source_target_pairs={{0,4},{4,8},{8,12},{12,16},{16,20},{20,24},{24,28},{28,32},{32,36}... | collective-permute-start | bytes 786440 | tf_op jit(solution)/shard_map/ppermute | solution.py:307
  58.0 8.6 %collective-permute-start.3 = (bf16[2,128,512]{2,1,0:T(8,128)(2,1)S(1)}, bf16[2,128,512]{2,1,0:T(8,128)(2,1)S(1)}, u32[]{:S(2)}, u32[]{:S(2)}) collective-permute-start(bf16[2,128,512]{2,1,0:T(8,128)(2,1)S(1)} %get-tuple-element.49), channel_id=1, source_target_pairs={{4,0},{8,4},{12,8},{16,12},{20,16},{24,20},{28,24},{32,28},{36,32}... | collective-permute-start | bytes 786440 | tf_op jit(solution)/shard_map/ppermute | solution.py:310
  66.6 0.7 fusion.81.refs_1_
  67.4 0.0 copy-start.4
  67.4 3.4 %collective-permute-done.2 = bf16[2,128,512]{2,1,0:T(8,128)(2,1)S(1)} collective-permute-done((bf16[2,128,512]{2,1,0:T(8,128)(2,1)S(1)}, bf16[2,128,512]{2,1,0:T(8,128)(2,1)S(1)}, u32[]{:S(2)}, u32[]{:S(2)}) %collective-permute-start.2) | collective-permute-done | bytes 262176 | tf_op jit(solution)/shard_map/ppermute | solution.py:307
  70.8 1.2 collective-permute-done.3
  71.9 0.5 fusion.62
  72.5 7.3 %convert_reduce_fusion.1 = (f32[512]{0:T(512)S(1)}, bf16[8,128,512]{2,1,0:T(8,128)(2,1)S(1)}) fusion(f32[8,128,512]{2,1,0:T(8,128)S(1)} %get-tuple-element.80, f32[512]{0:T(512)S(1)} %copy-done.4, f32[12,132,512]{2,1,0:T(8,128)S(1)} %fusion.62, f32[512]{0:T(512)S(1)} %bitcast.94, f32[512]{0:T(512)S(1)} %bitcast.96, f32[512]{0:T(512)S(1)} %bitcast.100, ...), kind=kLoop, calls=%fused_computation.117 | loop fusion | flops 32505344 | bytes 55629824 | tf_op jit(solution)/shard_map/reduce_sum | solution.py:374
  79.7 2.1 %fusion.69 = f32[8,128,512]{2,1,0:T(8,128)} fusion(bf16[8,128,512]{2,1,0:T(8,128)(2,1)S(1)} %get-tuple-element.45, bf16[512,512]{1,0:T(8,128)(2,1)S(1)} %copy-done), kind=kOutput, calls=%fused_computation.132 | convolution fusion | flops 536870912 | bytes 3670016 | tf_op jit(solution)/shard_map/rwh,ch->rwc/dot_general | solution.py:376
  81.8 0.7 fusion.80.refs_0_
  82.6 0.1 concatenate.11
  82.7 0.1 copy-done.1
  82.8 79.4 %shard_map.119 = (f32[512,512]{1,0:T(8,128)S(1)}, f32[512,512]{1,0:T(8,128)S(1)}, f32[32,512]{1,0:T(8,128)S(1)}, bf16[2,128,512]{2,1,0:T(8,128)(2,1)S(1)}) custom-call(f32[512,512]{1,0:T(8,128)S(1)} %fusion.80.refs_0_, f32[512,512]{1,0:T(8,128)S(1)} %fusion.81.refs_1_, f32[32,512]{1,0:T(8,128)S(1)} %pad.13.refs_2_, f32[4,2,128,512]{3,2,1,0:T(8,128)} %bitcast.82, ...), custom_call_target="tpu_custom_call" | custom-call | tf_op jit(solution)/shard_map/pallas_call | solution.py:219
  162.2 0.6 fusion.77
  162.8 0.7 copy.17
  163.5 1.0 copy.18
  164.5 0.6 copy.19
  165.1 1.0 copy.20
  (15 shorter events, 0.1 us)
Async XLA Ops:
  0.6 19.4 %copy-start = (bf16[512,512]{1,0:T(8,128)(2,1)S(1)}, bf16[512,512]{1,0:T(8,128)(2,1)}, u32[]{:S(2)}) copy-start(bf16[512,512]{1,0:T(8,128)(2,1)} %param.9) | copy-start | bytes 1572868
  20.0 14.6 %copy-start.2 = (f32[25,512]{1,0:T(8,128)S(1)}, f32[25,512]{1,0:T(8,128)}, u32[]{:S(2)}) copy-start(f32[25,512]{1,0:T(8,128)} %param.11) | copy-start | bytes 153604
  22.2 17.3 %collective-permute-start = (bf16[2,128,512]{2,1,0:T(8,128)(2,1)S(1)}, bf16[2,128,512]{2,1,0:T(8,128)(2,1)S(1)}, u32[]{:S(2)}, u32[]{:S(2)}) collective-permute-start(bf16[2,128,512]{2,1,0:T(8,128)(2,1)S(1)} %get-tuple-element.50), channel_id=1, source_target_pairs={{0,4},{4,8},{8,12},{12,16},{16,20},{20,24},{24,28},{28,32},{32,36}... | collective-permute-start | bytes 786440 | tf_op jit(solution)/shard_map/ppermute | solution.py:307
  25.6 15.1 %collective-permute-start.1 = (bf16[2,128,512]{2,1,0:T(8,128)(2,1)S(1)}, bf16[2,128,512]{2,1,0:T(8,128)(2,1)S(1)}, u32[]{:S(2)}, u32[]{:S(2)}) collective-permute-start(bf16[2,128,512]{2,1,0:T(8,128)(2,1)S(1)} %get-tuple-element.51), channel_id=1, source_target_pairs={{4,0},{8,4},{12,8},{16,12},{20,16},{24,20},{28,24},{32,28},{36,32}... | collective-permute-start | bytes 786440 | tf_op jit(solution)/shard_map/ppermute | solution.py:310
  34.7 6.5 %copy-start.3 = (f32[512]{0:T(512)S(1)}, f32[512]{0:T(512)}, u32[]{:S(2)}) copy-start(f32[512]{0:T(512)} %param.12) | copy-start | bytes 6148
  41.2 6.7 %copy-start.6 = (bf16[4,2,128,512]{3,2,1,0:T(8,128)(2,1)S(1)}, bf16[4,2,128,512]{3,2,1,0:T(8,128)(2,1)}, u32[]{:S(2)}) copy-start(bf16[4,2,128,512]{3,2,1,0:T(8,128)(2,1)} %get-tuple-element.13) | copy-start | bytes 3145732
  41.2 6.7 %copy-start.7 = (bf16[512,512]{1,0:T(8,128)(2,1)S(1)}, bf16[512,512]{1,0:T(8,128)(2,1)}, u32[]{:S(2)}) copy-start(bf16[512,512]{1,0:T(8,128)(2,1)} %param.13) | copy-start | bytes 1572868
  56.1 14.7 %collective-permute-start.2 = (bf16[2,128,512]{2,1,0:T(8,128)(2,1)S(1)}, bf16[2,128,512]{2,1,0:T(8,128)(2,1)S(1)}, u32[]{:S(2)}, u32[]{:S(2)}) collective-permute-start(bf16[2,128,512]{2,1,0:T(8,128)(2,1)S(1)} %get-tuple-element.48), channel_id=1, source_target_pairs={{0,4},{4,8},{8,12},{12,16},{16,20},{20,24},{24,28},{28,32},{32,36}... | collective-permute-start | bytes 786440 | tf_op jit(solution)/shard_map/ppermute | solution.py:307
  58.0 13.9 %collective-permute-start.3 = (bf16[2,128,512]{2,1,0:T(8,128)(2,1)S(1)}, bf16[2,128,512]{2,1,0:T(8,128)(2,1)S(1)}, u32[]{:S(2)}, u32[]{:S(2)}) collective-permute-start(bf16[2,128,512]{2,1,0:T(8,128)(2,1)S(1)} %get-tuple-element.49), channel_id=1, source_target_pairs={{4,0},{8,4},{12,8},{16,12},{20,16},{24,20},{28,24},{32,28},{36,32}... | collective-permute-start | bytes 786440 | tf_op jit(solution)/shard_map/ppermute | solution.py:310
  67.4 5.1 %copy-start.4 = (f32[512]{0:T(512)S(1)}, f32[512]{0:T(512)}, u32[]{:S(2)}) copy-start(f32[512]{0:T(512)} %param.10) | copy-start | bytes 6148
  79.7 2.1 %copy-start.5 = (bf16[4,2,128,512]{3,2,1,0:T(8,128)(2,1)S(1)}, bf16[4,2,128,512]{3,2,1,0:T(8,128)(2,1)}, u32[]{:S(2)}) copy-start(bf16[4,2,128,512]{3,2,1,0:T(8,128)(2,1)} %get-tuple-element.12) | copy-start | bytes 3145732
  81.8 1.0 copy-start.1

commit v9 on v5

--- a/solution.py
+++ b/solution.py
@@ -76,6 +76,7 @@
     def obig(h, kx):
         return xblock(h, kx)
 
+    pending = []
     for s in range(nx - 1):
         copies = []
         for h in range(2):
@@ -91,7 +92,7 @@
             copies[h].wait_recv()
             r, c = xblock(h, ix - sg * (s + 2))
             xs[h, s] = xs[h, s] + data[r, c]
-            copies[h].wait_send()
+        pending.extend(copies)
     last = nx - 2
     for c in chan_one:
         c.wait_recv()
@@ -121,8 +122,7 @@
         for d in range(1, nz):
             acc = acc + zs[h, d - 1]
         zs[h, nz] = acc
-    for c in copies:
-        c.wait_send()
+    pending.extend(copies)
     zl = nz
     c = pltpu.make_async_remote_copy(
         src_ref=zs.at[:, zl], dst_ref=ys, send_sem=ysend.at[0], recv_sem=yrecv.at[0],
@@ -136,7 +136,7 @@
         p.start()
     for p in placed:
         p.wait()
-    c.wait_send()
+    pending.append(c)
     copies = []
     for h in range(2):
         loc = oblock(h, ix, iz)
@@ -148,8 +148,7 @@
             copies.append(c)
     for c in copies:
         c.wait_recv()
-    for c in copies:
-        c.wait_send()
+    pending.extend(copies)
     for s in range(nx - 1):
         copies = []
         for h in range(2):
@@ -162,14 +161,13 @@
             copies.append(c)
         for h in range(2):
             copies[h].wait_recv()
-            copies[h].wait_send()
+        pending.extend(copies)
 
     chan_two.wait_recv()
     total = part[me] + from_pair[0] + from_far[...]
     grad_out[...] = (cot[...].astype(jnp.float32) + total).astype(grad_out.dtype)
-    for c in chan_one:
+    for c in chan_one + [chan_two] + pending:
         c.wait_send()
-    chan_two.wait_send()
 
 def row_group_allreduce(pieces, nx, nz, part, cot):
     cols = pieces[0].shape[-1]

time: 168 us -> 171 us (1.018)
  Pallas kernels: 98.7 us -> 103 us
    pallas_call x1, Pallas kernels: 79.4 us -> 83.2 us  [row_group_allreduce(): pl.pallas_call(body, out_shape=tuple((jax.ShapeDtypeStruct(p.shape, jnp.f...]
where the time goes in v9:
time: 171 us; the launch traced here: 170 us
  Pallas kernels  103 us (60%)
  starting transfers between devices  23 us (13%)
  other arithmetic  19.7 us (12%)
  waiting for transfers between devices  10.5 us (6%)
  matrix products  9.06 us (5%)
  local copies, waits for them, and re-layouts  4.23 us (2%)
    pallas_call x1, Pallas kernels, row_group_allreduce(): pl.pallas_call(body, out_shape=tuple((jax.ShapeDtypeStruct(p.shape, jnp.f...  83.2 us
    pallas_call x1, Pallas kernels, chan_gather(): pl.pallas_call(_chan_gather_kernel, out_shape=(jax.ShapeDtypeStruct(shape...  19.3 us
    ppermute x2, starting transfers between devices, extended(): lax.ppermute(lax.slice_in_dim(block, 0, width, axis=dim), axis, backward)  17.6 us
    ppermute x2, waiting for transfers between devices, extended(): lax.ppermute(lax.slice_in_dim(block, block.shape[dim] - width, None, axis...  8.16 us
    reduce_sum x1, other arithmetic, shards(): grad_b1 = jnp.sum(flat_act.astype(jnp.float32), axis=0)  7.26 us
    convert_element_type x1, other arithmetic, shards(): mixed = mixed.astype(jnp.bfloat16).reshape(nrows * ncols, hslice)  6.69 us
    ppermute x2, starting transfers between devices, extended(): lax.ppermute(lax.slice_in_dim(block, block.shape[dim] - width, None, axis...  5.34 us
    reduce_sum x1, other arithmetic, shards(): jnp.sum(padded[row_tap:row_tap + nrows, col_tap:col_tap + ncols] * grad_p...  4.67 us
  transfers between devices with their start and end apart: 4, of which 4 were waited for; matrix products, arithmetic and copies ran while one was open for 0% of the time, Pallas kernels for 0%

profile of v9, /device:TPU:8, one launch (start us, length us, event | category | flops | bytes accessed | tf_op | source)
XLA Modules:
  0.0 169.9 jit_solution(14769978687548621225)
XLA Ops:
  0.6 0.0 copy-start
  0.6 19.3 %shard_map.118 = (bf16[4,2,128,512]{3,2,1,0:T(8,128)(2,1)}, bf16[4,2,128,512]{3,2,1,0:T(8,128)(2,1)}) custom-call(bf16[2,128,512]{2,1,0:T(8,128)(2,1)} %first.1, bf16[2,128,512]{2,1,0:T(8,128)(2,1)} %refs_4_.1), custom_call_target="tpu_custom_call" | custom-call | tf_op jit(solution)/shard_map/pallas_call | solution.py:284
  20.0 0.0 copy-start.2
  20.0 2.1 %multiply_convert_fusion.1 = (bf16[8,128,512]{2,1,0:T(8,128)(2,1)S(1)}, f32[8,128,512]{2,1,0:T(8,128)S(1)}) fusion(f32[512]{0:T(512)} %param.10, bf16[8,128,512]{2,1,0:T(8,128)(2,1)} %bitcast.164, bf16[512,512]{1,0:T(8,128)(2,1)S(1)} %copy-done), kind=kOutput, calls=%fused_computation.121 | convolution fusion | flops 540016640 | bytes 4720640 | tf_op jit(solution)/shard_map/dot_general | solution.py:323
  22.2 3.4 %collective-permute-start = (bf16[2,128,512]{2,1,0:T(8,128)(2,1)S(1)}, bf16[2,128,512]{2,1,0:T(8,128)(2,1)S(1)}, u32[]{:S(2)}, u32[]{:S(2)}) collective-permute-start(bf16[2,128,512]{2,1,0:T(8,128)(2,1)S(1)} %get-tuple-element.50), channel_id=1, source_target_pairs={{0,4},{4,8},{8,12},{12,16},{16,20},{20,24},{24,28},{28,32},{32,36}... | collective-permute-start | bytes 786440 | tf_op jit(solution)/shard_map/ppermute | solution.py:302
  25.6 9.0 %collective-permute-start.1 = (bf16[2,128,512]{2,1,0:T(8,128)(2,1)S(1)}, bf16[2,128,512]{2,1,0:T(8,128)(2,1)S(1)}, u32[]{:S(2)}, u32[]{:S(2)}) collective-permute-start(bf16[2,128,512]{2,1,0:T(8,128)(2,1)S(1)} %get-tuple-element.51), channel_id=1, source_target_pairs={{4,0},{8,4},{12,8},{16,12},{20,16},{24,20},{28,24},{32,28},{36,32}... | collective-permute-start | bytes 786440 | tf_op jit(solution)/shard_map/ppermute | solution.py:305
  34.7 0.0 copy-start.3
  34.7 4.8 %collective-permute-done = bf16[2,128,512]{2,1,0:T(8,128)(2,1)S(1)} collective-permute-done((bf16[2,128,512]{2,1,0:T(8,128)(2,1)S(1)}, bf16[2,128,512]{2,1,0:T(8,128)(2,1)S(1)}, u32[]{:S(2)}, u32[]{:S(2)}) %collective-permute-start) | collective-permute-done | bytes 262176 | tf_op jit(solution)/shard_map/ppermute | solution.py:302
  39.5 1.2 collective-permute-done.1
  40.7 0.5 fusion.68
  41.2 0.0 copy-start.7
  41.3 6.7 %multiply_convert_fusion = (bf16[8,128,512]{2,1,0:T(8,128)(2,1)S(1)}, f32[8,128,512]{2,1,0:T(8,128)S(1)}) fusion(f32[12,132,512]{2,1,0:T(8,128)S(1)} %fusion.68, f32[512]{0:T(512)S(1)} %bitcast.93, f32[512]{0:T(512)S(1)} %bitcast.95, f32[512]{0:T(512)S(1)} %bitcast.99, f32[512]{0:T(512)S(1)} %bitcast.101, f32[512]{0:T(512)S(1)} %bitcast.103, ...), kind=kLoop, calls=%fused_computation.118 | loop fusion | flops 28835840 | bytes 55627776 | tf_op jit(solution)/shard_map/convert_element_type | solution.py:341
  48.0 3.4 %fusion.36 = (f32[512]{0:T(512)S(1)}, f32[512]{0:T(512)S(1)}, f32[512]{0:T(512)S(1)}, f32[512]{0:T(512)S(1)}, f32[512]{0:T(512)S(1)}, /*index=5*/f32[512]{0:T(51...) fusion(f32[12,132,512]{2,1,0:T(8,128)S(1)} %fusion.68, f32[8,128,512]{2,1,0:T(8,128)S(1)} %get-tuple-element.47, ...), kind=kOutput, calls=%fused_computation.66 | convolution fusion | flops 550498304 | bytes 19415040 | tf_op jit(solution)/shard_map/dot_general | solution.py:343
  51.4 4.7 %fusion.37 = (f32[512]{0:T(512)S(1)}, f32[512]{0:T(512)S(1)}, f32[512]{0:T(512)S(1)}, f32[512]{0:T(512)S(1)}, f32[512]{0:T(512)S(1)}, /*index=5*/f32[512]{0:T(51...) fusion(bf16[8,128,512]{2,1,0:T(8,128)(2,1)S(1)} %get-tuple-elem, ...), kind=kLoop, calls=%fused_computation.67 | loop fusion | flops 19389440 | bytes 38834176 | tf_op jit(solution)/shard_map/reduce_sum | solution.py:356
  56.1 1.9 %collective-permute-start.2 = (bf16[2,128,512]{2,1,0:T(8,128)(2,1)S(1)}, bf16[2,128,512]{2,1,0:T(8,128)(2,1)S(1)}, u32[]{:S(2)}, u32[]{:S(2)}) collective-permute-start(bf16[2,128,512]{2,1,0:T(8,128)(2,1)S(1)} %get-tuple-element.48), channel_id=1, source_target_pairs={{0,4},{4,8},{8,12},{12,16},{16,20},{20,24},{24,28},{28,32},{32,36}... | collective-permute-start | bytes 786440 | tf_op jit(solution)/shard_map/ppermute | solution.py:302
  58.0 8.6 %collective-permute-start.3 = (bf16[2,128,512]{2,1,0:T(8,128)(2,1)S(1)}, bf16[2,128,512]{2,1,0:T(8,128)(2,1)S(1)}, u32[]{:S(2)}, u32[]{:S(2)}) collective-permute-start(bf16[2,128,512]{2,1,0:T(8,128)(2,1)S(1)} %get-tuple-element.49), channel_id=1, source_target_pairs={{4,0},{8,4},{12,8},{16,12},{20,16},{24,20},{28,24},{32,28},{36,32}... | collective-permute-start | bytes 786440 | tf_op jit(solution)/shard_map/ppermute | solution.py:305
  66.6 0.7 fusion.81.refs_1_
  67.4 0.0 copy-start.4
  67.4 3.4 %collective-permute-done.2 = bf16[2,128,512]{2,1,0:T(8,128)(2,1)S(1)} collective-permute-done((bf16[2,128,512]{2,1,0:T(8,128)(2,1)S(1)}, bf16[2,128,512]{2,1,0:T(8,128)(2,1)S(1)}, u32[]{:S(2)}, u32[]{:S(2)}) %collective-permute-start.2) | collective-permute-done | bytes 262176 | tf_op jit(solution)/shard_map/ppermute | solution.py:302
  70.8 1.2 collective-permute-done.3
  71.9 0.5 fusion.62
  72.5 7.3 %convert_reduce_fusion.1 = (f32[512]{0:T(512)S(1)}, bf16[8,128,512]{2,1,0:T(8,128)(2,1)S(1)}) fusion(f32[8,128,512]{2,1,0:T(8,128)S(1)} %get-tuple-element.80, f32[512]{0:T(512)S(1)} %copy-done.4, f32[12,132,512]{2,1,0:T(8,128)S(1)} %fusion.62, f32[512]{0:T(512)S(1)} %bitcast.94, f32[512]{0:T(512)S(1)} %bitcast.96, f32[512]{0:T(512)S(1)} %bitcast.100, ...), kind=kLoop, calls=%fused_computation.117 | loop fusion | flops 32505344 | bytes 55629824 | tf_op jit(solution)/shard_map/reduce_sum | solution.py:369
  79.7 2.1 %fusion.69 = f32[8,128,512]{2,1,0:T(8,128)} fusion(bf16[8,128,512]{2,1,0:T(8,128)(2,1)S(1)} %get-tuple-element.45, bf16[512,512]{1,0:T(8,128)(2,1)S(1)} %copy-done), kind=kOutput, calls=%fused_computation.132 | convolution fusion | flops 536870912 | bytes 3670016 | tf_op jit(solution)/shard_map/rwh,ch->rwc/dot_general | solution.py:371
  81.8 0.7 fusion.80.refs_0_
  82.6 0.1 concatenate.11
  82.7 0.1 copy-done.1
  82.8 83.2 %shard_map.119 = (f32[512,512]{1,0:T(8,128)S(1)}, f32[512,512]{1,0:T(8,128)S(1)}, f32[32,512]{1,0:T(8,128)S(1)}, bf16[2,128,512]{2,1,0:T(8,128)(2,1)S(1)}) custom-call(f32[512,512]{1,0:T(8,128)S(1)} %fusion.80.refs_0_, f32[512,512]{1,0:T(8,128)S(1)} %fusion.81.refs_1_, f32[32,512]{1,0:T(8,128)S(1)} %pad.13.refs_2_, f32[4,2,128,512]{3,2,1,0:T(8,128)} %bitcast.82, ...), custom_call_target="tpu_custom_call" | custom-call | tf_op jit(solution)/shard_map/pallas_call | solution.py:216
  166.0 0.6 fusion.77
  166.6 0.7 copy.17
  167.3 1.0 copy.18
  168.3 0.6 copy.19
  168.9 1.0 copy.20
  (15 shorter events, 0.1 us)
Async XLA Ops:
  0.6 19.4 %copy-start = (bf16[512,512]{1,0:T(8,128)(2,1)S(1)}, bf16[512,512]{1,0:T(8,128)(2,1)}, u32[]{:S(2)}) copy-start(bf16[512,512]{1,0:T(8,128)(2,1)} %param.9) | copy-start | bytes 1572868
  20.0 14.6 %copy-start.2 = (f32[25,512]{1,0:T(8,128)S(1)}, f32[25,512]{1,0:T(8,128)}, u32[]{:S(2)}) copy-start(f32[25,512]{1,0:T(8,128)} %param.11) | copy-start | bytes 153604
  22.2 17.3 %collective-permute-start = (bf16[2,128,512]{2,1,0:T(8,128)(2,1)S(1)}, bf16[2,128,512]{2,1,0:T(8,128)(2,1)S(1)}, u32[]{:S(2)}, u32[]{:S(2)}) collective-permute-start(bf16[2,128,512]{2,1,0:T(8,128)(2,1)S(1)} %get-tuple-element.50), channel_id=1, source_target_pairs={{0,4},{4,8},{8,12},{12,16},{16,20},{20,24},{24,28},{28,32},{32,36}... | collective-permute-start | bytes 786440 | tf_op jit(solution)/shard_map/ppermute | solution.py:302
  25.6 15.1 %collective-permute-start.1 = (bf16[2,128,512]{2,1,0:T(8,128)(2,1)S(1)}, bf16[2,128,512]{2,1,0:T(8,128)(2,1)S(1)}, u32[]{:S(2)}, u32[]{:S(2)}) collective-permute-start(bf16[2,128,512]{2,1,0:T(8,128)(2,1)S(1)} %get-tuple-element.51), channel_id=1, source_target_pairs={{4,0},{8,4},{12,8},{16,12},{20,16},{24,20},{28,24},{32,28},{36,32}... | collective-permute-start | bytes 786440 | tf_op jit(solution)/shard_map/ppermute | solution.py:305
  34.7 6.5 %copy-start.3 = (f32[512]{0:T(512)S(1)}, f32[512]{0:T(512)}, u32[]{:S(2)}) copy-start(f32[512]{0:T(512)} %param.12) | copy-start | bytes 6148
  41.2 6.7 %copy-start.6 = (bf16[4,2,128,512]{3,2,1,0:T(8,128)(2,1)S(1)}, bf16[4,2,128,512]{3,2,1,0:T(8,128)(2,1)}, u32[]{:S(2)}) copy-start(bf16[4,2,128,512]{3,2,1,0:T(8,128)(2,1)} %get-tuple-element.13) | copy-start | bytes 3145732
  41.2 6.7 %copy-start.7 = (bf16[512,512]{1,0:T(8,128)(2,1)S(1)}, bf16[512,512]{1,0:T(8,128)(2,1)}, u32[]{:S(2)}) copy-start(bf16[512,512]{1,0:T(8,128)(2,1)} %param.13) | copy-start | bytes 1572868
  56.1 14.7 %collective-permute-start.2 = (bf16[2,128,512]{2,1,0:T(8,128)(2,1)S(1)}, bf16[2,128,512]{2,1,0:T(8,128)(2,1)S(1)}, u32[]{:S(2)}, u32[]{:S(2)}) collective-permute-start(bf16[2,128,512]{2,1,0:T(8,128)(2,1)S(1)} %get-tuple-element.48), channel_id=1, source_target_pairs={{0,4},{4,8},{8,12},{12,16},{16,20},{20,24},{24,28},{28,32},{32,36}... | collective-permute-start | bytes 786440 | tf_op jit(solution)/shard_map/ppermute | solution.py:302
  58.0 13.9 %collective-permute-start.3 = (bf16[2,128,512]{2,1,0:T(8,128)(2,1)S(1)}, bf16[2,128,512]{2,1,0:T(8,128)(2,1)S(1)}, u32[]{:S(2)}, u32[]{:S(2)}) collective-permute-start(bf16[2,128,512]{2,1,0:T(8,128)(2,1)S(1)} %get-tuple-element.49), channel_id=1, source_target_pairs={{4,0},{8,4},{12,8},{16,12},{20,16},{24,20},{28,24},{32,28},{36,32}... | collective-permute-start | bytes 786440 | tf_op jit(solution)/shard_map/ppermute | solution.py:305
  67.4 5.1 %copy-start.4 = (f32[512]{0:T(512)S(1)}, f32[512]{0:T(512)}, u32[]{:S(2)}) copy-start(f32[512]{0:T(512)} %param.10) | copy-start | bytes 6148
  79.7 2.1 %copy-start.5 = (bf16[4,2,128,512]{3,2,1,0:T(8,128)(2,1)S(1)}, bf16[4,2,128,512]{3,2,1,0:T(8,128)(2,1)}, u32[]{:S(2)}) copy-start(bf16[4,2,128,512]{3,2,1,0:T(8,128)(2,1)} %get-tuple-element.12) | copy-start | bytes 3145732
  81.8 1.0 copy-start.1

commit v10 on v5

--- a/solution.py
+++ b/solution.py
@@ -266,15 +266,16 @@
             step_one.append(c)
     for k in range(2):
         outs[k][me] = sources[k][...]
-    for c in step_one:
-        c.wait_recv()
     relay = []
     for k in range(2):
+        step_one[2 * k + 1].wait_recv()
         c = pltpu.make_async_remote_copy(
             src_ref=outs[k].at[over], dst_ref=outs[k].at[over], send_sem=sems.at[0, k, 2],
             recv_sem=sems.at[1, k, 2], device_id=pair, device_id_type=MESH_ID)
         c.start()
         relay.append(c)
+    for k in range(2):
+        step_one[2 * k].wait_recv()
     for c in relay:
         c.wait_recv()
     for c in step_one + relay:

time: 168 us -> 167 us (level)
  no operation moved by 1% of the time
where the time goes in v10:
time: 167 us; the launch traced here: 165 us
  Pallas kernels  97.4 us (58%)
  starting transfers between devices  22.9 us (14%)
  other arithmetic  19.6 us (12%)
  waiting for transfers between devices  10.5 us (6%)
  matrix products  9.12 us (5%)
  local copies, waits for them, and re-layouts  4.23 us (3%)
    pallas_call x1, Pallas kernels, row_group_allreduce(): pl.pallas_call(body, out_shape=tuple((jax.ShapeDtypeStruct(p.shape, jnp.f...  78.4 us
    pallas_call x1, Pallas kernels, chan_gather(): pl.pallas_call(_chan_gather_kernel, out_shape=(jax.ShapeDtypeStruct(shape...  19 us
    ppermute x2, starting transfers between devices, extended(): lax.ppermute(lax.slice_in_dim(block, 0, width, axis=dim), axis, backward)  17.5 us
    ppermute x2, waiting for transfers between devices, extended(): lax.ppermute(lax.slice_in_dim(block, block.shape[dim] - width, None, axis...  8.19 us
    reduce_sum x1, other arithmetic, shards(): grad_b1 = jnp.sum(flat_act.astype(jnp.float32), axis=0)  7.26 us
    convert_element_type x1, other arithmetic, shards(): mixed = mixed.astype(jnp.bfloat16).reshape(nrows * ncols, hslice)  6.69 us
    ppermute x2, starting transfers between devices, extended(): lax.ppermute(lax.slice_in_dim(block, block.shape[dim] - width, None, axis...  5.34 us
    reduce_sum x1, other arithmetic, shards(): jnp.sum(padded[row_tap:row_tap + nrows, col_tap:col_tap + ncols] * grad_p...  4.67 us
  transfers between devices with their start and end apart: 4, of which 4 were waited for; matrix products, arithmetic and copies ran while one was open for 0% of the time, Pallas kernels for 0%

profile of v10, /device:TPU:8, one launch (start us, length us, event | category | flops | bytes accessed | tf_op | source)
XLA Modules:
  0.0 164.7 jit_solution(10122541178938699285)
XLA Ops:
  0.6 0.0 copy-start
  0.6 19.0 %shard_map.118 = (bf16[4,2,128,512]{3,2,1,0:T(8,128)(2,1)}, bf16[4,2,128,512]{3,2,1,0:T(8,128)(2,1)}) custom-call(bf16[2,128,512]{2,1,0:T(8,128)(2,1)} %first.1, bf16[2,128,512]{2,1,0:T(8,128)(2,1)} %refs_4_.1), custom_call_target="tpu_custom_call" | custom-call | tf_op jit(solution)/shard_map/pallas_call | solution.py:287
  19.6 0.0 copy-start.2
  19.6 2.1 %multiply_convert_fusion.1 = (bf16[8,128,512]{2,1,0:T(8,128)(2,1)S(1)}, f32[8,128,512]{2,1,0:T(8,128)S(1)}) fusion(f32[512]{0:T(512)} %param.10, bf16[8,128,512]{2,1,0:T(8,128)(2,1)} %bitcast.164, bf16[512,512]{1,0:T(8,128)(2,1)S(1)} %copy-done), kind=kOutput, calls=%fused_computation.121 | convolution fusion | flops 540016640 | bytes 4720640 | tf_op jit(solution)/shard_map/dot_general | solution.py:326
  21.8 3.4 %collective-permute-start = (bf16[2,128,512]{2,1,0:T(8,128)(2,1)S(1)}, bf16[2,128,512]{2,1,0:T(8,128)(2,1)S(1)}, u32[]{:S(2)}, u32[]{:S(2)}) collective-permute-start(bf16[2,128,512]{2,1,0:T(8,128)(2,1)S(1)} %get-tuple-element.50), channel_id=1, source_target_pairs={{0,4},{4,8},{8,12},{12,16},{16,20},{20,24},{24,28},{28,32},{32,36}... | collective-permute-start | bytes 786440 | tf_op jit(solution)/shard_map/ppermute | solution.py:305
  25.3 9.0 %collective-permute-start.1 = (bf16[2,128,512]{2,1,0:T(8,128)(2,1)S(1)}, bf16[2,128,512]{2,1,0:T(8,128)(2,1)S(1)}, u32[]{:S(2)}, u32[]{:S(2)}) collective-permute-start(bf16[2,128,512]{2,1,0:T(8,128)(2,1)S(1)} %get-tuple-element.51), channel_id=1, source_target_pairs={{4,0},{8,4},{12,8},{16,12},{20,16},{24,20},{28,24},{32,28},{36,32}... | collective-permute-start | bytes 786440 | tf_op jit(solution)/shard_map/ppermute | solution.py:308
  34.3 0.0 copy-start.3
  34.3 4.8 %collective-permute-done = bf16[2,128,512]{2,1,0:T(8,128)(2,1)S(1)} collective-permute-done((bf16[2,128,512]{2,1,0:T(8,128)(2,1)S(1)}, bf16[2,128,512]{2,1,0:T(8,128)(2,1)S(1)}, u32[]{:S(2)}, u32[]{:S(2)}) %collective-permute-start) | collective-permute-done | bytes 262176 | tf_op jit(solution)/shard_map/ppermute | solution.py:305
  39.1 1.2 collective-permute-done.1
  40.3 0.5 fusion.68
  40.9 0.0 copy-start.7
  40.9 6.7 %multiply_convert_fusion = (bf16[8,128,512]{2,1,0:T(8,128)(2,1)S(1)}, f32[8,128,512]{2,1,0:T(8,128)S(1)}) fusion(f32[12,132,512]{2,1,0:T(8,128)S(1)} %fusion.68, f32[512]{0:T(512)S(1)} %bitcast.93, f32[512]{0:T(512)S(1)} %bitcast.95, f32[512]{0:T(512)S(1)} %bitcast.99, f32[512]{0:T(512)S(1)} %bitcast.101, f32[512]{0:T(512)S(1)} %bitcast.103, ...), kind=kLoop, calls=%fused_computation.118 | loop fusion | flops 28835840 | bytes 55627776 | tf_op jit(solution)/shard_map/convert_element_type | solution.py:344
  47.6 3.4 %fusion.36 = (f32[512]{0:T(512)S(1)}, f32[512]{0:T(512)S(1)}, f32[512]{0:T(512)S(1)}, f32[512]{0:T(512)S(1)}, f32[512]{0:T(512)S(1)}, /*index=5*/f32[512]{0:T(51...) fusion(f32[12,132,512]{2,1,0:T(8,128)S(1)} %fusion.68, f32[8,128,512]{2,1,0:T(8,128)S(1)} %get-tuple-element.47, ...), kind=kOutput, calls=%fused_computation.66 | convolution fusion | flops 550498304 | bytes 19415040 | tf_op jit(solution)/shard_map/dot_general | solution.py:346
  51.0 4.7 %fusion.37 = (f32[512]{0:T(512)S(1)}, f32[512]{0:T(512)S(1)}, f32[512]{0:T(512)S(1)}, f32[512]{0:T(512)S(1)}, f32[512]{0:T(512)S(1)}, /*index=5*/f32[512]{0:T(51...) fusion(bf16[8,128,512]{2,1,0:T(8,128)(2,1)S(1)} %get-tuple-elem, ...), kind=kLoop, calls=%fused_computation.67 | loop fusion | flops 19389440 | bytes 38834176 | tf_op jit(solution)/shard_map/reduce_sum | solution.py:359
  55.7 1.9 %collective-permute-start.2 = (bf16[2,128,512]{2,1,0:T(8,128)(2,1)S(1)}, bf16[2,128,512]{2,1,0:T(8,128)(2,1)S(1)}, u32[]{:S(2)}, u32[]{:S(2)}) collective-permute-start(bf16[2,128,512]{2,1,0:T(8,128)(2,1)S(1)} %get-tuple-element.48), channel_id=1, source_target_pairs={{0,4},{4,8},{8,12},{12,16},{16,20},{20,24},{24,28},{28,32},{32,36}... | collective-permute-start | bytes 786440 | tf_op jit(solution)/shard_map/ppermute | solution.py:305
  57.7 8.6 %collective-permute-start.3 = (bf16[2,128,512]{2,1,0:T(8,128)(2,1)S(1)}, bf16[2,128,512]{2,1,0:T(8,128)(2,1)S(1)}, u32[]{:S(2)}, u32[]{:S(2)}) collective-permute-start(bf16[2,128,512]{2,1,0:T(8,128)(2,1)S(1)} %get-tuple-element.49), channel_id=1, source_target_pairs={{4,0},{8,4},{12,8},{16,12},{20,16},{24,20},{28,24},{32,28},{36,32}... | collective-permute-start | bytes 786440 | tf_op jit(solution)/shard_map/ppermute | solution.py:308
  66.2 0.7 fusion.81.refs_1_
  67.0 0.0 copy-start.4
  67.0 3.4 %collective-permute-done.2 = bf16[2,128,512]{2,1,0:T(8,128)(2,1)S(1)} collective-permute-done((bf16[2,128,512]{2,1,0:T(8,128)(2,1)S(1)}, bf16[2,128,512]{2,1,0:T(8,128)(2,1)S(1)}, u32[]{:S(2)}, u32[]{:S(2)}) %collective-permute-start.2) | collective-permute-done | bytes 262176 | tf_op jit(solution)/shard_map/ppermute | solution.py:305
  70.4 1.2 collective-permute-done.3
  71.5 0.5 fusion.62
  72.1 7.3 %convert_reduce_fusion.1 = (f32[512]{0:T(512)S(1)}, bf16[8,128,512]{2,1,0:T(8,128)(2,1)S(1)}) fusion(f32[8,128,512]{2,1,0:T(8,128)S(1)} %get-tuple-element.80, f32[512]{0:T(512)S(1)} %copy-done.4, f32[12,132,512]{2,1,0:T(8,128)S(1)} %fusion.62, f32[512]{0:T(512)S(1)} %bitcast.94, f32[512]{0:T(512)S(1)} %bitcast.96, f32[512]{0:T(512)S(1)} %bitcast.100, ...), kind=kLoop, calls=%fused_computation.117 | loop fusion | flops 32505344 | bytes 55629824 | tf_op jit(solution)/shard_map/reduce_sum | solution.py:372
  79.4 2.1 %fusion.69 = f32[8,128,512]{2,1,0:T(8,128)} fusion(bf16[8,128,512]{2,1,0:T(8,128)(2,1)S(1)} %get-tuple-element.45, bf16[512,512]{1,0:T(8,128)(2,1)S(1)} %copy-done), kind=kOutput, calls=%fused_computation.132 | convolution fusion | flops 536870912 | bytes 3670016 | tf_op jit(solution)/shard_map/rwh,ch->rwc/dot_general | solution.py:374
  81.5 0.7 fusion.80.refs_0_
  82.2 0.1 concatenate.11
  82.3 0.1 copy-done.1
  82.4 78.4 %shard_map.119 = (f32[512,512]{1,0:T(8,128)S(1)}, f32[512,512]{1,0:T(8,128)S(1)}, f32[32,512]{1,0:T(8,128)S(1)}, bf16[2,128,512]{2,1,0:T(8,128)(2,1)S(1)}) custom-call(f32[512,512]{1,0:T(8,128)S(1)} %fusion.80.refs_0_, f32[512,512]{1,0:T(8,128)S(1)} %fusion.81.refs_1_, f32[32,512]{1,0:T(8,128)S(1)} %pad.13.refs_2_, f32[4,2,128,512]{3,2,1,0:T(8,128)} %bitcast.82, ...), custom_call_target="tpu_custom_call" | custom-call | tf_op jit(solution)/shard_map/pallas_call | solution.py:218
  160.8 0.6 fusion.77
  161.4 0.7 copy.17
  162.1 1.0 copy.18
  163.1 0.6 copy.19
  163.7 1.0 copy.20
  (15 shorter events, 0.1 us)
Async XLA Ops:
  0.6 19.0 %copy-start = (bf16[512,512]{1,0:T(8,128)(2,1)S(1)}, bf16[512,512]{1,0:T(8,128)(2,1)}, u32[]{:S(2)}) copy-start(bf16[512,512]{1,0:T(8,128)(2,1)} %param.9) | copy-start | bytes 1572868
  19.6 14.6 %copy-start.2 = (f32[25,512]{1,0:T(8,128)S(1)}, f32[25,512]{1,0:T(8,128)}, u32[]{:S(2)}) copy-start(f32[25,512]{1,0:T(8,128)} %param.11) | copy-start | bytes 153604
  21.8 17.3 %collective-permute-start = (bf16[2,128,512]{2,1,0:T(8,128)(2,1)S(1)}, bf16[2,128,512]{2,1,0:T(8,128)(2,1)S(1)}, u32[]{:S(2)}, u32[]{:S(2)}) collective-permute-start(bf16[2,128,512]{2,1,0:T(8,128)(2,1)S(1)} %get-tuple-element.50), channel_id=1, source_target_pairs={{0,4},{4,8},{8,12},{12,16},{16,20},{20,24},{24,28},{28,32},{32,36}... | collective-permute-start | bytes 786440 | tf_op jit(solution)/shard_map/ppermute | solution.py:305
  25.3 15.1 %collective-permute-start.1 = (bf16[2,128,512]{2,1,0:T(8,128)(2,1)S(1)}, bf16[2,128,512]{2,1,0:T(8,128)(2,1)S(1)}, u32[]{:S(2)}, u32[]{:S(2)}) collective-permute-start(bf16[2,128,512]{2,1,0:T(8,128)(2,1)S(1)} %get-tuple-element.51), channel_id=1, source_target_pairs={{4,0},{8,4},{12,8},{16,12},{20,16},{24,20},{28,24},{32,28},{36,32}... | collective-permute-start | bytes 786440 | tf_op jit(solution)/shard_map/ppermute | solution.py:308
  34.3 6.5 %copy-start.3 = (f32[512]{0:T(512)S(1)}, f32[512]{0:T(512)}, u32[]{:S(2)}) copy-start(f32[512]{0:T(512)} %param.12) | copy-start | bytes 6148
  40.9 6.7 %copy-start.6 = (bf16[4,2,128,512]{3,2,1,0:T(8,128)(2,1)S(1)}, bf16[4,2,128,512]{3,2,1,0:T(8,128)(2,1)}, u32[]{:S(2)}) copy-start(bf16[4,2,128,512]{3,2,1,0:T(8,128)(2,1)} %get-tuple-element.13) | copy-start | bytes 3145732
  40.9 6.7 %copy-start.7 = (bf16[512,512]{1,0:T(8,128)(2,1)S(1)}, bf16[512,512]{1,0:T(8,128)(2,1)}, u32[]{:S(2)}) copy-start(bf16[512,512]{1,0:T(8,128)(2,1)} %param.13) | copy-start | bytes 1572868
  55.7 14.6 %collective-permute-start.2 = (bf16[2,128,512]{2,1,0:T(8,128)(2,1)S(1)}, bf16[2,128,512]{2,1,0:T(8,128)(2,1)S(1)}, u32[]{:S(2)}, u32[]{:S(2)}) collective-permute-start(bf16[2,128,512]{2,1,0:T(8,128)(2,1)S(1)} %get-tuple-element.48), channel_id=1, source_target_pairs={{0,4},{4,8},{8,12},{12,16},{16,20},{20,24},{24,28},{28,32},{32,36}... | collective-permute-start | bytes 786440 | tf_op jit(solution)/shard_map/ppermute | solution.py:305
  57.7 13.9 %collective-permute-start.3 = (bf16[2,128,512]{2,1,0:T(8,128)(2,1)S(1)}, bf16[2,128,512]{2,1,0:T(8,128)(2,1)S(1)}, u32[]{:S(2)}, u32[]{:S(2)}) collective-permute-start(bf16[2,128,512]{2,1,0:T(8,128)(2,1)S(1)} %get-tuple-element.49), channel_id=1, source_target_pairs={{4,0},{8,4},{12,8},{16,12},{20,16},{24,20},{28,24},{32,28},{36,32}... | collective-permute-start | bytes 786440 | tf_op jit(solution)/shard_map/ppermute | solution.py:308
  67.0 5.1 %copy-start.4 = (f32[512]{0:T(512)S(1)}, f32[512]{0:T(512)}, u32[]{:S(2)}) copy-start(f32[512]{0:T(512)} %param.10) | copy-start | bytes 6148
  79.3 2.1 %copy-start.5 = (bf16[4,2,128,512]{3,2,1,0:T(8,128)(2,1)S(1)}, bf16[4,2,128,512]{3,2,1,0:T(8,128)(2,1)}, u32[]{:S(2)}) copy-start(bf16[4,2,128,512]{3,2,1,0:T(8,128)(2,1)} %get-tuple-element.12) | copy-start | bytes 3145732
  81.5 1.0 copy-start.1

commit v11 on v10

--- a/solution.py
+++ b/solution.py
@@ -150,19 +150,30 @@
         c.wait_recv()
     for c in copies:
         c.wait_send()
-    for s in range(nx - 1):
-        copies = []
-        for h in range(2):
-            sg = steps[h]
-            loc = obig(h, ix - sg * s)
+    first = [[None, None], [None, None]]
+    for h in range(2):
+        loc = obig(h, ix)
+        for j in range(2):
             c = pltpu.make_async_remote_copy(
-                src_ref=out.at[loc], dst_ref=out.at[loc], send_sem=gxsend.at[h * nx + s],
-                recv_sem=gxrecv.at[h * nx + s], device_id=x_next[h], device_id_type=MESH_ID)
-            c.start()
-            copies.append(c)
-        for h in range(2):
-            copies[h].wait_recv()
-            copies[h].wait_send()
+                src_ref=out.at[loc], dst_ref=out.at[loc], send_sem=gxsend.at[h * nx + j],
+                recv_sem=gxrecv.at[h * nx + j], device_id=x_next[j], device_id_type=MESH_ID)
+            c.start()
+            first[h][j] = c
+    second = []
+    for h in range(2):
+        first[h][h].wait_recv()
+        loc = obig(h, ix - steps[h])
+        c = pltpu.make_async_remote_copy(
+            src_ref=out.at[loc], dst_ref=out.at[loc], send_sem=gxsend.at[h * nx + 2],
+            recv_sem=gxrecv.at[h * nx + 2], device_id=x_next[h], device_id_type=MESH_ID)
+        c.start()
+        second.append(c)
+    for h in range(2):
+        first[h][1 - h].wait_recv()
+    for c in second:
+        c.wait_recv()
+    for c in first[0] + first[1] + second:
+        c.wait_send()
 
     chan_two.wait_recv()
     total = part[me] + from_pair[0] + from_far[...]

time: 167 us -> 164 us (0.982)
  Pallas kernels: 97.4 us -> 94.5 us
    pallas_call x1, Pallas kernels: 78.4 us -> 75.5 us  [row_group_allreduce(): pl.pallas_call(body, out_shape=tuple((jax.ShapeDtypeStruct(p.shape, jnp.f...]
where the time goes in v11:
time: 164 us; the launch traced here: 162 us
  Pallas kernels  94.5 us (58%)
  starting transfers between devices  22.9 us (14%)
  other arithmetic  19.6 us (12%)
  waiting for transfers between devices  10.5 us (6%)
  matrix products  9.12 us (6%)
  local copies, waits for them, and re-layouts  4.23 us (3%)
    pallas_call x1, Pallas kernels, row_group_allreduce(): pl.pallas_call(body, out_shape=tuple((jax.ShapeDtypeStruct(p.shape, jnp.f...  75.5 us
    pallas_call x1, Pallas kernels, chan_gather(): pl.pallas_call(_chan_gather_kernel, out_shape=(jax.ShapeDtypeStruct(shape...  19 us
    ppermute x2, starting transfers between devices, extended(): lax.ppermute(lax.slice_in_dim(block, 0, width, axis=dim), axis, backward)  17.5 us
    ppermute x2, waiting for transfers between devices, extended(): lax.ppermute(lax.slice_in_dim(block, block.shape[dim] - width, None, axis...  8.19 us
    reduce_sum x1, other arithmetic, shards(): grad_b1 = jnp.sum(flat_act.astype(jnp.float32), axis=0)  7.26 us
    convert_element_type x1, other arithmetic, shards(): mixed = mixed.astype(jnp.bfloat16).reshape(nrows * ncols, hslice)  6.69 us
    ppermute x2, starting transfers between devices, extended(): lax.ppermute(lax.slice_in_dim(block, block.shape[dim] - width, None, axis...  5.34 us
    reduce_sum x1, other arithmetic, shards(): jnp.sum(padded[row_tap:row_tap + nrows, col_tap:col_tap + ncols] * grad_p...  4.67 us
  transfers between devices with their start and end apart: 4, of which 4 were waited for; matrix products, arithmetic and copies ran while one was open for 0% of the time, Pallas kernels for 0%

profile of v11, /device:TPU:8, one launch (start us, length us, event | category | flops | bytes accessed | tf_op | source)
XLA Modules:
  0.0 161.8 jit_solution(3402825980606549857)
XLA Ops:
  0.6 0.0 copy-start
  0.6 19.0 %shard_map.118 = (bf16[4,2,128,512]{3,2,1,0:T(8,128)(2,1)}, bf16[4,2,128,512]{3,2,1,0:T(8,128)(2,1)}) custom-call(bf16[2,128,512]{2,1,0:T(8,128)(2,1)} %first.1, bf16[2,128,512]{2,1,0:T(8,128)(2,1)} %refs_4_.1), custom_call_target="tpu_custom_call" | custom-call | tf_op jit(solution)/shard_map/pallas_call | solution.py:298
  19.6 0.0 copy-start.2
  19.6 2.1 %multiply_convert_fusion.1 = (bf16[8,128,512]{2,1,0:T(8,128)(2,1)S(1)}, f32[8,128,512]{2,1,0:T(8,128)S(1)}) fusion(f32[512]{0:T(512)} %param.10, bf16[8,128,512]{2,1,0:T(8,128)(2,1)} %bitcast.164, bf16[512,512]{1,0:T(8,128)(2,1)S(1)} %copy-done), kind=kOutput, calls=%fused_computation.121 | convolution fusion | flops 540016640 | bytes 4720640 | tf_op jit(solution)/shard_map/dot_general | solution.py:337
  21.8 3.4 %collective-permute-start = (bf16[2,128,512]{2,1,0:T(8,128)(2,1)S(1)}, bf16[2,128,512]{2,1,0:T(8,128)(2,1)S(1)}, u32[]{:S(2)}, u32[]{:S(2)}) collective-permute-start(bf16[2,128,512]{2,1,0:T(8,128)(2,1)S(1)} %get-tuple-element.50), channel_id=1, source_target_pairs={{0,4},{4,8},{8,12},{12,16},{16,20},{20,24},{24,28},{28,32},{32,36}... | collective-permute-start | bytes 786440 | tf_op jit(solution)/shard_map/ppermute | solution.py:316
  25.3 9.0 %collective-permute-start.1 = (bf16[2,128,512]{2,1,0:T(8,128)(2,1)S(1)}, bf16[2,128,512]{2,1,0:T(8,128)(2,1)S(1)}, u32[]{:S(2)}, u32[]{:S(2)}) collective-permute-start(bf16[2,128,512]{2,1,0:T(8,128)(2,1)S(1)} %get-tuple-element.51), channel_id=1, source_target_pairs={{4,0},{8,4},{12,8},{16,12},{20,16},{24,20},{28,24},{32,28},{36,32}... | collective-permute-start | bytes 786440 | tf_op jit(solution)/shard_map/ppermute | solution.py:319
  34.3 0.0 copy-start.3
  34.3 4.8 %collective-permute-done = bf16[2,128,512]{2,1,0:T(8,128)(2,1)S(1)} collective-permute-done((bf16[2,128,512]{2,1,0:T(8,128)(2,1)S(1)}, bf16[2,128,512]{2,1,0:T(8,128)(2,1)S(1)}, u32[]{:S(2)}, u32[]{:S(2)}) %collective-permute-start) | collective-permute-done | bytes 262176 | tf_op jit(solution)/shard_map/ppermute | solution.py:316
  39.1 1.2 collective-permute-done.1
  40.3 0.5 fusion.68
  40.9 0.0 copy-start.7
  40.9 6.7 %multiply_convert_fusion = (bf16[8,128,512]{2,1,0:T(8,128)(2,1)S(1)}, f32[8,128,512]{2,1,0:T(8,128)S(1)}) fusion(f32[12,132,512]{2,1,0:T(8,128)S(1)} %fusion.68, f32[512]{0:T(512)S(1)} %bitcast.93, f32[512]{0:T(512)S(1)} %bitcast.95, f32[512]{0:T(512)S(1)} %bitcast.99, f32[512]{0:T(512)S(1)} %bitcast.101, f32[512]{0:T(512)S(1)} %bitcast.103, ...), kind=kLoop, calls=%fused_computation.118 | loop fusion | flops 28835840 | bytes 55627776 | tf_op jit(solution)/shard_map/convert_element_type | solution.py:355
  47.6 3.4 %fusion.36 = (f32[512]{0:T(512)S(1)}, f32[512]{0:T(512)S(1)}, f32[512]{0:T(512)S(1)}, f32[512]{0:T(512)S(1)}, f32[512]{0:T(512)S(1)}, /*index=5*/f32[512]{0:T(51...) fusion(f32[12,132,512]{2,1,0:T(8,128)S(1)} %fusion.68, f32[8,128,512]{2,1,0:T(8,128)S(1)} %get-tuple-element.47, ...), kind=kOutput, calls=%fused_computation.66 | convolution fusion | flops 550498304 | bytes 19415040 | tf_op jit(solution)/shard_map/dot_general | solution.py:357
  51.0 4.7 %fusion.37 = (f32[512]{0:T(512)S(1)}, f32[512]{0:T(512)S(1)}, f32[512]{0:T(512)S(1)}, f32[512]{0:T(512)S(1)}, f32[512]{0:T(512)S(1)}, /*index=5*/f32[512]{0:T(51...) fusion(bf16[8,128,512]{2,1,0:T(8,128)(2,1)S(1)} %get-tuple-elem, ...), kind=kLoop, calls=%fused_computation.67 | loop fusion | flops 19389440 | bytes 38834176 | tf_op jit(solution)/shard_map/reduce_sum | solution.py:370
  55.7 1.9 %collective-permute-start.2 = (bf16[2,128,512]{2,1,0:T(8,128)(2,1)S(1)}, bf16[2,128,512]{2,1,0:T(8,128)(2,1)S(1)}, u32[]{:S(2)}, u32[]{:S(2)}) collective-permute-start(bf16[2,128,512]{2,1,0:T(8,128)(2,1)S(1)} %get-tuple-element.48), channel_id=1, source_target_pairs={{0,4},{4,8},{8,12},{12,16},{16,20},{20,24},{24,28},{28,32},{32,36}... | collective-permute-start | bytes 786440 | tf_op jit(solution)/shard_map/ppermute | solution.py:316
  57.7 8.6 %collective-permute-start.3 = (bf16[2,128,512]{2,1,0:T(8,128)(2,1)S(1)}, bf16[2,128,512]{2,1,0:T(8,128)(2,1)S(1)}, u32[]{:S(2)}, u32[]{:S(2)}) collective-permute-start(bf16[2,128,512]{2,1,0:T(8,128)(2,1)S(1)} %get-tuple-element.49), channel_id=1, source_target_pairs={{4,0},{8,4},{12,8},{16,12},{20,16},{24,20},{28,24},{32,28},{36,32}... | collective-permute-start | bytes 786440 | tf_op jit(solution)/shard_map/ppermute | solution.py:319
  66.2 0.7 fusion.81.refs_1_
  67.0 0.0 copy-start.4
  67.0 3.4 %collective-permute-done.2 = bf16[2,128,512]{2,1,0:T(8,128)(2,1)S(1)} collective-permute-done((bf16[2,128,512]{2,1,0:T(8,128)(2,1)S(1)}, bf16[2,128,512]{2,1,0:T(8,128)(2,1)S(1)}, u32[]{:S(2)}, u32[]{:S(2)}) %collective-permute-start.2) | collective-permute-done | bytes 262176 | tf_op jit(solution)/shard_map/ppermute | solution.py:316
  70.4 1.2 collective-permute-done.3
  71.5 0.5 fusion.62
  72.1 7.3 %convert_reduce_fusion.1 = (f32[512]{0:T(512)S(1)}, bf16[8,128,512]{2,1,0:T(8,128)(2,1)S(1)}) fusion(f32[8,128,512]{2,1,0:T(8,128)S(1)} %get-tuple-element.80, f32[512]{0:T(512)S(1)} %copy-done.4, f32[12,132,512]{2,1,0:T(8,128)S(1)} %fusion.62, f32[512]{0:T(512)S(1)} %bitcast.94, f32[512]{0:T(512)S(1)} %bitcast.96, f32[512]{0:T(512)S(1)} %bitcast.100, ...), kind=kLoop, calls=%fused_computation.117 | loop fusion | flops 32505344 | bytes 55629824 | tf_op jit(solution)/shard_map/reduce_sum | solution.py:383
  79.4 2.1 %fusion.69 = f32[8,128,512]{2,1,0:T(8,128)} fusion(bf16[8,128,512]{2,1,0:T(8,128)(2,1)S(1)} %get-tuple-element.45, bf16[512,512]{1,0:T(8,128)(2,1)S(1)} %copy-done), kind=kOutput, calls=%fused_computation.132 | convolution fusion | flops 536870912 | bytes 3670016 | tf_op jit(solution)/shard_map/rwh,ch->rwc/dot_general | solution.py:385
  81.5 0.7 fusion.80.refs_0_
  82.2 0.1 concatenate.11
  82.3 0.1 copy-done.1
  82.4 75.5 %shard_map.119 = (f32[512,512]{1,0:T(8,128)S(1)}, f32[512,512]{1,0:T(8,128)S(1)}, f32[32,512]{1,0:T(8,128)S(1)}, bf16[2,128,512]{2,1,0:T(8,128)(2,1)S(1)}) custom-call(f32[512,512]{1,0:T(8,128)S(1)} %fusion.80.refs_0_, f32[512,512]{1,0:T(8,128)S(1)} %fusion.81.refs_1_, f32[32,512]{1,0:T(8,128)S(1)} %pad.13.refs_2_, f32[4,2,128,512]{3,2,1,0:T(8,128)} %bitcast.82, ...), custom_call_target="tpu_custom_call" | custom-call | tf_op jit(solution)/shard_map/pallas_call | solution.py:229
  158.0 0.6 fusion.77
  158.5 0.7 copy.17
  159.2 1.0 copy.18
  160.2 0.6 copy.19
  160.8 1.0 copy.20
  (15 shorter events, 0.1 us)
Async XLA Ops:
  0.6 19.0 %copy-start = (bf16[512,512]{1,0:T(8,128)(2,1)S(1)}, bf16[512,512]{1,0:T(8,128)(2,1)}, u32[]{:S(2)}) copy-start(bf16[512,512]{1,0:T(8,128)(2,1)} %param.9) | copy-start | bytes 1572868
  19.6 14.6 %copy-start.2 = (f32[25,512]{1,0:T(8,128)S(1)}, f32[25,512]{1,0:T(8,128)}, u32[]{:S(2)}) copy-start(f32[25,512]{1,0:T(8,128)} %param.11) | copy-start | bytes 153604
  21.8 17.3 %collective-permute-start = (bf16[2,128,512]{2,1,0:T(8,128)(2,1)S(1)}, bf16[2,128,512]{2,1,0:T(8,128)(2,1)S(1)}, u32[]{:S(2)}, u32[]{:S(2)}) collective-permute-start(bf16[2,128,512]{2,1,0:T(8,128)(2,1)S(1)} %get-tuple-element.50), channel_id=1, source_target_pairs={{0,4},{4,8},{8,12},{12,16},{16,20},{20,24},{24,28},{28,32},{32,36}... | collective-permute-start | bytes 786440 | tf_op jit(solution)/shard_map/ppermute | solution.py:316
  25.3 15.1 %collective-permute-start.1 = (bf16[2,128,512]{2,1,0:T(8,128)(2,1)S(1)}, bf16[2,128,512]{2,1,0:T(8,128)(2,1)S(1)}, u32[]{:S(2)}, u32[]{:S(2)}) collective-permute-start(bf16[2,128,512]{2,1,0:T(8,128)(2,1)S(1)} %get-tuple-element.51), channel_id=1, source_target_pairs={{4,0},{8,4},{12,8},{16,12},{20,16},{24,20},{28,24},{32,28},{36,32}... | collective-permute-start | bytes 786440 | tf_op jit(solution)/shard_map/ppermute | solution.py:319
  34.3 6.5 %copy-start.3 = (f32[512]{0:T(512)S(1)}, f32[512]{0:T(512)}, u32[]{:S(2)}) copy-start(f32[512]{0:T(512)} %param.12) | copy-start | bytes 6148
  40.9 6.7 %copy-start.6 = (bf16[4,2,128,512]{3,2,1,0:T(8,128)(2,1)S(1)}, bf16[4,2,128,512]{3,2,1,0:T(8,128)(2,1)}, u32[]{:S(2)}) copy-start(bf16[4,2,128,512]{3,2,1,0:T(8,128)(2,1)} %get-tuple-element.13) | copy-start | bytes 3145732
  40.9 6.7 %copy-start.7 = (bf16[512,512]{1,0:T(8,128)(2,1)S(1)}, bf16[512,512]{1,0:T(8,128)(2,1)}, u32[]{:S(2)}) copy-start(bf16[512,512]{1,0:T(8,128)(2,1)} %param.13) | copy-start | bytes 1572868
  55.7 14.6 %collective-permute-start.2 = (bf16[2,128,512]{2,1,0:T(8,128)(2,1)S(1)}, bf16[2,128,512]{2,1,0:T(8,128)(2,1)S(1)}, u32[]{:S(2)}, u32[]{:S(2)}) collective-permute-start(bf16[2,128,512]{2,1,0:T(8,128)(2,1)S(1)} %get-tuple-element.48), channel_id=1, source_target_pairs={{0,4},{4,8},{8,12},{12,16},{16,20},{20,24},{24,28},{28,32},{32,36}... | collective-permute-start | bytes 786440 | tf_op jit(solution)/shard_map/ppermute | solution.py:316
  57.7 13.9 %collective-permute-start.3 = (bf16[2,128,512]{2,1,0:T(8,128)(2,1)S(1)}, bf16[2,128,512]{2,1,0:T(8,128)(2,1)S(1)}, u32[]{:S(2)}, u32[]{:S(2)}) collective-permute-start(bf16[2,128,512]{2,1,0:T(8,128)(2,1)S(1)} %get-tuple-element.49), channel_id=1, source_target_pairs={{4,0},{8,4},{12,8},{16,12},{20,16},{24,20},{28,24},{32,28},{36,32}... | collective-permute-start | bytes 786440 | tf_op jit(solution)/shard_map/ppermute | solution.py:319
  67.0 5.1 %copy-start.4 = (f32[512]{0:T(512)S(1)}, f32[512]{0:T(512)}, u32[]{:S(2)}) copy-start(f32[512]{0:T(512)} %param.10) | copy-start | bytes 6148
  79.3 2.1 %copy-start.5 = (bf16[4,2,128,512]{3,2,1,0:T(8,128)(2,1)S(1)}, bf16[4,2,128,512]{3,2,1,0:T(8,128)(2,1)}, u32[]{:S(2)}) copy-start(bf16[4,2,128,512]{3,2,1,0:T(8,128)(2,1)} %get-tuple-element.12) | copy-start | bytes 3145732
  81.5 1.0 copy-start.1

commit v12 on v11

--- a/solution.py
+++ b/solution.py
@@ -76,22 +76,33 @@
     def obig(h, kx):
         return xblock(h, kx)
 
-    for s in range(nx - 1):
-        copies = []
-        for h in range(2):
-            sg = steps[h]
-            src = data.at[xblock(h, ix - sg)] if s == 0 else xs.at[h, s - 1]
+    rs_one = [[None, None], [None, None]]
+    for h in range(2):
+        sg = steps[h]
+        for j, (k, target) in enumerate(((ix + 2 * sg, x_next[h]), (ix - sg, x_next[1 - h]))):
             c = pltpu.make_async_remote_copy(
-                src_ref=src, dst_ref=xs.at[h, s], send_sem=xsend.at[h * nx + s],
-                recv_sem=xrecv.at[h * nx + s], device_id=x_next[h], device_id_type=MESH_ID)
-            c.start()
-            copies.append(c)
-        for h in range(2):
-            sg = steps[h]
-            copies[h].wait_recv()
-            r, c = xblock(h, ix - sg * (s + 2))
-            xs[h, s] = xs[h, s] + data[r, c]
-            copies[h].wait_send()
+                src_ref=data.at[xblock(h, k)], dst_ref=xs.at[h, j], send_sem=xsend.at[h * nx + j],
+                recv_sem=xrecv.at[h * nx + j], device_id=target, device_id_type=MESH_ID)
+            c.start()
+            rs_one[h][j] = c
+    rs_two = []
+    for h in range(2):
+        sg = steps[h]
+        rs_one[h][0].wait_recv()
+        r, c = xblock(h, ix + sg)
+        xs[h, 0] = xs[h, 0] + data[r, c]
+        copy = pltpu.make_async_remote_copy(
+            src_ref=xs.at[h, 0], dst_ref=xs.at[h, 2], send_sem=xsend.at[h * nx + 2],
+            recv_sem=xrecv.at[h * nx + 2], device_id=x_next[h], device_id_type=MESH_ID)
+        copy.start()
+        rs_two.append(copy)
+    for h in range(2):
+        rs_one[h][1].wait_recv()
+        rs_two[h].wait_recv()
+        r, c = xblock(h, ix)
+        xs[h, 2] = xs[h, 2] + xs[h, 1] + data[r, c]
+    for c in rs_one[0] + rs_one[1] + rs_two:
+        c.wait_send()
     last = nx - 2
     for c in chan_one:
         c.wait_recv()

time: 164 us -> 165 us (level)
  no operation moved by 1% of the time
where the time goes in v12:
time: 165 us; the launch traced here: 162 us
  Pallas kernels  94.5 us (57%)
  starting transfers between devices  22.9 us (14%)
  other arithmetic  19.6 us (12%)
  waiting for transfers between devices  10.5 us (6%)
  matrix products  9.12 us (6%)
  local copies, waits for them, and re-layouts  4.23 us (3%)
    pallas_call x1, Pallas kernels, row_group_allreduce(): pl.pallas_call(body, out_shape=tuple((jax.ShapeDtypeStruct(p.shape, jnp.f...  75.5 us
    pallas_call x1, Pallas kernels, chan_gather(): pl.pallas_call(_chan_gather_kernel, out_shape=(jax.ShapeDtypeStruct(shape...  19 us
    ppermute x2, starting transfers between devices, extended(): lax.ppermute(lax.slice_in_dim(block, 0, width, axis=dim), axis, backward)  17.5 us
    ppermute x2, waiting for transfers between devices, extended(): lax.ppermute(lax.slice_in_dim(block, block.shape[dim] - width, None, axis...  8.19 us
    reduce_sum x1, other arithmetic, shards(): grad_b1 = jnp.sum(flat_act.astype(jnp.float32), axis=0)  7.26 us
    convert_element_type x1, other arithmetic, shards(): mixed = mixed.astype(jnp.bfloat16).reshape(nrows * ncols, hslice)  6.69 us
    ppermute x2, starting transfers between devices, extended(): lax.ppermute(lax.slice_in_dim(block, block.shape[dim] - width, None, axis...  5.34 us
    reduce_sum x1, other arithmetic, shards(): jnp.sum(padded[row_tap:row_tap + nrows, col_tap:col_tap + ncols] * grad_p...  4.67 us
  transfers between devices with their start and end apart: 4, of which 4 were waited for; matrix products, arithmetic and copies ran while one was open for 0% of the time, Pallas kernels for 0%

profile of v12, /device:TPU:8, one launch (start us, length us, event | category | flops | bytes accessed | tf_op | source)
XLA Modules:
  0.0 161.8 jit_solution(2616599826668636514)
XLA Ops:
  0.6 0.0 copy-start
  0.6 19.0 %shard_map.118 = (bf16[4,2,128,512]{3,2,1,0:T(8,128)(2,1)}, bf16[4,2,128,512]{3,2,1,0:T(8,128)(2,1)}) custom-call(bf16[2,128,512]{2,1,0:T(8,128)(2,1)} %first.1, bf16[2,128,512]{2,1,0:T(8,128)(2,1)} %refs_4_.1), custom_call_target="tpu_custom_call" | custom-call | tf_op jit(solution)/shard_map/pallas_call | solution.py:309
  19.6 0.0 copy-start.2
  19.6 2.1 %multiply_convert_fusion.1 = (bf16[8,128,512]{2,1,0:T(8,128)(2,1)S(1)}, f32[8,128,512]{2,1,0:T(8,128)S(1)}) fusion(f32[512]{0:T(512)} %param.10, bf16[8,128,512]{2,1,0:T(8,128)(2,1)} %bitcast.164, bf16[512,512]{1,0:T(8,128)(2,1)S(1)} %copy-done), kind=kOutput, calls=%fused_computation.121 | convolution fusion | flops 540016640 | bytes 4720640 | tf_op jit(solution)/shard_map/dot_general | solution.py:348
  21.8 3.4 %collective-permute-start = (bf16[2,128,512]{2,1,0:T(8,128)(2,1)S(1)}, bf16[2,128,512]{2,1,0:T(8,128)(2,1)S(1)}, u32[]{:S(2)}, u32[]{:S(2)}) collective-permute-start(bf16[2,128,512]{2,1,0:T(8,128)(2,1)S(1)} %get-tuple-element.50), channel_id=1, source_target_pairs={{0,4},{4,8},{8,12},{12,16},{16,20},{20,24},{24,28},{28,32},{32,36}... | collective-permute-start | bytes 786440 | tf_op jit(solution)/shard_map/ppermute | solution.py:327
  25.3 9.0 %collective-permute-start.1 = (bf16[2,128,512]{2,1,0:T(8,128)(2,1)S(1)}, bf16[2,128,512]{2,1,0:T(8,128)(2,1)S(1)}, u32[]{:S(2)}, u32[]{:S(2)}) collective-permute-start(bf16[2,128,512]{2,1,0:T(8,128)(2,1)S(1)} %get-tuple-element.51), channel_id=1, source_target_pairs={{4,0},{8,4},{12,8},{16,12},{20,16},{24,20},{28,24},{32,28},{36,32}... | collective-permute-start | bytes 786440 | tf_op jit(solution)/shard_map/ppermute | solution.py:330
  34.3 0.0 copy-start.3
  34.3 4.8 %collective-permute-done = bf16[2,128,512]{2,1,0:T(8,128)(2,1)S(1)} collective-permute-done((bf16[2,128,512]{2,1,0:T(8,128)(2,1)S(1)}, bf16[2,128,512]{2,1,0:T(8,128)(2,1)S(1)}, u32[]{:S(2)}, u32[]{:S(2)}) %collective-permute-start) | collective-permute-done | bytes 262176 | tf_op jit(solution)/shard_map/ppermute | solution.py:327
  39.1 1.2 collective-permute-done.1
  40.3 0.5 fusion.68
  40.9 0.0 copy-start.7
  40.9 6.7 %multiply_convert_fusion = (bf16[8,128,512]{2,1,0:T(8,128)(2,1)S(1)}, f32[8,128,512]{2,1,0:T(8,128)S(1)}) fusion(f32[12,132,512]{2,1,0:T(8,128)S(1)} %fusion.68, f32[512]{0:T(512)S(1)} %bitcast.93, f32[512]{0:T(512)S(1)} %bitcast.95, f32[512]{0:T(512)S(1)} %bitcast.99, f32[512]{0:T(512)S(1)} %bitcast.101, f32[512]{0:T(512)S(1)} %bitcast.103, ...), kind=kLoop, calls=%fused_computation.118 | loop fusion | flops 28835840 | bytes 55627776 | tf_op jit(solution)/shard_map/convert_element_type | solution.py:366
  47.6 3.4 %fusion.36 = (f32[512]{0:T(512)S(1)}, f32[512]{0:T(512)S(1)}, f32[512]{0:T(512)S(1)}, f32[512]{0:T(512)S(1)}, f32[512]{0:T(512)S(1)}, /*index=5*/f32[512]{0:T(51...) fusion(f32[12,132,512]{2,1,0:T(8,128)S(1)} %fusion.68, f32[8,128,512]{2,1,0:T(8,128)S(1)} %get-tuple-element.47, ...), kind=kOutput, calls=%fused_computation.66 | convolution fusion | flops 550498304 | bytes 19415040 | tf_op jit(solution)/shard_map/dot_general | solution.py:368
  51.0 4.7 %fusion.37 = (f32[512]{0:T(512)S(1)}, f32[512]{0:T(512)S(1)}, f32[512]{0:T(512)S(1)}, f32[512]{0:T(512)S(1)}, f32[512]{0:T(512)S(1)}, /*index=5*/f32[512]{0:T(51...) fusion(bf16[8,128,512]{2,1,0:T(8,128)(2,1)S(1)} %get-tuple-elem, ...), kind=kLoop, calls=%fused_computation.67 | loop fusion | flops 19389440 | bytes 38834176 | tf_op jit(solution)/shard_map/reduce_sum | solution.py:381
  55.7 1.9 %collective-permute-start.2 = (bf16[2,128,512]{2,1,0:T(8,128)(2,1)S(1)}, bf16[2,128,512]{2,1,0:T(8,128)(2,1)S(1)}, u32[]{:S(2)}, u32[]{:S(2)}) collective-permute-start(bf16[2,128,512]{2,1,0:T(8,128)(2,1)S(1)} %get-tuple-element.48), channel_id=1, source_target_pairs={{0,4},{4,8},{8,12},{12,16},{16,20},{20,24},{24,28},{28,32},{32,36}... | collective-permute-start | bytes 786440 | tf_op jit(solution)/shard_map/ppermute | solution.py:327
  57.7 8.6 %collective-permute-start.3 = (bf16[2,128,512]{2,1,0:T(8,128)(2,1)S(1)}, bf16[2,128,512]{2,1,0:T(8,128)(2,1)S(1)}, u32[]{:S(2)}, u32[]{:S(2)}) collective-permute-start(bf16[2,128,512]{2,1,0:T(8,128)(2,1)S(1)} %get-tuple-element.49), channel_id=1, source_target_pairs={{4,0},{8,4},{12,8},{16,12},{20,16},{24,20},{28,24},{32,28},{36,32}... | collective-permute-start | bytes 786440 | tf_op jit(solution)/shard_map/ppermute | solution.py:330
  66.2 0.7 fusion.81.refs_1_
  67.0 0.0 copy-start.4
  67.0 3.4 %collective-permute-done.2 = bf16[2,128,512]{2,1,0:T(8,128)(2,1)S(1)} collective-permute-done((bf16[2,128,512]{2,1,0:T(8,128)(2,1)S(1)}, bf16[2,128,512]{2,1,0:T(8,128)(2,1)S(1)}, u32[]{:S(2)}, u32[]{:S(2)}) %collective-permute-start.2) | collective-permute-done | bytes 262176 | tf_op jit(solution)/shard_map/ppermute | solution.py:327
  70.4 1.2 collective-permute-done.3
  71.5 0.5 fusion.62
  72.1 7.3 %convert_reduce_fusion.1 = (f32[512]{0:T(512)S(1)}, bf16[8,128,512]{2,1,0:T(8,128)(2,1)S(1)}) fusion(f32[8,128,512]{2,1,0:T(8,128)S(1)} %get-tuple-element.80, f32[512]{0:T(512)S(1)} %copy-done.4, f32[12,132,512]{2,1,0:T(8,128)S(1)} %fusion.62, f32[512]{0:T(512)S(1)} %bitcast.94, f32[512]{0:T(512)S(1)} %bitcast.96, f32[512]{0:T(512)S(1)} %bitcast.100, ...), kind=kLoop, calls=%fused_computation.117 | loop fusion | flops 32505344 | bytes 55629824 | tf_op jit(solution)/shard_map/reduce_sum | solution.py:394
  79.4 2.1 %fusion.69 = f32[8,128,512]{2,1,0:T(8,128)} fusion(bf16[8,128,512]{2,1,0:T(8,128)(2,1)S(1)} %get-tuple-element.45, bf16[512,512]{1,0:T(8,128)(2,1)S(1)} %copy-done), kind=kOutput, calls=%fused_computation.132 | convolution fusion | flops 536870912 | bytes 3670016 | tf_op jit(solution)/shard_map/rwh,ch->rwc/dot_general | solution.py:396
  81.5 0.7 fusion.80.refs_0_
  82.2 0.1 concatenate.11
  82.3 0.1 copy-done.1
  82.4 75.5 %shard_map.119 = (f32[512,512]{1,0:T(8,128)S(1)}, f32[512,512]{1,0:T(8,128)S(1)}, f32[32,512]{1,0:T(8,128)S(1)}, bf16[2,128,512]{2,1,0:T(8,128)(2,1)S(1)}) custom-call(f32[512,512]{1,0:T(8,128)S(1)} %fusion.80.refs_0_, f32[512,512]{1,0:T(8,128)S(1)} %fusion.81.refs_1_, f32[32,512]{1,0:T(8,128)S(1)} %pad.13.refs_2_, f32[4,2,128,512]{3,2,1,0:T(8,128)} %bitcast.82, ...), custom_call_target="tpu_custom_call" | custom-call | tf_op jit(solution)/shard_map/pallas_call | solution.py:240
  157.9 0.6 fusion.77
  158.5 0.7 copy.17
  159.2 1.0 copy.18
  160.2 0.6 copy.19
  160.8 1.0 copy.20
  (15 shorter events, 0.1 us)
Async XLA Ops:
  0.6 19.0 %copy-start = (bf16[512,512]{1,0:T(8,128)(2,1)S(1)}, bf16[512,512]{1,0:T(8,128)(2,1)}, u32[]{:S(2)}) copy-start(bf16[512,512]{1,0:T(8,128)(2,1)} %param.9) | copy-start | bytes 1572868
  19.6 14.6 %copy-start.2 = (f32[25,512]{1,0:T(8,128)S(1)}, f32[25,512]{1,0:T(8,128)}, u32[]{:S(2)}) copy-start(f32[25,512]{1,0:T(8,128)} %param.11) | copy-start | bytes 153604
  21.8 17.3 %collective-permute-start = (bf16[2,128,512]{2,1,0:T(8,128)(2,1)S(1)}, bf16[2,128,512]{2,1,0:T(8,128)(2,1)S(1)}, u32[]{:S(2)}, u32[]{:S(2)}) collective-permute-start(bf16[2,128,512]{2,1,0:T(8,128)(2,1)S(1)} %get-tuple-element.50), channel_id=1, source_target_pairs={{0,4},{4,8},{8,12},{12,16},{16,20},{20,24},{24,28},{28,32},{32,36}... | collective-permute-start | bytes 786440 | tf_op jit(solution)/shard_map/ppermute | solution.py:327
  25.3 15.1 %collective-permute-start.1 = (bf16[2,128,512]{2,1,0:T(8,128)(2,1)S(1)}, bf16[2,128,512]{2,1,0:T(8,128)(2,1)S(1)}, u32[]{:S(2)}, u32[]{:S(2)}) collective-permute-start(bf16[2,128,512]{2,1,0:T(8,128)(2,1)S(1)} %get-tuple-element.51), channel_id=1, source_target_pairs={{4,0},{8,4},{12,8},{16,12},{20,16},{24,20},{28,24},{32,28},{36,32}... | collective-permute-start | bytes 786440 | tf_op jit(solution)/shard_map/ppermute | solution.py:330
  34.3 6.5 %copy-start.3 = (f32[512]{0:T(512)S(1)}, f32[512]{0:T(512)}, u32[]{:S(2)}) copy-start(f32[512]{0:T(512)} %param.12) | copy-start | bytes 6148
  40.9 6.7 %copy-start.6 = (bf16[4,2,128,512]{3,2,1,0:T(8,128)(2,1)S(1)}, bf16[4,2,128,512]{3,2,1,0:T(8,128)(2,1)}, u32[]{:S(2)}) copy-start(bf16[4,2,128,512]{3,2,1,0:T(8,128)(2,1)} %get-tuple-element.13) | copy-start | bytes 3145732
  40.9 6.7 %copy-start.7 = (bf16[512,512]{1,0:T(8,128)(2,1)S(1)}, bf16[512,512]{1,0:T(8,128)(2,1)}, u32[]{:S(2)}) copy-start(bf16[512,512]{1,0:T(8,128)(2,1)} %param.13) | copy-start | bytes 1572868
  55.7 14.6 %collective-permute-start.2 = (bf16[2,128,512]{2,1,0:T(8,128)(2,1)S(1)}, bf16[2,128,512]{2,1,0:T(8,128)(2,1)S(1)}, u32[]{:S(2)}, u32[]{:S(2)}) collective-permute-start(bf16[2,128,512]{2,1,0:T(8,128)(2,1)S(1)} %get-tuple-element.48), channel_id=1, source_target_pairs={{0,4},{4,8},{8,12},{12,16},{16,20},{20,24},{24,28},{28,32},{32,36}... | collective-permute-start | bytes 786440 | tf_op jit(solution)/shard_map/ppermute | solution.py:327
  57.7 13.9 %collective-permute-start.3 = (bf16[2,128,512]{2,1,0:T(8,128)(2,1)S(1)}, bf16[2,128,512]{2,1,0:T(8,128)(2,1)S(1)}, u32[]{:S(2)}, u32[]{:S(2)}) collective-permute-start(bf16[2,128,512]{2,1,0:T(8,128)(2,1)S(1)} %get-tuple-element.49), channel_id=1, source_target_pairs={{4,0},{8,4},{12,8},{16,12},{20,16},{24,20},{28,24},{32,28},{36,32}... | collective-permute-start | bytes 786440 | tf_op jit(solution)/shard_map/ppermute | solution.py:330
  67.0 5.1 %copy-start.4 = (f32[512]{0:T(512)S(1)}, f32[512]{0:T(512)}, u32[]{:S(2)}) copy-start(f32[512]{0:T(512)} %param.10) | copy-start | bytes 6148
  79.3 2.1 %copy-start.5 = (bf16[4,2,128,512]{3,2,1,0:T(8,128)(2,1)S(1)}, bf16[4,2,128,512]{3,2,1,0:T(8,128)(2,1)}, u32[]{:S(2)}) copy-start(bf16[4,2,128,512]{3,2,1,0:T(8,128)(2,1)} %get-tuple-element.12) | copy-start | bytes 3145732
  81.5 1.0 copy-start.1

commit v13 on v11

--- a/solution.py
+++ b/solution.py
@@ -124,6 +124,9 @@
     for c in copies:
         c.wait_send()
     zl = nz
+    chan_two.wait_recv()
+    total = part[me] + from_pair[0] + from_far[...]
+    grad_out[...] = (cot[...].astype(jnp.float32) + total).astype(grad_out.dtype)
     c = pltpu.make_async_remote_copy(
         src_ref=zs.at[:, zl], dst_ref=ys, send_sem=ysend.at[0], recv_sem=yrecv.at[0],
         device_id=partner, device_id_type=MESH_ID)
@@ -175,9 +178,6 @@
     for c in first[0] + first[1] + second:
         c.wait_send()
 
-    chan_two.wait_recv()
-    total = part[me] + from_pair[0] + from_far[...]
-    grad_out[...] = (cot[...].astype(jnp.float32) + total).astype(grad_out.dtype)
     for c in chan_one:
         c.wait_send()
     chan_two.wait_send()

time: 164 us -> 163 us (level)
  no operation moved by 1% of the time
where the time goes in v13:
time: 163 us; the launch traced here: 161 us
  Pallas kernels  93.8 us (58%)
  starting transfers between devices  22.9 us (14%)
  other arithmetic  19.6 us (12%)
  waiting for transfers between devices  10.5 us (6%)
  matrix products  9.12 us (6%)
  local copies, waits for them, and re-layouts  4.23 us (3%)
    pallas_call x1, Pallas kernels, row_group_allreduce(): pl.pallas_call(body, out_shape=tuple((jax.ShapeDtypeStruct(p.shape, jnp.f...  74.8 us
    pallas_call x1, Pallas kernels, chan_gather(): pl.pallas_call(_chan_gather_kernel, out_shape=(jax.ShapeDtypeStruct(shape...  19 us
    ppermute x2, starting transfers between devices, extended(): lax.ppermute(lax.slice_in_dim(block, 0, width, axis=dim), axis, backward)  17.5 us
    ppermute x2, waiting for transfers between devices, extended(): lax.ppermute(lax.slice_in_dim(block, block.shape[dim] - width, None, axis...  8.19 us
    reduce_sum x1, other arithmetic, shards(): grad_b1 = jnp.sum(flat_act.astype(jnp.float32), axis=0)  7.26 us
    convert_element_type x1, other arithmetic, shards(): mixed = mixed.astype(jnp.bfloat16).reshape(nrows * ncols, hslice)  6.69 us
    ppermute x2, starting transfers between devices, extended(): lax.ppermute(lax.slice_in_dim(block, block.shape[dim] - width, None, axis...  5.34 us
    reduce_sum x1, other arithmetic, shards(): jnp.sum(padded[row_tap:row_tap + nrows, col_tap:col_tap + ncols] * grad_p...  4.67 us
  transfers between devices with their start and end apart: 4, of which 4 were waited for; matrix products, arithmetic and copies ran while one was open for 0% of the time, Pallas kernels for 0%

profile of v13, /device:TPU:8, one launch (start us, length us, event | category | flops | bytes accessed | tf_op | source)
XLA Modules:
  0.0 161.1 jit_solution(13458349757454965919)
XLA Ops:
  0.6 0.0 copy-start
  0.6 19.0 %shard_map.118 = (bf16[4,2,128,512]{3,2,1,0:T(8,128)(2,1)}, bf16[4,2,128,512]{3,2,1,0:T(8,128)(2,1)}) custom-call(bf16[2,128,512]{2,1,0:T(8,128)(2,1)} %first.1, bf16[2,128,512]{2,1,0:T(8,128)(2,1)} %refs_4_.1), custom_call_target="tpu_custom_call" | custom-call | tf_op jit(solution)/shard_map/pallas_call | solution.py:298
  19.6 0.0 copy-start.2
  19.6 2.1 %multiply_convert_fusion.1 = (bf16[8,128,512]{2,1,0:T(8,128)(2,1)S(1)}, f32[8,128,512]{2,1,0:T(8,128)S(1)}) fusion(f32[512]{0:T(512)} %param.10, bf16[8,128,512]{2,1,0:T(8,128)(2,1)} %bitcast.164, bf16[512,512]{1,0:T(8,128)(2,1)S(1)} %copy-done), kind=kOutput, calls=%fused_computation.121 | convolution fusion | flops 540016640 | bytes 4720640 | tf_op jit(solution)/shard_map/dot_general | solution.py:337
  21.8 3.4 %collective-permute-start = (bf16[2,128,512]{2,1,0:T(8,128)(2,1)S(1)}, bf16[2,128,512]{2,1,0:T(8,128)(2,1)S(1)}, u32[]{:S(2)}, u32[]{:S(2)}) collective-permute-start(bf16[2,128,512]{2,1,0:T(8,128)(2,1)S(1)} %get-tuple-element.50), channel_id=1, source_target_pairs={{0,4},{4,8},{8,12},{12,16},{16,20},{20,24},{24,28},{28,32},{32,36}... | collective-permute-start | bytes 786440 | tf_op jit(solution)/shard_map/ppermute | solution.py:316
  25.3 9.0 %collective-permute-start.1 = (bf16[2,128,512]{2,1,0:T(8,128)(2,1)S(1)}, bf16[2,128,512]{2,1,0:T(8,128)(2,1)S(1)}, u32[]{:S(2)}, u32[]{:S(2)}) collective-permute-start(bf16[2,128,512]{2,1,0:T(8,128)(2,1)S(1)} %get-tuple-element.51), channel_id=1, source_target_pairs={{4,0},{8,4},{12,8},{16,12},{20,16},{24,20},{28,24},{32,28},{36,32}... | collective-permute-start | bytes 786440 | tf_op jit(solution)/shard_map/ppermute | solution.py:319
  34.3 0.0 copy-start.3
  34.3 4.8 %collective-permute-done = bf16[2,128,512]{2,1,0:T(8,128)(2,1)S(1)} collective-permute-done((bf16[2,128,512]{2,1,0:T(8,128)(2,1)S(1)}, bf16[2,128,512]{2,1,0:T(8,128)(2,1)S(1)}, u32[]{:S(2)}, u32[]{:S(2)}) %collective-permute-start) | collective-permute-done | bytes 262176 | tf_op jit(solution)/shard_map/ppermute | solution.py:316
  39.1 1.2 collective-permute-done.1
  40.3 0.5 fusion.68
  40.9 0.0 copy-start.7
  40.9 6.7 %multiply_convert_fusion = (bf16[8,128,512]{2,1,0:T(8,128)(2,1)S(1)}, f32[8,128,512]{2,1,0:T(8,128)S(1)}) fusion(f32[12,132,512]{2,1,0:T(8,128)S(1)} %fusion.68, f32[512]{0:T(512)S(1)} %bitcast.93, f32[512]{0:T(512)S(1)} %bitcast.95, f32[512]{0:T(512)S(1)} %bitcast.99, f32[512]{0:T(512)S(1)} %bitcast.101, f32[512]{0:T(512)S(1)} %bitcast.103, ...), kind=kLoop, calls=%fused_computation.118 | loop fusion | flops 28835840 | bytes 55627776 | tf_op jit(solution)/shard_map/convert_element_type | solution.py:355
  47.6 3.4 %fusion.36 = (f32[512]{0:T(512)S(1)}, f32[512]{0:T(512)S(1)}, f32[512]{0:T(512)S(1)}, f32[512]{0:T(512)S(1)}, f32[512]{0:T(512)S(1)}, /*index=5*/f32[512]{0:T(51...) fusion(f32[12,132,512]{2,1,0:T(8,128)S(1)} %fusion.68, f32[8,128,512]{2,1,0:T(8,128)S(1)} %get-tuple-element.47, ...), kind=kOutput, calls=%fused_computation.66 | convolution fusion | flops 550498304 | bytes 19415040 | tf_op jit(solution)/shard_map/dot_general | solution.py:357
  51.0 4.7 %fusion.37 = (f32[512]{0:T(512)S(1)}, f32[512]{0:T(512)S(1)}, f32[512]{0:T(512)S(1)}, f32[512]{0:T(512)S(1)}, f32[512]{0:T(512)S(1)}, /*index=5*/f32[512]{0:T(51...) fusion(bf16[8,128,512]{2,1,0:T(8,128)(2,1)S(1)} %get-tuple-elem, ...), kind=kLoop, calls=%fused_computation.67 | loop fusion | flops 19389440 | bytes 38834176 | tf_op jit(solution)/shard_map/reduce_sum | solution.py:370
  55.7 1.9 %collective-permute-start.2 = (bf16[2,128,512]{2,1,0:T(8,128)(2,1)S(1)}, bf16[2,128,512]{2,1,0:T(8,128)(2,1)S(1)}, u32[]{:S(2)}, u32[]{:S(2)}) collective-permute-start(bf16[2,128,512]{2,1,0:T(8,128)(2,1)S(1)} %get-tuple-element.48), channel_id=1, source_target_pairs={{0,4},{4,8},{8,12},{12,16},{16,20},{20,24},{24,28},{28,32},{32,36}... | collective-permute-start | bytes 786440 | tf_op jit(solution)/shard_map/ppermute | solution.py:316
  57.7 8.6 %collective-permute-start.3 = (bf16[2,128,512]{2,1,0:T(8,128)(2,1)S(1)}, bf16[2,128,512]{2,1,0:T(8,128)(2,1)S(1)}, u32[]{:S(2)}, u32[]{:S(2)}) collective-permute-start(bf16[2,128,512]{2,1,0:T(8,128)(2,1)S(1)} %get-tuple-element.49), channel_id=1, source_target_pairs={{4,0},{8,4},{12,8},{16,12},{20,16},{24,20},{28,24},{32,28},{36,32}... | collective-permute-start | bytes 786440 | tf_op jit(solution)/shard_map/ppermute | solution.py:319
  66.2 0.7 fusion.81.refs_1_
  67.0 0.0 copy-start.4
  67.0 3.4 %collective-permute-done.2 = bf16[2,128,512]{2,1,0:T(8,128)(2,1)S(1)} collective-permute-done((bf16[2,128,512]{2,1,0:T(8,128)(2,1)S(1)}, bf16[2,128,512]{2,1,0:T(8,128)(2,1)S(1)}, u32[]{:S(2)}, u32[]{:S(2)}) %collective-permute-start.2) | collective-permute-done | bytes 262176 | tf_op jit(solution)/shard_map/ppermute | solution.py:316
  70.4 1.2 collective-permute-done.3
  71.5 0.5 fusion.62
  72.1 7.3 %convert_reduce_fusion.1 = (f32[512]{0:T(512)S(1)}, bf16[8,128,512]{2,1,0:T(8,128)(2,1)S(1)}) fusion(f32[8,128,512]{2,1,0:T(8,128)S(1)} %get-tuple-element.80, f32[512]{0:T(512)S(1)} %copy-done.4, f32[12,132,512]{2,1,0:T(8,128)S(1)} %fusion.62, f32[512]{0:T(512)S(1)} %bitcast.94, f32[512]{0:T(512)S(1)} %bitcast.96, f32[512]{0:T(512)S(1)} %bitcast.100, ...), kind=kLoop, calls=%fused_computation.117 | loop fusion | flops 32505344 | bytes 55629824 | tf_op jit(solution)/shard_map/reduce_sum | solution.py:383
  79.4 2.1 %fusion.69 = f32[8,128,512]{2,1,0:T(8,128)} fusion(bf16[8,128,512]{2,1,0:T(8,128)(2,1)S(1)} %get-tuple-element.45, bf16[512,512]{1,0:T(8,128)(2,1)S(1)} %copy-done), kind=kOutput, calls=%fused_computation.132 | convolution fusion | flops 536870912 | bytes 3670016 | tf_op jit(solution)/shard_map/rwh,ch->rwc/dot_general | solution.py:385
  81.5 0.7 fusion.80.refs_0_
  82.2 0.1 concatenate.11
  82.3 0.1 copy-done.1
  82.4 74.8 %shard_map.119 = (f32[512,512]{1,0:T(8,128)S(1)}, f32[512,512]{1,0:T(8,128)S(1)}, f32[32,512]{1,0:T(8,128)S(1)}, bf16[2,128,512]{2,1,0:T(8,128)(2,1)S(1)}) custom-call(f32[512,512]{1,0:T(8,128)S(1)} %fusion.80.refs_0_, f32[512,512]{1,0:T(8,128)S(1)} %fusion.81.refs_1_, f32[32,512]{1,0:T(8,128)S(1)} %pad.13.refs_2_, f32[4,2,128,512]{3,2,1,0:T(8,128)} %bitcast.82, ...), custom_call_target="tpu_custom_call" | custom-call | tf_op jit(solution)/shard_map/pallas_call | solution.py:229
  157.3 0.6 fusion.77
  157.8 0.7 copy.17
  158.5 1.0 copy.18
  159.5 0.6 copy.19
  160.1 1.0 copy.20
  (15 shorter events, 0.1 us)
Async XLA Ops:
  0.6 19.0 %copy-start = (bf16[512,512]{1,0:T(8,128)(2,1)S(1)}, bf16[512,512]{1,0:T(8,128)(2,1)}, u32[]{:S(2)}) copy-start(bf16[512,512]{1,0:T(8,128)(2,1)} %param.9) | copy-start | bytes 1572868
  19.6 14.6 %copy-start.2 = (f32[25,512]{1,0:T(8,128)S(1)}, f32[25,512]{1,0:T(8,128)}, u32[]{:S(2)}) copy-start(f32[25,512]{1,0:T(8,128)} %param.11) | copy-start | bytes 153604
  21.8 17.3 %collective-permute-start = (bf16[2,128,512]{2,1,0:T(8,128)(2,1)S(1)}, bf16[2,128,512]{2,1,0:T(8,128)(2,1)S(1)}, u32[]{:S(2)}, u32[]{:S(2)}) collective-permute-start(bf16[2,128,512]{2,1,0:T(8,128)(2,1)S(1)} %get-tuple-element.50), channel_id=1, source_target_pairs={{0,4},{4,8},{8,12},{12,16},{16,20},{20,24},{24,28},{28,32},{32,36}... | collective-permute-start | bytes 786440 | tf_op jit(solution)/shard_map/ppermute | solution.py:316
  25.3 15.1 %collective-permute-start.1 = (bf16[2,128,512]{2,1,0:T(8,128)(2,1)S(1)}, bf16[2,128,512]{2,1,0:T(8,128)(2,1)S(1)}, u32[]{:S(2)}, u32[]{:S(2)}) collective-permute-start(bf16[2,128,512]{2,1,0:T(8,128)(2,1)S(1)} %get-tuple-element.51), channel_id=1, source_target_pairs={{4,0},{8,4},{12,8},{16,12},{20,16},{24,20},{28,24},{32,28},{36,32}... | collective-permute-start | bytes 786440 | tf_op jit(solution)/shard_map/ppermute | solution.py:319
  34.3 6.5 %copy-start.3 = (f32[512]{0:T(512)S(1)}, f32[512]{0:T(512)}, u32[]{:S(2)}) copy-start(f32[512]{0:T(512)} %param.12) | copy-start | bytes 6148
  40.9 6.7 %copy-start.6 = (bf16[4,2,128,512]{3,2,1,0:T(8,128)(2,1)S(1)}, bf16[4,2,128,512]{3,2,1,0:T(8,128)(2,1)}, u32[]{:S(2)}) copy-start(bf16[4,2,128,512]{3,2,1,0:T(8,128)(2,1)} %get-tuple-element.13) | copy-start | bytes 3145732
  40.9 6.7 %copy-start.7 = (bf16[512,512]{1,0:T(8,128)(2,1)S(1)}, bf16[512,512]{1,0:T(8,128)(2,1)}, u32[]{:S(2)}) copy-start(bf16[512,512]{1,0:T(8,128)(2,1)} %param.13) | copy-start | bytes 1572868
  55.7 14.6 %collective-permute-start.2 = (bf16[2,128,512]{2,1,0:T(8,128)(2,1)S(1)}, bf16[2,128,512]{2,1,0:T(8,128)(2,1)S(1)}, u32[]{:S(2)}, u32[]{:S(2)}) collective-permute-start(bf16[2,128,512]{2,1,0:T(8,128)(2,1)S(1)} %get-tuple-element.48), channel_id=1, source_target_pairs={{0,4},{4,8},{8,12},{12,16},{16,20},{20,24},{24,28},{28,32},{32,36}... | collective-permute-start | bytes 786440 | tf_op jit(solution)/shard_map/ppermute | solution.py:316
  57.7 13.9 %collective-permute-start.3 = (bf16[2,128,512]{2,1,0:T(8,128)(2,1)S(1)}, bf16[2,128,512]{2,1,0:T(8,128)(2,1)S(1)}, u32[]{:S(2)}, u32[]{:S(2)}) collective-permute-start(bf16[2,128,512]{2,1,0:T(8,128)(2,1)S(1)} %get-tuple-element.49), channel_id=1, source_target_pairs={{4,0},{8,4},{12,8},{16,12},{20,16},{24,20},{28,24},{32,28},{36,32}... | collective-permute-start | bytes 786440 | tf_op jit(solution)/shard_map/ppermute | solution.py:319
  67.0 5.1 %copy-start.4 = (f32[512]{0:T(512)S(1)}, f32[512]{0:T(512)}, u32[]{:S(2)}) copy-start(f32[512]{0:T(512)} %param.10) | copy-start | bytes 6148
  79.3 2.1 %copy-start.5 = (bf16[4,2,128,512]{3,2,1,0:T(8,128)(2,1)S(1)}, bf16[4,2,128,512]{3,2,1,0:T(8,128)(2,1)}, u32[]{:S(2)}) copy-start(bf16[4,2,128,512]{3,2,1,0:T(8,128)(2,1)} %get-tuple-element.12) | copy-start | bytes 3145732
  81.5 1.0 copy-start.1

commit v14 on v13

--- a/solution.py
+++ b/solution.py
@@ -267,14 +267,14 @@
 
     sources = (first, second)
     outs = (out_first, out_second)
-    step_one = []
-    for k in range(2):
-        for j, target in enumerate((pair, far)):
+    step_one = [None] * 4
+    for j, target in ((1, far), (0, pair)):
+        for k in range(2):
             c = pltpu.make_async_remote_copy(
                 src_ref=sources[k], dst_ref=outs[k].at[me], send_sem=sems.at[0, k, j],
                 recv_sem=sems.at[1, k, j], device_id=target, device_id_type=MESH_ID)
             c.start()
-            step_one.append(c)
+            step_one[2 * k + j] = c
     for k in range(2):
         outs[k][me] = sources[k][...]
     relay = []

time: 163 us -> 163 us (level)
  no operation moved by 1% of the time
where the time goes in v14:
time: 163 us; the launch traced here: 162 us
  Pallas kernels  94.4 us (58%)
  starting transfers between devices  22.9 us (14%)
  other arithmetic  19.6 us (12%)
  waiting for transfers between devices  10.5 us (6%)
  matrix products  9.11 us (6%)
  local copies, waits for them, and re-layouts  4.23 us (3%)
    pallas_call x1, Pallas kernels, row_group_allreduce(): pl.pallas_call(body, out_shape=tuple((jax.ShapeDtypeStruct(p.shape, jnp.f...  75.4 us
    pallas_call x1, Pallas kernels, chan_gather(): pl.pallas_call(_chan_gather_kernel, out_shape=(jax.ShapeDtypeStruct(shape...  19 us
    ppermute x2, starting transfers between devices, extended(): lax.ppermute(lax.slice_in_dim(block, 0, width, axis=dim), axis, backward)  17.5 us
    ppermute x2, waiting for transfers between devices, extended(): lax.ppermute(lax.slice_in_dim(block, block.shape[dim] - width, None, axis...  8.19 us
    reduce_sum x1, other arithmetic, shards(): grad_b1 = jnp.sum(flat_act.astype(jnp.float32), axis=0)  7.26 us
    convert_element_type x1, other arithmetic, shards(): mixed = mixed.astype(jnp.bfloat16).reshape(nrows * ncols, hslice)  6.69 us
    ppermute x2, starting transfers between devices, extended(): lax.ppermute(lax.slice_in_dim(block, block.shape[dim] - width, None, axis...  5.34 us
    reduce_sum x1, other arithmetic, shards(): jnp.sum(padded[row_tap:row_tap + nrows, col_tap:col_tap + ncols] * grad_p...  4.67 us
  transfers between devices with their start and end apart: 4, of which 4 were waited for; matrix products, arithmetic and copies ran while one was open for 0% of the time, Pallas kernels for 0%

profile of v14, /device:TPU:8, one launch (start us, length us, event | category | flops | bytes accessed | tf_op | source)
XLA Modules:
  0.0 161.7 jit_solution(6247036732293270359)
XLA Ops:
  0.6 0.0 copy-start
  0.6 19.0 %shard_map.118 = (bf16[4,2,128,512]{3,2,1,0:T(8,128)(2,1)}, bf16[4,2,128,512]{3,2,1,0:T(8,128)(2,1)}) custom-call(bf16[2,128,512]{2,1,0:T(8,128)(2,1)} %first.1, bf16[2,128,512]{2,1,0:T(8,128)(2,1)} %refs_4_.1), custom_call_target="tpu_custom_call" | custom-call | tf_op jit(solution)/shard_map/pallas_call | solution.py:298
  19.6 0.0 copy-start.2
  19.6 2.1 %multiply_convert_fusion.1 = (bf16[8,128,512]{2,1,0:T(8,128)(2,1)S(1)}, f32[8,128,512]{2,1,0:T(8,128)S(1)}) fusion(f32[512]{0:T(512)} %param.10, bf16[8,128,512]{2,1,0:T(8,128)(2,1)} %bitcast.164, bf16[512,512]{1,0:T(8,128)(2,1)S(1)} %copy-done), kind=kOutput, calls=%fused_computation.121 | convolution fusion | flops 540016640 | bytes 4720640 | tf_op jit(solution)/shard_map/dot_general | solution.py:337
  21.8 3.4 %collective-permute-start = (bf16[2,128,512]{2,1,0:T(8,128)(2,1)S(1)}, bf16[2,128,512]{2,1,0:T(8,128)(2,1)S(1)}, u32[]{:S(2)}, u32[]{:S(2)}) collective-permute-start(bf16[2,128,512]{2,1,0:T(8,128)(2,1)S(1)} %get-tuple-element.50), channel_id=1, source_target_pairs={{0,4},{4,8},{8,12},{12,16},{16,20},{20,24},{24,28},{28,32},{32,36}... | collective-permute-start | bytes 786440 | tf_op jit(solution)/shard_map/ppermute | solution.py:316
  25.3 9.0 %collective-permute-start.1 = (bf16[2,128,512]{2,1,0:T(8,128)(2,1)S(1)}, bf16[2,128,512]{2,1,0:T(8,128)(2,1)S(1)}, u32[]{:S(2)}, u32[]{:S(2)}) collective-permute-start(bf16[2,128,512]{2,1,0:T(8,128)(2,1)S(1)} %get-tuple-element.51), channel_id=1, source_target_pairs={{4,0},{8,4},{12,8},{16,12},{20,16},{24,20},{28,24},{32,28},{36,32}... | collective-permute-start | bytes 786440 | tf_op jit(solution)/shard_map/ppermute | solution.py:319
  34.3 0.0 copy-start.3
  34.3 4.8 %collective-permute-done = bf16[2,128,512]{2,1,0:T(8,128)(2,1)S(1)} collective-permute-done((bf16[2,128,512]{2,1,0:T(8,128)(2,1)S(1)}, bf16[2,128,512]{2,1,0:T(8,128)(2,1)S(1)}, u32[]{:S(2)}, u32[]{:S(2)}) %collective-permute-start) | collective-permute-done | bytes 262176 | tf_op jit(solution)/shard_map/ppermute | solution.py:316
  39.1 1.2 collective-permute-done.1
  40.3 0.5 fusion.68
  40.9 0.0 copy-start.7
  40.9 6.7 %multiply_convert_fusion = (bf16[8,128,512]{2,1,0:T(8,128)(2,1)S(1)}, f32[8,128,512]{2,1,0:T(8,128)S(1)}) fusion(f32[12,132,512]{2,1,0:T(8,128)S(1)} %fusion.68, f32[512]{0:T(512)S(1)} %bitcast.93, f32[512]{0:T(512)S(1)} %bitcast.95, f32[512]{0:T(512)S(1)} %bitcast.99, f32[512]{0:T(512)S(1)} %bitcast.101, f32[512]{0:T(512)S(1)} %bitcast.103, ...), kind=kLoop, calls=%fused_computation.118 | loop fusion | flops 28835840 | bytes 55627776 | tf_op jit(solution)/shard_map/convert_element_type | solution.py:355
  47.6 3.4 %fusion.36 = (f32[512]{0:T(512)S(1)}, f32[512]{0:T(512)S(1)}, f32[512]{0:T(512)S(1)}, f32[512]{0:T(512)S(1)}, f32[512]{0:T(512)S(1)}, /*index=5*/f32[512]{0:T(51...) fusion(f32[12,132,512]{2,1,0:T(8,128)S(1)} %fusion.68, f32[8,128,512]{2,1,0:T(8,128)S(1)} %get-tuple-element.47, ...), kind=kOutput, calls=%fused_computation.66 | convolution fusion | flops 550498304 | bytes 19415040 | tf_op jit(solution)/shard_map/dot_general | solution.py:357
  51.0 4.7 %fusion.37 = (f32[512]{0:T(512)S(1)}, f32[512]{0:T(512)S(1)}, f32[512]{0:T(512)S(1)}, f32[512]{0:T(512)S(1)}, f32[512]{0:T(512)S(1)}, /*index=5*/f32[512]{0:T(51...) fusion(bf16[8,128,512]{2,1,0:T(8,128)(2,1)S(1)} %get-tuple-elem, ...), kind=kLoop, calls=%fused_computation.67 | loop fusion | flops 19389440 | bytes 38834176 | tf_op jit(solution)/shard_map/reduce_sum | solution.py:370
  55.7 1.9 %collective-permute-start.2 = (bf16[2,128,512]{2,1,0:T(8,128)(2,1)S(1)}, bf16[2,128,512]{2,1,0:T(8,128)(2,1)S(1)}, u32[]{:S(2)}, u32[]{:S(2)}) collective-permute-start(bf16[2,128,512]{2,1,0:T(8,128)(2,1)S(1)} %get-tuple-element.48), channel_id=1, source_target_pairs={{0,4},{4,8},{8,12},{12,16},{16,20},{20,24},{24,28},{28,32},{32,36}... | collective-permute-start | bytes 786440 | tf_op jit(solution)/shard_map/ppermute | solution.py:316
  57.7 8.6 %collective-permute-start.3 = (bf16[2,128,512]{2,1,0:T(8,128)(2,1)S(1)}, bf16[2,128,512]{2,1,0:T(8,128)(2,1)S(1)}, u32[]{:S(2)}, u32[]{:S(2)}) collective-permute-start(bf16[2,128,512]{2,1,0:T(8,128)(2,1)S(1)} %get-tuple-element.49), channel_id=1, source_target_pairs={{4,0},{8,4},{12,8},{16,12},{20,16},{24,20},{28,24},{32,28},{36,32}... | collective-permute-start | bytes 786440 | tf_op jit(solution)/shard_map/ppermute | solution.py:319
  66.2 0.7 fusion.81.refs_1_
  67.0 0.0 copy-start.4
  67.0 3.4 %collective-permute-done.2 = bf16[2,128,512]{2,1,0:T(8,128)(2,1)S(1)} collective-permute-done((bf16[2,128,512]{2,1,0:T(8,128)(2,1)S(1)}, bf16[2,128,512]{2,1,0:T(8,128)(2,1)S(1)}, u32[]{:S(2)}, u32[]{:S(2)}) %collective-permute-start.2) | collective-permute-done | bytes 262176 | tf_op jit(solution)/shard_map/ppermute | solution.py:316
  70.4 1.2 collective-permute-done.3
  71.5 0.5 fusion.62
  72.1 7.3 %convert_reduce_fusion.1 = (f32[512]{0:T(512)S(1)}, bf16[8,128,512]{2,1,0:T(8,128)(2,1)S(1)}) fusion(f32[8,128,512]{2,1,0:T(8,128)S(1)} %get-tuple-element.80, f32[512]{0:T(512)S(1)} %copy-done.4, f32[12,132,512]{2,1,0:T(8,128)S(1)} %fusion.62, f32[512]{0:T(512)S(1)} %bitcast.94, f32[512]{0:T(512)S(1)} %bitcast.96, f32[512]{0:T(512)S(1)} %bitcast.100, ...), kind=kLoop, calls=%fused_computation.117 | loop fusion | flops 32505344 | bytes 55629824 | tf_op jit(solution)/shard_map/reduce_sum | solution.py:383
  79.4 2.1 %fusion.69 = f32[8,128,512]{2,1,0:T(8,128)} fusion(bf16[8,128,512]{2,1,0:T(8,128)(2,1)S(1)} %get-tuple-element.45, bf16[512,512]{1,0:T(8,128)(2,1)S(1)} %copy-done), kind=kOutput, calls=%fused_computation.132 | convolution fusion | flops 536870912 | bytes 3670016 | tf_op jit(solution)/shard_map/rwh,ch->rwc/dot_general | solution.py:385
  81.5 0.7 fusion.80.refs_0_
  82.2 0.1 concatenate.11
  82.3 0.1 copy-done.1
  82.4 75.4 %shard_map.119 = (f32[512,512]{1,0:T(8,128)S(1)}, f32[512,512]{1,0:T(8,128)S(1)}, f32[32,512]{1,0:T(8,128)S(1)}, bf16[2,128,512]{2,1,0:T(8,128)(2,1)S(1)}) custom-call(f32[512,512]{1,0:T(8,128)S(1)} %fusion.80.refs_0_, f32[512,512]{1,0:T(8,128)S(1)} %fusion.81.refs_1_, f32[32,512]{1,0:T(8,128)S(1)} %pad.13.refs_2_, f32[4,2,128,512]{3,2,1,0:T(8,128)} %bitcast.82, ...), custom_call_target="tpu_custom_call" | custom-call | tf_op jit(solution)/shard_map/pallas_call | solution.py:229
  157.8 0.6 fusion.77
  158.4 0.7 copy.17
  159.1 1.0 copy.18
  160.1 0.6 copy.19
  160.7 1.0 copy.20
  (15 shorter events, 0.1 us)
Async XLA Ops:
  0.6 19.0 %copy-start = (bf16[512,512]{1,0:T(8,128)(2,1)S(1)}, bf16[512,512]{1,0:T(8,128)(2,1)}, u32[]{:S(2)}) copy-start(bf16[512,512]{1,0:T(8,128)(2,1)} %param.9) | copy-start | bytes 1572868
  19.6 14.6 %copy-start.2 = (f32[25,512]{1,0:T(8,128)S(1)}, f32[25,512]{1,0:T(8,128)}, u32[]{:S(2)}) copy-start(f32[25,512]{1,0:T(8,128)} %param.11) | copy-start | bytes 153604
  21.8 17.3 %collective-permute-start = (bf16[2,128,512]{2,1,0:T(8,128)(2,1)S(1)}, bf16[2,128,512]{2,1,0:T(8,128)(2,1)S(1)}, u32[]{:S(2)}, u32[]{:S(2)}) collective-permute-start(bf16[2,128,512]{2,1,0:T(8,128)(2,1)S(1)} %get-tuple-element.50), channel_id=1, source_target_pairs={{0,4},{4,8},{8,12},{12,16},{16,20},{20,24},{24,28},{28,32},{32,36}... | collective-permute-start | bytes 786440 | tf_op jit(solution)/shard_map/ppermute | solution.py:316
  25.3 15.1 %collective-permute-start.1 = (bf16[2,128,512]{2,1,0:T(8,128)(2,1)S(1)}, bf16[2,128,512]{2,1,0:T(8,128)(2,1)S(1)}, u32[]{:S(2)}, u32[]{:S(2)}) collective-permute-start(bf16[2,128,512]{2,1,0:T(8,128)(2,1)S(1)} %get-tuple-element.51), channel_id=1, source_target_pairs={{4,0},{8,4},{12,8},{16,12},{20,16},{24,20},{28,24},{32,28},{36,32}... | collective-permute-start | bytes 786440 | tf_op jit(solution)/shard_map/ppermute | solution.py:319
  34.3 6.5 %copy-start.3 = (f32[512]{0:T(512)S(1)}, f32[512]{0:T(512)}, u32[]{:S(2)}) copy-start(f32[512]{0:T(512)} %param.12) | copy-start | bytes 6148
  40.9 6.7 %copy-start.6 = (bf16[4,2,128,512]{3,2,1,0:T(8,128)(2,1)S(1)}, bf16[4,2,128,512]{3,2,1,0:T(8,128)(2,1)}, u32[]{:S(2)}) copy-start(bf16[4,2,128,512]{3,2,1,0:T(8,128)(2,1)} %get-tuple-element.13) | copy-start | bytes 3145732
  40.9 6.7 %copy-start.7 = (bf16[512,512]{1,0:T(8,128)(2,1)S(1)}, bf16[512,512]{1,0:T(8,128)(2,1)}, u32[]{:S(2)}) copy-start(bf16[512,512]{1,0:T(8,128)(2,1)} %param.13) | copy-start | bytes 1572868
  55.7 14.6 %collective-permute-start.2 = (bf16[2,128,512]{2,1,0:T(8,128)(2,1)S(1)}, bf16[2,128,512]{2,1,0:T(8,128)(2,1)S(1)}, u32[]{:S(2)}, u32[]{:S(2)}) collective-permute-start(bf16[2,128,512]{2,1,0:T(8,128)(2,1)S(1)} %get-tuple-element.48), channel_id=1, source_target_pairs={{0,4},{4,8},{8,12},{12,16},{16,20},{20,24},{24,28},{28,32},{32,36}... | collective-permute-start | bytes 786440 | tf_op jit(solution)/shard_map/ppermute | solution.py:316
  57.7 13.9 %collective-permute-start.3 = (bf16[2,128,512]{2,1,0:T(8,128)(2,1)S(1)}, bf16[2,128,512]{2,1,0:T(8,128)(2,1)S(1)}, u32[]{:S(2)}, u32[]{:S(2)}) collective-permute-start(bf16[2,128,512]{2,1,0:T(8,128)(2,1)S(1)} %get-tuple-element.49), channel_id=1, source_target_pairs={{4,0},{8,4},{12,8},{16,12},{20,16},{24,20},{28,24},{32,28},{36,32}... | collective-permute-start | bytes 786440 | tf_op jit(solution)/shard_map/ppermute | solution.py:319
  67.0 5.1 %copy-start.4 = (f32[512]{0:T(512)S(1)}, f32[512]{0:T(512)}, u32[]{:S(2)}) copy-start(f32[512]{0:T(512)} %param.10) | copy-start | bytes 6148
  79.3 2.1 %copy-start.5 = (bf16[4,2,128,512]{3,2,1,0:T(8,128)(2,1)S(1)}, bf16[4,2,128,512]{3,2,1,0:T(8,128)(2,1)}, u32[]{:S(2)}) copy-start(bf16[4,2,128,512]{3,2,1,0:T(8,128)(2,1)} %get-tuple-element.12) | copy-start | bytes 3145732
  81.5 1.0 copy-start.1

commit v15 on v14

--- a/solution.py
+++ b/solution.py
@@ -114,9 +114,9 @@
         c.start()
     for c in own:
         c.wait()
-    for c in copies:
-        c.wait_recv()
-    for h in range(2):
+    for h in range(2):
+        for c in copies[h * (nz - 1) : (h + 1) * (nz - 1)]:
+            c.wait_recv()
         acc = zs[h, nz - 1]
         for d in range(1, nz):
             acc = acc + zs[h, d - 1]

time: 163 us -> 163 us (level)
  no operation moved by 1% of the time
where the time goes in v15:
time: 163 us; the launch traced here: 162 us
  Pallas kernels  94.3 us (58%)
  starting transfers between devices  22.9 us (14%)
  other arithmetic  19.6 us (12%)
  waiting for transfers between devices  10.5 us (6%)
  matrix products  9.11 us (6%)
  local copies, waits for them, and re-layouts  4.23 us (3%)
    pallas_call x1, Pallas kernels, row_group_allreduce(): pl.pallas_call(body, out_shape=tuple((jax.ShapeDtypeStruct(p.shape, jnp.f...  75.4 us
    pallas_call x1, Pallas kernels, chan_gather(): pl.pallas_call(_chan_gather_kernel, out_shape=(jax.ShapeDtypeStruct(shape...  19 us
    ppermute x2, starting transfers between devices, extended(): lax.ppermute(lax.slice_in_dim(block, 0, width, axis=dim), axis, backward)  17.5 us
    ppermute x2, waiting for transfers between devices, extended(): lax.ppermute(lax.slice_in_dim(block, block.shape[dim] - width, None, axis...  8.19 us
    reduce_sum x1, other arithmetic, shards(): grad_b1 = jnp.sum(flat_act.astype(jnp.float32), axis=0)  7.26 us
    convert_element_type x1, other arithmetic, shards(): mixed = mixed.astype(jnp.bfloat16).reshape(nrows * ncols, hslice)  6.69 us
    ppermute x2, starting transfers between devices, extended(): lax.ppermute(lax.slice_in_dim(block, block.shape[dim] - width, None, axis...  5.34 us
    reduce_sum x1, other arithmetic, shards(): jnp.sum(padded[row_tap:row_tap + nrows, col_tap:col_tap + ncols] * grad_p...  4.67 us
  transfers between devices with their start and end apart: 4, of which 4 were waited for; matrix products, arithmetic and copies ran while one was open for 0% of the time, Pallas kernels for 0%

profile of v15, /device:TPU:8, one launch (start us, length us, event | category | flops | bytes accessed | tf_op | source)
XLA Modules:
  0.0 161.6 jit_solution(5127837165850812410)
XLA Ops:
  0.6 0.0 copy-start
  0.6 19.0 %shard_map.118 = (bf16[4,2,128,512]{3,2,1,0:T(8,128)(2,1)}, bf16[4,2,128,512]{3,2,1,0:T(8,128)(2,1)}) custom-call(bf16[2,128,512]{2,1,0:T(8,128)(2,1)} %first.1, bf16[2,128,512]{2,1,0:T(8,128)(2,1)} %refs_4_.1), custom_call_target="tpu_custom_call" | custom-call | tf_op jit(solution)/shard_map/pallas_call | solution.py:298
  19.6 0.0 copy-start.2
  19.6 2.1 %multiply_convert_fusion.1 = (bf16[8,128,512]{2,1,0:T(8,128)(2,1)S(1)}, f32[8,128,512]{2,1,0:T(8,128)S(1)}) fusion(f32[512]{0:T(512)} %param.10, bf16[8,128,512]{2,1,0:T(8,128)(2,1)} %bitcast.164, bf16[512,512]{1,0:T(8,128)(2,1)S(1)} %copy-done), kind=kOutput, calls=%fused_computation.121 | convolution fusion | flops 540016640 | bytes 4720640 | tf_op jit(solution)/shard_map/dot_general | solution.py:337
  21.8 3.4 %collective-permute-start = (bf16[2,128,512]{2,1,0:T(8,128)(2,1)S(1)}, bf16[2,128,512]{2,1,0:T(8,128)(2,1)S(1)}, u32[]{:S(2)}, u32[]{:S(2)}) collective-permute-start(bf16[2,128,512]{2,1,0:T(8,128)(2,1)S(1)} %get-tuple-element.50), channel_id=1, source_target_pairs={{0,4},{4,8},{8,12},{12,16},{16,20},{20,24},{24,28},{28,32},{32,36}... | collective-permute-start | bytes 786440 | tf_op jit(solution)/shard_map/ppermute | solution.py:316
  25.3 9.0 %collective-permute-start.1 = (bf16[2,128,512]{2,1,0:T(8,128)(2,1)S(1)}, bf16[2,128,512]{2,1,0:T(8,128)(2,1)S(1)}, u32[]{:S(2)}, u32[]{:S(2)}) collective-permute-start(bf16[2,128,512]{2,1,0:T(8,128)(2,1)S(1)} %get-tuple-element.51), channel_id=1, source_target_pairs={{4,0},{8,4},{12,8},{16,12},{20,16},{24,20},{28,24},{32,28},{36,32}... | collective-permute-start | bytes 786440 | tf_op jit(solution)/shard_map/ppermute | solution.py:319
  34.3 0.0 copy-start.3
  34.3 4.8 %collective-permute-done = bf16[2,128,512]{2,1,0:T(8,128)(2,1)S(1)} collective-permute-done((bf16[2,128,512]{2,1,0:T(8,128)(2,1)S(1)}, bf16[2,128,512]{2,1,0:T(8,128)(2,1)S(1)}, u32[]{:S(2)}, u32[]{:S(2)}) %collective-permute-start) | collective-permute-done | bytes 262176 | tf_op jit(solution)/shard_map/ppermute | solution.py:316
  39.1 1.2 collective-permute-done.1
  40.3 0.5 fusion.68
  40.9 0.0 copy-start.7
  40.9 6.7 %multiply_convert_fusion = (bf16[8,128,512]{2,1,0:T(8,128)(2,1)S(1)}, f32[8,128,512]{2,1,0:T(8,128)S(1)}) fusion(f32[12,132,512]{2,1,0:T(8,128)S(1)} %fusion.68, f32[512]{0:T(512)S(1)} %bitcast.93, f32[512]{0:T(512)S(1)} %bitcast.95, f32[512]{0:T(512)S(1)} %bitcast.99, f32[512]{0:T(512)S(1)} %bitcast.101, f32[512]{0:T(512)S(1)} %bitcast.103, ...), kind=kLoop, calls=%fused_computation.118 | loop fusion | flops 28835840 | bytes 55627776 | tf_op jit(solution)/shard_map/convert_element_type | solution.py:355
  47.6 3.4 %fusion.36 = (f32[512]{0:T(512)S(1)}, f32[512]{0:T(512)S(1)}, f32[512]{0:T(512)S(1)}, f32[512]{0:T(512)S(1)}, f32[512]{0:T(512)S(1)}, /*index=5*/f32[512]{0:T(51...) fusion(f32[12,132,512]{2,1,0:T(8,128)S(1)} %fusion.68, f32[8,128,512]{2,1,0:T(8,128)S(1)} %get-tuple-element.47, ...), kind=kOutput, calls=%fused_computation.66 | convolution fusion | flops 550498304 | bytes 19415040 | tf_op jit(solution)/shard_map/dot_general | solution.py:357
  51.0 4.7 %fusion.37 = (f32[512]{0:T(512)S(1)}, f32[512]{0:T(512)S(1)}, f32[512]{0:T(512)S(1)}, f32[512]{0:T(512)S(1)}, f32[512]{0:T(512)S(1)}, /*index=5*/f32[512]{0:T(51...) fusion(bf16[8,128,512]{2,1,0:T(8,128)(2,1)S(1)} %get-tuple-elem, ...), kind=kLoop, calls=%fused_computation.67 | loop fusion | flops 19389440 | bytes 38834176 | tf_op jit(solution)/shard_map/reduce_sum | solution.py:370
  55.7 1.9 %collective-permute-start.2 = (bf16[2,128,512]{2,1,0:T(8,128)(2,1)S(1)}, bf16[2,128,512]{2,1,0:T(8,128)(2,1)S(1)}, u32[]{:S(2)}, u32[]{:S(2)}) collective-permute-start(bf16[2,128,512]{2,1,0:T(8,128)(2,1)S(1)} %get-tuple-element.48), channel_id=1, source_target_pairs={{0,4},{4,8},{8,12},{12,16},{16,20},{20,24},{24,28},{28,32},{32,36}... | collective-permute-start | bytes 786440 | tf_op jit(solution)/shard_map/ppermute | solution.py:316
  57.7 8.6 %collective-permute-start.3 = (bf16[2,128,512]{2,1,0:T(8,128)(2,1)S(1)}, bf16[2,128,512]{2,1,0:T(8,128)(2,1)S(1)}, u32[]{:S(2)}, u32[]{:S(2)}) collective-permute-start(bf16[2,128,512]{2,1,0:T(8,128)(2,1)S(1)} %get-tuple-element.49), channel_id=1, source_target_pairs={{4,0},{8,4},{12,8},{16,12},{20,16},{24,20},{28,24},{32,28},{36,32}... | collective-permute-start | bytes 786440 | tf_op jit(solution)/shard_map/ppermute | solution.py:319
  66.2 0.7 fusion.81.refs_1_
  67.0 0.0 copy-start.4
  67.0 3.4 %collective-permute-done.2 = bf16[2,128,512]{2,1,0:T(8,128)(2,1)S(1)} collective-permute-done((bf16[2,128,512]{2,1,0:T(8,128)(2,1)S(1)}, bf16[2,128,512]{2,1,0:T(8,128)(2,1)S(1)}, u32[]{:S(2)}, u32[]{:S(2)}) %collective-permute-start.2) | collective-permute-done | bytes 262176 | tf_op jit(solution)/shard_map/ppermute | solution.py:316
  70.4 1.2 collective-permute-done.3
  71.5 0.5 fusion.62
  72.1 7.3 %convert_reduce_fusion.1 = (f32[512]{0:T(512)S(1)}, bf16[8,128,512]{2,1,0:T(8,128)(2,1)S(1)}) fusion(f32[8,128,512]{2,1,0:T(8,128)S(1)} %get-tuple-element.80, f32[512]{0:T(512)S(1)} %copy-done.4, f32[12,132,512]{2,1,0:T(8,128)S(1)} %fusion.62, f32[512]{0:T(512)S(1)} %bitcast.94, f32[512]{0:T(512)S(1)} %bitcast.96, f32[512]{0:T(512)S(1)} %bitcast.100, ...), kind=kLoop, calls=%fused_computation.117 | loop fusion | flops 32505344 | bytes 55629824 | tf_op jit(solution)/shard_map/reduce_sum | solution.py:383
  79.4 2.1 %fusion.69 = f32[8,128,512]{2,1,0:T(8,128)} fusion(bf16[8,128,512]{2,1,0:T(8,128)(2,1)S(1)} %get-tuple-element.45, bf16[512,512]{1,0:T(8,128)(2,1)S(1)} %copy-done), kind=kOutput, calls=%fused_computation.132 | convolution fusion | flops 536870912 | bytes 3670016 | tf_op jit(solution)/shard_map/rwh,ch->rwc/dot_general | solution.py:385
  81.5 0.7 fusion.80.refs_0_
  82.2 0.1 concatenate.11
  82.3 0.1 copy-done.1
  82.4 75.4 %shard_map.119 = (f32[512,512]{1,0:T(8,128)S(1)}, f32[512,512]{1,0:T(8,128)S(1)}, f32[32,512]{1,0:T(8,128)S(1)}, bf16[2,128,512]{2,1,0:T(8,128)(2,1)S(1)}) custom-call(f32[512,512]{1,0:T(8,128)S(1)} %fusion.80.refs_0_, f32[512,512]{1,0:T(8,128)S(1)} %fusion.81.refs_1_, f32[32,512]{1,0:T(8,128)S(1)} %pad.13.refs_2_, f32[4,2,128,512]{3,2,1,0:T(8,128)} %bitcast.82, ...), custom_call_target="tpu_custom_call" | custom-call | tf_op jit(solution)/shard_map/pallas_call | solution.py:229
  157.8 0.6 fusion.77
  158.4 0.7 copy.17
  159.1 1.0 copy.18
  160.0 0.6 copy.19
  160.7 1.0 copy.20
  (15 shorter events, 0.1 us)
Async XLA Ops:
  0.6 19.0 %copy-start = (bf16[512,512]{1,0:T(8,128)(2,1)S(1)}, bf16[512,512]{1,0:T(8,128)(2,1)}, u32[]{:S(2)}) copy-start(bf16[512,512]{1,0:T(8,128)(2,1)} %param.9) | copy-start | bytes 1572868
  19.6 14.6 %copy-start.2 = (f32[25,512]{1,0:T(8,128)S(1)}, f32[25,512]{1,0:T(8,128)}, u32[]{:S(2)}) copy-start(f32[25,512]{1,0:T(8,128)} %param.11) | copy-start | bytes 153604
  21.8 17.3 %collective-permute-start = (bf16[2,128,512]{2,1,0:T(8,128)(2,1)S(1)}, bf16[2,128,512]{2,1,0:T(8,128)(2,1)S(1)}, u32[]{:S(2)}, u32[]{:S(2)}) collective-permute-start(bf16[2,128,512]{2,1,0:T(8,128)(2,1)S(1)} %get-tuple-element.50), channel_id=1, source_target_pairs={{0,4},{4,8},{8,12},{12,16},{16,20},{20,24},{24,28},{28,32},{32,36}... | collective-permute-start | bytes 786440 | tf_op jit(solution)/shard_map/ppermute | solution.py:316
  25.3 15.1 %collective-permute-start.1 = (bf16[2,128,512]{2,1,0:T(8,128)(2,1)S(1)}, bf16[2,128,512]{2,1,0:T(8,128)(2,1)S(1)}, u32[]{:S(2)}, u32[]{:S(2)}) collective-permute-start(bf16[2,128,512]{2,1,0:T(8,128)(2,1)S(1)} %get-tuple-element.51), channel_id=1, source_target_pairs={{4,0},{8,4},{12,8},{16,12},{20,16},{24,20},{28,24},{32,28},{36,32}... | collective-permute-start | bytes 786440 | tf_op jit(solution)/shard_map/ppermute | solution.py:319
  34.3 6.5 %copy-start.3 = (f32[512]{0:T(512)S(1)}, f32[512]{0:T(512)}, u32[]{:S(2)}) copy-start(f32[512]{0:T(512)} %param.12) | copy-start | bytes 6148
  40.9 6.7 %copy-start.6 = (bf16[4,2,128,512]{3,2,1,0:T(8,128)(2,1)S(1)}, bf16[4,2,128,512]{3,2,1,0:T(8,128)(2,1)}, u32[]{:S(2)}) copy-start(bf16[4,2,128,512]{3,2,1,0:T(8,128)(2,1)} %get-tuple-element.13) | copy-start | bytes 3145732
  40.9 6.7 %copy-start.7 = (bf16[512,512]{1,0:T(8,128)(2,1)S(1)}, bf16[512,512]{1,0:T(8,128)(2,1)}, u32[]{:S(2)}) copy-start(bf16[512,512]{1,0:T(8,128)(2,1)} %param.13) | copy-start | bytes 1572868
  55.7 14.6 %collective-permute-start.2 = (bf16[2,128,512]{2,1,0:T(8,128)(2,1)S(1)}, bf16[2,128,512]{2,1,0:T(8,128)(2,1)S(1)}, u32[]{:S(2)}, u32[]{:S(2)}) collective-permute-start(bf16[2,128,512]{2,1,0:T(8,128)(2,1)S(1)} %get-tuple-element.48), channel_id=1, source_target_pairs={{0,4},{4,8},{8,12},{12,16},{16,20},{20,24},{24,28},{28,32},{32,36}... | collective-permute-start | bytes 786440 | tf_op jit(solution)/shard_map/ppermute | solution.py:316
  57.7 13.9 %collective-permute-start.3 = (bf16[2,128,512]{2,1,0:T(8,128)(2,1)S(1)}, bf16[2,128,512]{2,1,0:T(8,128)(2,1)S(1)}, u32[]{:S(2)}, u32[]{:S(2)}) collective-permute-start(bf16[2,128,512]{2,1,0:T(8,128)(2,1)S(1)} %get-tuple-element.49), channel_id=1, source_target_pairs={{4,0},{8,4},{12,8},{16,12},{20,16},{24,20},{28,24},{32,28},{36,32}... | collective-permute-start | bytes 786440 | tf_op jit(solution)/shard_map/ppermute | solution.py:319
  67.0 5.1 %copy-start.4 = (f32[512]{0:T(512)S(1)}, f32[512]{0:T(512)}, u32[]{:S(2)}) copy-start(f32[512]{0:T(512)} %param.10) | copy-start | bytes 6148
  79.3 2.1 %copy-start.5 = (bf16[4,2,128,512]{3,2,1,0:T(8,128)(2,1)S(1)}, bf16[4,2,128,512]{3,2,1,0:T(8,128)(2,1)}, u32[]{:S(2)}) copy-start(bf16[4,2,128,512]{3,2,1,0:T(8,128)(2,1)} %get-tuple-element.12) | copy-start | bytes 3145732
  81.5 1.0 copy-start.1

commit v16 on v15

--- a/solution.py
+++ b/solution.py
@@ -46,13 +46,6 @@
         pl.semaphore_signal(barrier, inc=1, device_id=d, device_id_type=MESH_ID)
     pl.semaphore_wait(barrier, len(peers))
 
-    chan_one = []
-    for j, src in enumerate((part.at[pair_at], part.at[diag_at])):
-        c = pltpu.make_async_remote_copy(
-            src_ref=src, dst_ref=from_pair.at[j], send_sem=csems.at[0, j],
-            recv_sem=csems.at[1, j], device_id=pair, device_id_type=MESH_ID)
-        c.start()
-        chan_one.append(c)
 
     rows, cols = data.shape
     half = cols // 2
@@ -86,6 +79,14 @@
                 recv_sem=xrecv.at[h * nx + s], device_id=x_next[h], device_id_type=MESH_ID)
             c.start()
             copies.append(c)
+        if s == 0:
+            chan_one = []
+            for j, src in enumerate((part.at[pair_at], part.at[diag_at])):
+                c = pltpu.make_async_remote_copy(
+                    src_ref=src, dst_ref=from_pair.at[j], send_sem=csems.at[0, j],
+                    recv_sem=csems.at[1, j], device_id=pair, device_id_type=MESH_ID)
+                c.start()
+                chan_one.append(c)
         for h in range(2):
             sg = steps[h]
             copies[h].wait_recv()

time: 163 us -> 163 us (level)
  no operation moved by 1% of the time
where the time goes in v16:
time: 163 us; the launch traced here: 162 us
  Pallas kernels  94.3 us (58%)
  starting transfers between devices  22.9 us (14%)
  other arithmetic  19.6 us (12%)
  waiting for transfers between devices  10.5 us (6%)
  matrix products  9.11 us (6%)
  local copies, waits for them, and re-layouts  4.23 us (3%)
    pallas_call x1, Pallas kernels, row_group_allreduce(): pl.pallas_call(body, out_shape=tuple((jax.ShapeDtypeStruct(p.shape, jnp.f...  75.4 us
    pallas_call x1, Pallas kernels, chan_gather(): pl.pallas_call(_chan_gather_kernel, out_shape=(jax.ShapeDtypeStruct(shape...  19 us
    ppermute x2, starting transfers between devices, extended(): lax.ppermute(lax.slice_in_dim(block, 0, width, axis=dim), axis, backward)  17.5 us
    ppermute x2, waiting for transfers between devices, extended(): lax.ppermute(lax.slice_in_dim(block, block.shape[dim] - width, None, axis...  8.19 us
    reduce_sum x1, other arithmetic, shards(): grad_b1 = jnp.sum(flat_act.astype(jnp.float32), axis=0)  7.26 us
    convert_element_type x1, other arithmetic, shards(): mixed = mixed.astype(jnp.bfloat16).reshape(nrows * ncols, hslice)  6.69 us
    ppermute x2, starting transfers between devices, extended(): lax.ppermute(lax.slice_in_dim(block, block.shape[dim] - width, None, axis...  5.34 us
    reduce_sum x1, other arithmetic, shards(): jnp.sum(padded[row_tap:row_tap + nrows, col_tap:col_tap + ncols] * grad_p...  4.67 us
  transfers between devices with their start and end apart: 4, of which 4 were waited for; matrix products, arithmetic and copies ran while one was open for 0% of the time, Pallas kernels for 0%

profile of v16, /device:TPU:8, one launch (start us, length us, event | category | flops | bytes accessed | tf_op | source)
XLA Modules:
  0.0 161.6 jit_solution(17671585940056095687)
XLA Ops:
  0.6 0.0 copy-start
  0.6 19.0 %shard_map.118 = (bf16[4,2,128,512]{3,2,1,0:T(8,128)(2,1)}, bf16[4,2,128,512]{3,2,1,0:T(8,128)(2,1)}) custom-call(bf16[2,128,512]{2,1,0:T(8,128)(2,1)} %first.1, bf16[2,128,512]{2,1,0:T(8,128)(2,1)} %refs_4_.1), custom_call_target="tpu_custom_call" | custom-call | tf_op jit(solution)/shard_map/pallas_call | solution.py:299
  19.6 0.0 copy-start.2
  19.6 2.1 %multiply_convert_fusion.1 = (bf16[8,128,512]{2,1,0:T(8,128)(2,1)S(1)}, f32[8,128,512]{2,1,0:T(8,128)S(1)}) fusion(f32[512]{0:T(512)} %param.10, bf16[8,128,512]{2,1,0:T(8,128)(2,1)} %bitcast.164, bf16[512,512]{1,0:T(8,128)(2,1)S(1)} %copy-done), kind=kOutput, calls=%fused_computation.121 | convolution fusion | flops 540016640 | bytes 4720640 | tf_op jit(solution)/shard_map/dot_general | solution.py:338
  21.8 3.4 %collective-permute-start = (bf16[2,128,512]{2,1,0:T(8,128)(2,1)S(1)}, bf16[2,128,512]{2,1,0:T(8,128)(2,1)S(1)}, u32[]{:S(2)}, u32[]{:S(2)}) collective-permute-start(bf16[2,128,512]{2,1,0:T(8,128)(2,1)S(1)} %get-tuple-element.50), channel_id=1, source_target_pairs={{0,4},{4,8},{8,12},{12,16},{16,20},{20,24},{24,28},{28,32},{32,36}... | collective-permute-start | bytes 786440 | tf_op jit(solution)/shard_map/ppermute | solution.py:317
  25.3 9.0 %collective-permute-start.1 = (bf16[2,128,512]{2,1,0:T(8,128)(2,1)S(1)}, bf16[2,128,512]{2,1,0:T(8,128)(2,1)S(1)}, u32[]{:S(2)}, u32[]{:S(2)}) collective-permute-start(bf16[2,128,512]{2,1,0:T(8,128)(2,1)S(1)} %get-tuple-element.51), channel_id=1, source_target_pairs={{4,0},{8,4},{12,8},{16,12},{20,16},{24,20},{28,24},{32,28},{36,32}... | collective-permute-start | bytes 786440 | tf_op jit(solution)/shard_map/ppermute | solution.py:320
  34.3 0.0 copy-start.3
  34.3 4.8 %collective-permute-done = bf16[2,128,512]{2,1,0:T(8,128)(2,1)S(1)} collective-permute-done((bf16[2,128,512]{2,1,0:T(8,128)(2,1)S(1)}, bf16[2,128,512]{2,1,0:T(8,128)(2,1)S(1)}, u32[]{:S(2)}, u32[]{:S(2)}) %collective-permute-start) | collective-permute-done | bytes 262176 | tf_op jit(solution)/shard_map/ppermute | solution.py:317
  39.1 1.2 collective-permute-done.1
  40.3 0.5 fusion.68
  40.9 0.0 copy-start.7
  40.9 6.7 %multiply_convert_fusion = (bf16[8,128,512]{2,1,0:T(8,128)(2,1)S(1)}, f32[8,128,512]{2,1,0:T(8,128)S(1)}) fusion(f32[12,132,512]{2,1,0:T(8,128)S(1)} %fusion.68, f32[512]{0:T(512)S(1)} %bitcast.93, f32[512]{0:T(512)S(1)} %bitcast.95, f32[512]{0:T(512)S(1)} %bitcast.99, f32[512]{0:T(512)S(1)} %bitcast.101, f32[512]{0:T(512)S(1)} %bitcast.103, ...), kind=kLoop, calls=%fused_computation.118 | loop fusion | flops 28835840 | bytes 55627776 | tf_op jit(solution)/shard_map/convert_element_type | solution.py:356
  47.6 3.4 %fusion.36 = (f32[512]{0:T(512)S(1)}, f32[512]{0:T(512)S(1)}, f32[512]{0:T(512)S(1)}, f32[512]{0:T(512)S(1)}, f32[512]{0:T(512)S(1)}, /*index=5*/f32[512]{0:T(51...) fusion(f32[12,132,512]{2,1,0:T(8,128)S(1)} %fusion.68, f32[8,128,512]{2,1,0:T(8,128)S(1)} %get-tuple-element.47, ...), kind=kOutput, calls=%fused_computation.66 | convolution fusion | flops 550498304 | bytes 19415040 | tf_op jit(solution)/shard_map/dot_general | solution.py:358
  51.0 4.7 %fusion.37 = (f32[512]{0:T(512)S(1)}, f32[512]{0:T(512)S(1)}, f32[512]{0:T(512)S(1)}, f32[512]{0:T(512)S(1)}, f32[512]{0:T(512)S(1)}, /*index=5*/f32[512]{0:T(51...) fusion(bf16[8,128,512]{2,1,0:T(8,128)(2,1)S(1)} %get-tuple-elem, ...), kind=kLoop, calls=%fused_computation.67 | loop fusion | flops 19389440 | bytes 38834176 | tf_op jit(solution)/shard_map/reduce_sum | solution.py:371
  55.7 1.9 %collective-permute-start.2 = (bf16[2,128,512]{2,1,0:T(8,128)(2,1)S(1)}, bf16[2,128,512]{2,1,0:T(8,128)(2,1)S(1)}, u32[]{:S(2)}, u32[]{:S(2)}) collective-permute-start(bf16[2,128,512]{2,1,0:T(8,128)(2,1)S(1)} %get-tuple-element.48), channel_id=1, source_target_pairs={{0,4},{4,8},{8,12},{12,16},{16,20},{20,24},{24,28},{28,32},{32,36}... | collective-permute-start | bytes 786440 | tf_op jit(solution)/shard_map/ppermute | solution.py:317
  57.7 8.6 %collective-permute-start.3 = (bf16[2,128,512]{2,1,0:T(8,128)(2,1)S(1)}, bf16[2,128,512]{2,1,0:T(8,128)(2,1)S(1)}, u32[]{:S(2)}, u32[]{:S(2)}) collective-permute-start(bf16[2,128,512]{2,1,0:T(8,128)(2,1)S(1)} %get-tuple-element.49), channel_id=1, source_target_pairs={{4,0},{8,4},{12,8},{16,12},{20,16},{24,20},{28,24},{32,28},{36,32}... | collective-permute-start | bytes 786440 | tf_op jit(solution)/shard_map/ppermute | solution.py:320
  66.2 0.7 fusion.81.refs_1_
  67.0 0.0 copy-start.4
  67.0 3.4 %collective-permute-done.2 = bf16[2,128,512]{2,1,0:T(8,128)(2,1)S(1)} collective-permute-done((bf16[2,128,512]{2,1,0:T(8,128)(2,1)S(1)}, bf16[2,128,512]{2,1,0:T(8,128)(2,1)S(1)}, u32[]{:S(2)}, u32[]{:S(2)}) %collective-permute-start.2) | collective-permute-done | bytes 262176 | tf_op jit(solution)/shard_map/ppermute | solution.py:317
  70.4 1.2 collective-permute-done.3
  71.5 0.5 fusion.62
  72.1 7.3 %convert_reduce_fusion.1 = (f32[512]{0:T(512)S(1)}, bf16[8,128,512]{2,1,0:T(8,128)(2,1)S(1)}) fusion(f32[8,128,512]{2,1,0:T(8,128)S(1)} %get-tuple-element.80, f32[512]{0:T(512)S(1)} %copy-done.4, f32[12,132,512]{2,1,0:T(8,128)S(1)} %fusion.62, f32[512]{0:T(512)S(1)} %bitcast.94, f32[512]{0:T(512)S(1)} %bitcast.96, f32[512]{0:T(512)S(1)} %bitcast.100, ...), kind=kLoop, calls=%fused_computation.117 | loop fusion | flops 32505344 | bytes 55629824 | tf_op jit(solution)/shard_map/reduce_sum | solution.py:384
  79.4 2.1 %fusion.69 = f32[8,128,512]{2,1,0:T(8,128)} fusion(bf16[8,128,512]{2,1,0:T(8,128)(2,1)S(1)} %get-tuple-element.45, bf16[512,512]{1,0:T(8,128)(2,1)S(1)} %copy-done), kind=kOutput, calls=%fused_computation.132 | convolution fusion | flops 536870912 | bytes 3670016 | tf_op jit(solution)/shard_map/rwh,ch->rwc/dot_general | solution.py:386
  81.5 0.7 fusion.80.refs_0_
  82.2 0.1 concatenate.11
  82.3 0.1 copy-done.1
  82.4 75.4 %shard_map.119 = (f32[512,512]{1,0:T(8,128)S(1)}, f32[512,512]{1,0:T(8,128)S(1)}, f32[32,512]{1,0:T(8,128)S(1)}, bf16[2,128,512]{2,1,0:T(8,128)(2,1)S(1)}) custom-call(f32[512,512]{1,0:T(8,128)S(1)} %fusion.80.refs_0_, f32[512,512]{1,0:T(8,128)S(1)} %fusion.81.refs_1_, f32[32,512]{1,0:T(8,128)S(1)} %pad.13.refs_2_, f32[4,2,128,512]{3,2,1,0:T(8,128)} %bitcast.82, ...), custom_call_target="tpu_custom_call" | custom-call | tf_op jit(solution)/shard_map/pallas_call | solution.py:230
  157.8 0.6 fusion.77
  158.4 0.7 copy.17
  159.1 1.0 copy.18
  160.0 0.6 copy.19
  160.7 1.0 copy.20
  (15 shorter events, 0.1 us)
Async XLA Ops:
  0.6 19.0 %copy-start = (bf16[512,512]{1,0:T(8,128)(2,1)S(1)}, bf16[512,512]{1,0:T(8,128)(2,1)}, u32[]{:S(2)}) copy-start(bf16[512,512]{1,0:T(8,128)(2,1)} %param.9) | copy-start | bytes 1572868
  19.6 14.6 %copy-start.2 = (f32[25,512]{1,0:T(8,128)S(1)}, f32[25,512]{1,0:T(8,128)}, u32[]{:S(2)}) copy-start(f32[25,512]{1,0:T(8,128)} %param.11) | copy-start | bytes 153604
  21.8 17.3 %collective-permute-start = (bf16[2,128,512]{2,1,0:T(8,128)(2,1)S(1)}, bf16[2,128,512]{2,1,0:T(8,128)(2,1)S(1)}, u32[]{:S(2)}, u32[]{:S(2)}) collective-permute-start(bf16[2,128,512]{2,1,0:T(8,128)(2,1)S(1)} %get-tuple-element.50), channel_id=1, source_target_pairs={{0,4},{4,8},{8,12},{12,16},{16,20},{20,24},{24,28},{28,32},{32,36}... | collective-permute-start | bytes 786440 | tf_op jit(solution)/shard_map/ppermute | solution.py:317
  25.3 15.1 %collective-permute-start.1 = (bf16[2,128,512]{2,1,0:T(8,128)(2,1)S(1)}, bf16[2,128,512]{2,1,0:T(8,128)(2,1)S(1)}, u32[]{:S(2)}, u32[]{:S(2)}) collective-permute-start(bf16[2,128,512]{2,1,0:T(8,128)(2,1)S(1)} %get-tuple-element.51), channel_id=1, source_target_pairs={{4,0},{8,4},{12,8},{16,12},{20,16},{24,20},{28,24},{32,28},{36,32}... | collective-permute-start | bytes 786440 | tf_op jit(solution)/shard_map/ppermute | solution.py:320
  34.3 6.5 %copy-start.3 = (f32[512]{0:T(512)S(1)}, f32[512]{0:T(512)}, u32[]{:S(2)}) copy-start(f32[512]{0:T(512)} %param.12) | copy-start | bytes 6148
  40.9 6.7 %copy-start.6 = (bf16[4,2,128,512]{3,2,1,0:T(8,128)(2,1)S(1)}, bf16[4,2,128,512]{3,2,1,0:T(8,128)(2,1)}, u32[]{:S(2)}) copy-start(bf16[4,2,128,512]{3,2,1,0:T(8,128)(2,1)} %get-tuple-element.13) | copy-start | bytes 3145732
  40.9 6.7 %copy-start.7 = (bf16[512,512]{1,0:T(8,128)(2,1)S(1)}, bf16[512,512]{1,0:T(8,128)(2,1)}, u32[]{:S(2)}) copy-start(bf16[512,512]{1,0:T(8,128)(2,1)} %param.13) | copy-start | bytes 1572868
  55.7 14.6 %collective-permute-start.2 = (bf16[2,128,512]{2,1,0:T(8,128)(2,1)S(1)}, bf16[2,128,512]{2,1,0:T(8,128)(2,1)S(1)}, u32[]{:S(2)}, u32[]{:S(2)}) collective-permute-start(bf16[2,128,512]{2,1,0:T(8,128)(2,1)S(1)} %get-tuple-element.48), channel_id=1, source_target_pairs={{0,4},{4,8},{8,12},{12,16},{16,20},{20,24},{24,28},{28,32},{32,36}... | collective-permute-start | bytes 786440 | tf_op jit(solution)/shard_map/ppermute | solution.py:317
  57.7 13.9 %collective-permute-start.3 = (bf16[2,128,512]{2,1,0:T(8,128)(2,1)S(1)}, bf16[2,128,512]{2,1,0:T(8,128)(2,1)S(1)}, u32[]{:S(2)}, u32[]{:S(2)}) collective-permute-start(bf16[2,128,512]{2,1,0:T(8,128)(2,1)S(1)} %get-tuple-element.49), channel_id=1, source_target_pairs={{4,0},{8,4},{12,8},{16,12},{20,16},{24,20},{28,24},{32,28},{36,32}... | collective-permute-start | bytes 786440 | tf_op jit(solution)/shard_map/ppermute | solution.py:320
  67.0 5.1 %copy-start.4 = (f32[512]{0:T(512)S(1)}, f32[512]{0:T(512)}, u32[]{:S(2)}) copy-start(f32[512]{0:T(512)} %param.10) | copy-start | bytes 6148
  79.3 2.1 %copy-start.5 = (bf16[4,2,128,512]{3,2,1,0:T(8,128)(2,1)S(1)}, bf16[4,2,128,512]{3,2,1,0:T(8,128)(2,1)}, u32[]{:S(2)}) copy-start(bf16[4,2,128,512]{3,2,1,0:T(8,128)(2,1)} %get-tuple-element.12) | copy-start | bytes 3145732
  81.5 1.0 copy-start.1
